TPU v7x, 32 devices: a whole 2x2x4 slice. The times are simulated.
32 devices in a mesh: groups: 2 (over y), rows: 4 (over z), experts: 2 (over x), heads: 2 (over core).
Axes of the slice: x: 2, y: 2, z: 4, core: 2. Of those that a mesh axis runs over, the one named last changes fastest.
Arguments:
- queries: bfloat16 [2, 32, 6144], P(None, ('groups', 'rows', 'experts'), 'heads'), parts along dimension 1, may hold values from -192 to 192
- new_kv: bfloat16 [2, 32, 2, 1024], P(None, ('groups', 'rows', 'experts'), None, 'heads'), parts along dimension 1, may hold values from -24 to 24
- prefix_kv: bfloat16 [8, 128, 2, 1024], P(('groups', 'experts'), 'rows', None, 'heads'), parts along dimension 0, may hold values from -6 to 6
- cont_prompt: int32 [32], P(('groups', 'rows', 'experts')), parts along dimension 0, may hold values from 0 to 3, as said below
- resid: bfloat16 [2, 32, 6144], P(None, ('groups', 'rows', 'experts'), 'heads'), parts along dimension 1, may hold values from -400 to 400
- norm_gain: bfloat16 [6144], replicated, may hold values from 0.099609375 to 1.8984375
- w_gate: bfloat16 [2, 6144, 8192], P('experts', None, ('rows', 'heads')), may hold values from -0.078125 to 0.078125
- w_up: bfloat16 [2, 6144, 8192], P('experts', None, ('rows', 'heads')), may hold values from -0.078125 to 0.078125
- w_down: bfloat16 [2, 8192, 6144], P('experts', 'rows', 'heads'), may hold values from -0.0625 to 0.0625
- routes: int32 [2, 32, 2], P(None, ('groups', 'rows', 'experts')), parts along dimension 1, may hold values from 0 to 1, as said below
- route_gates: float32 [2, 32, 2], P(None, ('groups', 'rows', 'experts')), parts along dimension 1, may hold values from 0.2 to 1
Outputs:
- attn_out: bfloat16 [2, 32, 6144], P(None, ('groups', 'rows', 'experts'), 'heads'), parts along dimension 1
- moe_out: bfloat16 [2, 32, 6144], P(None, ('groups', 'rows', 'experts'), 'heads'), parts along dimension 1
There are 2 independent parts, one for each index of `groups`. A program takes and returns all parts, laid end to end along the dimension named above; an argument that names none is the same for every part. Nothing has to cross between parts.
Inputs may be any that keep to these rules, and one draw needn't show every extreme that they name: `cont_prompt`: continuation c belongs to one of the 2 prompts numbered from o * 2, where o = (c // 2) % 2. `routes`: each token names 2 different experts; no expert is named by more than 32 tokens, and one expert is named by exactly 32.
All inputs are finite; a program needn't handle non-finite values.
Results may differ from a plain program's by a relative error of at most 0.025.
Values may be sent and summed in bfloat16 or wider, within the bound.
No kernel may reach another device: no remote copies, remote signals or barrier semaphores. Data moves between devices by JAX's collectives and lax.ppermute only.
A program may use at most 64 MiB of HBM per device.

v0:
```python
import jax
import jax.numpy as jnp
from jax import lax
from jax.sharding import PartitionSpec as P

HEADS = 48
KV_HEADS = 8
HEAD_DIM = 128


def fresh_terms(queries, new_kv):
    step_count, own_rows = (queries.shape[0], queries.shape[1])
    kv_local = new_kv.shape[-1] // HEAD_DIM
    group_size = HEADS // KV_HEADS
    grouped = queries.reshape(step_count, own_rows, kv_local, group_size, HEAD_DIM)
    fresh_keys = new_kv[:, :, 0].reshape(step_count, own_rows, kv_local, HEAD_DIM)
    fresh_values = new_kv[:, :, 1].reshape(step_count, own_rows, kv_local, HEAD_DIM)
    fresh_scores = jnp.einsum(
        "scgnd,tcgd->scgnt", grouped, fresh_keys, preferred_element_type=jnp.float32
    ) * HEAD_DIM ** (-0.5)
    future = jnp.arange(step_count)[None, :] > jnp.arange(step_count)[:, None]
    fresh_scores = jnp.where(future[:, None, None, None, :], -jnp.inf, fresh_scores)
    return (grouped, fresh_scores, fresh_values)


def attend_gathered(queries, new_kv, prefix_kv, local_prompt):
    grouped, fresh_scores, fresh_values = fresh_terms(queries, new_kv)
    own_rows = queries.shape[1]
    kv_local = new_kv.shape[-1] // HEAD_DIM
    cache = lax.all_gather(prefix_kv, "rows", axis=1, tiled=True)
    length = cache.shape[1]
    picked = jnp.take(cache, local_prompt, axis=0)
    cache_keys = picked[:, :, 0].reshape(own_rows, length, kv_local, HEAD_DIM)
    cache_values = picked[:, :, 1].reshape(own_rows, length, kv_local, HEAD_DIM)
    prefix_scores = jnp.einsum(
        "scgnd,ckgd->scgnk", grouped, cache_keys, preferred_element_type=jnp.float32
    ) * HEAD_DIM ** (-0.5)
    highest = jnp.maximum(jnp.max(prefix_scores, axis=-1), jnp.max(fresh_scores, axis=-1))
    prefix_expo = jnp.exp(prefix_scores - highest[..., None])
    fresh_expo = jnp.exp(fresh_scores - highest[..., None])
    totals = jnp.sum(prefix_expo, axis=-1) + jnp.sum(fresh_expo, axis=-1)
    weighted = jnp.einsum(
        "scgnk,ckgd->scgnd",
        prefix_expo.astype(jnp.bfloat16),
        cache_values,
        preferred_element_type=jnp.float32,
    )
    weighted = weighted + jnp.einsum(
        "scgnt,tcgd->scgnd",
        fresh_expo.astype(jnp.bfloat16),
        fresh_values,
        preferred_element_type=jnp.float32,
    )
    return (weighted, totals)


def per_device(
    queries,
    new_kv,
    prefix_kv,
    cont_prompt,
    resid,
    norm_gain,
    w_gate,
    w_up,
    w_down,
    routes,
    route_gates,
):
    step_count, own_rows, half_width = queries.shape
    prompt_count = prefix_kv.shape[0]
    local_prompt = cont_prompt - lax.axis_index("experts") * prompt_count
    weighted, totals = attend_gathered(queries, new_kv, prefix_kv, local_prompt)
    attn_out = (
        (weighted / totals[..., None])
        .astype(jnp.bfloat16)
        .reshape(step_count, own_rows, half_width)
    )
    halves = (
        lax.all_gather(resid, "heads", axis=2, tiled=True),
        lax.all_gather(attn_out, "heads", axis=2, tiled=True),
    )
    combined = halves[0].astype(jnp.float32) + halves[1].astype(jnp.float32)
    square_mean = jnp.mean(combined * combined, axis=-1, keepdims=True)
    normed = (combined * lax.rsqrt(square_mean + 1e-05) * norm_gain.astype(jnp.float32)).astype(
        jnp.bfloat16
    )
    token_count = step_count * own_rows
    flat_tokens = normed.reshape(token_count, -1)
    flat_routes = routes.reshape(token_count, -1)
    experts = lax.axis_size("experts")
    matches = flat_routes[:, :, None] == jnp.arange(experts)[None, None, :]
    gate_weights = w_gate[0]
    up_weights = w_up[0]
    wanted = jnp.transpose(jnp.any(matches, axis=1))
    outgoing = jnp.where(wanted[:, :, None], flat_tokens[None], jnp.zeros((), jnp.bfloat16))
    arrived = lax.all_to_all(outgoing, "experts", split_axis=0, concat_axis=0, tiled=True)
    segment = lax.all_gather(arrived.reshape(experts * token_count, -1), "rows", axis=0, tiled=True)
    gate = jnp.dot(segment, gate_weights, preferred_element_type=jnp.float32)
    up_part = jnp.dot(segment, up_weights, preferred_element_type=jnp.float32)
    hidden = (jax.nn.silu(gate) * up_part).astype(jnp.bfloat16)
    paired = lax.all_gather(hidden, "heads", axis=1, tiled=True)
    down_rows = w_down[0]
    segment = paired
    summed = lax.psum_scatter(
        jnp.dot(segment, down_rows, preferred_element_type=jnp.float32).astype(jnp.bfloat16),
        "rows",
        scatter_dimension=0,
        tiled=True,
    )
    result = summed.reshape(experts, token_count, -1)
    returned = lax.all_to_all(result, "experts", split_axis=0, concat_axis=0, tiled=True)
    mixing = jnp.sum(
        jnp.where(matches, route_gates.reshape(token_count, -1)[:, :, None], 0.0), axis=1
    )
    mixture = jnp.einsum("ne,end->nd", mixing, returned.astype(jnp.float32))
    moe_out = mixture.astype(jnp.bfloat16).reshape(step_count, own_rows, half_width)
    return (attn_out, moe_out)


def solution(mesh):
    placed = (
        P(None, ("groups", "rows", "experts"), "heads"),
        P(None, ("groups", "rows", "experts"), None, "heads"),
        P(("groups", "experts"), "rows", None, "heads"),
        P(("groups", "rows", "experts")),
        P(None, ("groups", "rows", "experts"), "heads"),
        P(),
        P("experts", None, ("rows", "heads")),
        P("experts", None, ("rows", "heads")),
        P("experts", "rows", "heads"),
        P(None, ("groups", "rows", "experts"), None),
        P(None, ("groups", "rows", "experts"), None),
    )
    return jax.shard_map(
        per_device,
        mesh=mesh,
        in_specs=placed,
        out_specs=(
            P(None, ("groups", "rows", "experts"), "heads"),
            P(None, ("groups", "rows", "experts"), "heads"),
        ),
        check_vma=False,
    )
```

profile of v0, /device:TPU:0, one launch (start us, length us, event | category | flops | bytes accessed | tf_op | source)
XLA Modules:
  0.0 113.6 jit_solution(1748175390592555168)
XLA Ops:
  7.2 0.7 compare_and_fusion
  7.9 0.9 copy.47
  8.8 17.4 %all_gather.15 = bf16[2,128,2,512]{3,1,2,0:T(8,128)(2,1)S(1)} all-gather(bf16[2,32,2,512]{3,1,2,0:T(8,128)(2,1)S(1)} %copy.47), channel_id=1, replica_groups=mesh['groups'=2,'rows'=4,'experts'=2,'heads'=2] {'rows'}, dimensions={1}, use_global_device_ids=true | all-gather | bytes 655360 | tf_op jit(solution)/shard_map/all_gather | solution.py:30
  26.2 0.6 gather_fusion
  26.8 0.1 broadcast_select_fusion
  27.0 0.2 copy.49
  27.1 0.8 reshape.58
  27.9 0.8 slice_reduce_fusion
  28.7 0.3 fusion.37
  29.0 0.3 fusion.38
  29.3 0.2 fusion.21
  29.5 0.2 copy.48
  29.7 0.3 convolution_bitcast_fusion.1
  30.0 0.2 fusion.18
  30.3 1.8 %all_gather.17 = bf16[2,2,6144]{2,1,0:T(2,128)(2,1)S(1)} all-gather(bf16[2,2,3072]{2,1,0:T(2,128)(2,1)S(1)} %reshape.59), channel_id=1, replica_groups=mesh['groups'=2,'rows'=4,'experts'=2,'heads'=2] {'heads'}, dimensions={2}, use_global_device_ids=true | all-gather | bytes 73728 | tf_op jit(solution)/shard_map/all_gather | solution.py:81
  32.1 2.0 %all_gather.16 = bf16[2,2,6144]{2,1,0:T(2,128)(2,1)S(1)} all-gather(bf16[2,2,3072]{2,1,0:T(2,128)(2,1)} %param.15), channel_id=1, replica_groups=mesh['groups'=2,'rows'=4,'experts'=2,'heads'=2] {'heads'}, dimensions={2}, use_global_device_ids=true | all-gather | bytes 73728 | tf_op jit(solution)/shard_map/all_gather | solution.py:80
  34.2 0.2 multiply_reduce_fusion
  34.4 0.7 convert_element_type.36
  35.1 0.1 multiply_convert_fusion
  35.2 0.8 copy.76
  36.3 6.9 %all_to_all.10 = bf16[2,4,6144]{2,1,0:T(4,128)(2,1)S(1)} all-to-all(bf16[2,4,6144]{2,1,0:T(4,128)(2,1)S(1)} %broadcast_select_fusion.1), channel_id=1, replica_groups=mesh['groups'=2,'rows'=4,'experts'=2,'heads'=2] {'experts'}, dimensions={0} | all-to-all | bytes 196608 | tf_op jit(solution)/shard_map/all_to_all | solution.py:97
  43.2 14.6 %all_gather.18 = bf16[32,6144]{1,0:T(8,128)(2,1)S(1)} all-gather(bf16[8,6144]{1,0:T(8,128)(2,1)S(1)} %reshape.60), channel_id=1, replica_groups=mesh['groups'=2,'rows'=4,'experts'=2,'heads'=2] {'rows'}, dimensions={0}, use_global_device_ids=true | all-gather | bytes 491520 | tf_op jit(solution)/shard_map/all_gather | solution.py:98
  57.8 7.0 %fusion.4 = f32[32,1024]{1,0:T(8,128)S(1)} fusion(bf16[32,6144]{1,0:T(8,128)(2,1)S(1)} %all_gather.18, bf16[1,6144,1024]{2,1,0:T(8,128)(2,1)} %param.17), kind=kOutput, calls=%fused_computation.5 | convolution fusion | flops 402653184 | bytes 13107200 | tf_op jit(solution)/shard_map/dot_general | solution.py:99
  64.8 7.0 %fusion.12 = bf16[32,1024]{1,0:T(8,128)(2,1)S(1)} fusion(bf16[32,6144]{1,0:T(8,128)(2,1)S(1)} %all_gather.18, bf16[1,6144,1024]{2,1,0:T(8,128)(2,1)} %param.18, f32[32,1024]{1,0:T(8,128)S(1)} %fusion.4), kind=kOutput, calls=%fused_computation.9 | convolution fusion | flops 402849792 | bytes 13172736 | tf_op jit(solution)/shard_map/dot_general | solution.py:100
  71.9 1.9 %all_gather.19 = bf16[32,2048]{1,0:T(8,128)(2,1)S(1)} all-gather(bf16[32,1024]{1,0:T(8,128)(2,1)S(1)} %fusion.12), channel_id=1, replica_groups=mesh['groups'=2,'rows'=4,'experts'=2,'heads'=2] {'heads'}, dimensions={1}, use_global_device_ids=true | all-gather | bytes 196608 | tf_op jit(solution)/shard_map/all_gather | solution.py:102
  73.8 2.9 %fusion.6 = bf16[32,3072]{1,0:T(8,128)(2,1)} fusion(bf16[32,2048]{1,0:T(8,128)(2,1)S(1)} %all_gather.19, bf16[1,2048,3072]{2,1,0:T(8,128)(2,1)S(1)} %bitcast.57), kind=kOutput, calls=%fused_computation.7 | convolution fusion | flops 402751488 | bytes 12910592 | tf_op jit(solution)/shard_map/dot_general | solution.py:106
  76.8 20.3 %reduce-scatter.2.cloned.1.call-done = bf16[8,3072]{1,0:T(8,128)(2,1)} async-done(((bf16[32,3072]{1,0:T(8,128)(2,1)}), bf16[8,3072]{1,0:T(8,128)(2,1)}) %reduce-scatter.2.cloned.1.call-update) | async-done | bytes 49168 | tf_op jit(solution)/shard_map/reduce_scatter | solution.py:105
  97.2 1.4 %reshape.61 = bf16[2,4,3072]{2,1,0:T(4,128)(2,1)} reshape(bf16[8,3072]{1,0:T(8,128)(2,1)} %reduce-scatter.2.cloned.1.call-done) | data formatting | bytes 98304 | tf_op jit(solution)/shard_map/reshape | solution.py:111
  98.6 3.3 %all-to-all-start.1 = ((bf16[2,4,3072]{2,1,0:T(4,128)(2,1)}), bf16[2,4,3072]{2,1,0:T(4,128)(2,1)S(1)}, u32[]{:S(2)}, u32[]{:S(2)}) async-start(bf16[2,4,3072]{2,1,0:T(4,128)(2,1)} %reshape.61), calls=%async_computation.2 | async-start | bytes 98304 | tf_op jit(solution)/shard_map/all_to_all | solution.py:112
  102.2 3.7 %all-to-all-done.1 = bf16[2,4,3072]{2,1,0:T(4,128)(2,1)S(1)} async-done(((bf16[2,4,3072]{2,1,0:T(4,128)(2,1)}), bf16[2,4,3072]{2,1,0:T(4,128)(2,1)S(1)}, u32[]{:S(2)}, u32[]{:S(2)}) %all-to-all-start.1) | async-done | bytes 49184 | tf_op jit(solution)/shard_map/all_to_all | solution.py:112
  105.9 0.2 fusion.23
  106.2 0.6 reshape.62
  (34 shorter events, 1.0 us)
Async XLA Ops:
  7.2 90.0 %reduce-scatter.2.cloned.1.call-start = ((), (), s32[]{:S(2)}) async-start(), calls=%async_computation.3 | async-start | bytes 245760 | tf_op jit(solution)/shard_map/reduce_scatter | solution.py:105
  30.3 41.5 %copy-start = (bf16[2,2,3072]{2,1,0:T(2,128)(2,1)}, bf16[2,2,3072]{2,1,0:T(2,128)(2,1)S(1)}, u32[]{:S(2)}) copy-start(bf16[2,2,3072]{2,1,0:T(2,128)(2,1)S(1)} %reshape.59) | copy-start | bytes 73732
  57.8 15.9 %slice-start = ((s8[12582912]{0:T(1024)(128)(4,1)}), s8[4194304]{0:T(1024)(128)(4,1)S(1)}, s32[]{:S(2)}) async-start(s8[12582912]{0:T(1024)(128)(4,1)} %bitcast.56), calls=%async_computation.4 | async-start | bytes 8388608
  57.8 15.9 %slice-start.1 = ((s8[12582912]{0:T(1024)(128)(4,1)}), s8[4194304]{0:T(1024)(128)(4,1)S(1)}, s32[]{:S(2)}) async-start(s8[12582912]{0:T(1024)(128)(4,1)} %bitcast.56), calls=%async_computation.5 | async-start | bytes 8388608
  64.8 8.9 %slice-start.2 = ((s8[12582912]{0:T(1024)(128)(4,1)}), s8[4194304]{0:T(1024)(128)(4,1)S(1)}, s32[]{:S(2)}) async-start(s8[12582912]{0:T(1024)(128)(4,1)} %bitcast.56), calls=%async_computation.6 | async-start | bytes 8388608
  71.8 4.9 %copy-start.1 = (f32[2,2,2]{2,1,0:T(2,128)S(1)}, f32[2,2,2]{2,1,0:T(2,128)}, u32[]{:S(2)}) copy-start(f32[2,2,2]{2,1,0:T(2,128)} %param.21) | copy-start | bytes 100
  98.6 7.3 %all-to-all-start.1 = ((bf16[2,4,3072]{2,1,0:T(4,128)(2,1)}), bf16[2,4,3072]{2,1,0:T(4,128)(2,1)S(1)}, u32[]{:S(2)}, u32[]{:S(2)}) async-start(bf16[2,4,3072]{2,1,0:T(4,128)(2,1)} %reshape.61), calls=%async_computation.2 | async-start | bytes 98304 | tf_op jit(solution)/shard_map/all_to_all | solution.py:112
Sparse Core Ops, SparseCore 0:
  76.9 20.2 reduce-scatter.1
where the time goes:
time: 114 us
  blocking collectives  44.7 us (39%)
  waiting for transfers between devices  24.1 us (21%)
  matrix products  18.1 us (16%)
  between operations  14.2 us (12%)
  local copies, waits for them, and re-layouts  6.88 us (6%)
  starting transfers between devices  3.31 us (3%)
  other arithmetic  2.32 us (2%)
    reduce_scatter x1, waiting for transfers between devices, per_device(): lax.psum_scatter(jnp.dot(segment, down_rows, preferred_element_type=jnp.f...  20.3 us
    all_gather x1, blocking collectives, attend_gathered(): cache = lax.all_gather(prefix_kv, 'rows', axis=1, tiled=True)  17.4 us
    all_gather x1, blocking collectives, per_device(): lax.all_gather(arrived.reshape(experts * token_count, -1), 'rows', axis=0...  14.6 us
    dot_general x1, matrix products, per_device(): up_part = jnp.dot(segment, up_weights, preferred_element_type=jnp.float32)  7 us
    dot_general x1, matrix products, per_device(): gate = jnp.dot(segment, gate_weights, preferred_element_type=jnp.float32)  6.98 us
    all_to_all x1, blocking collectives, per_device(): lax.all_to_all(outgoing, 'experts', split_axis=0, concat_axis=0, tiled=True)  6.86 us
    all_to_all x1, waiting for transfers between devices, per_device(): lax.all_to_all(result, 'experts', split_axis=0, concat_axis=0, tiled=True)  3.71 us
    all_to_all x1, starting transfers between devices, per_device(): lax.all_to_all(result, 'experts', split_axis=0, concat_axis=0, tiled=True)  3.28 us
  transfers between devices with their start and end apart: 2, of which 2 were waited for; matrix products, arithmetic and copies ran while one was open for 0% of the time, Pallas kernels for 0%

commit v1 on v0

--- a/solution.py
+++ b/solution.py
@@ -1,11 +1,19 @@
+import functools
+
 import jax
 import jax.numpy as jnp
 from jax import lax
+from jax.experimental import pallas as pl
+from jax.experimental.pallas import tpu as pltpu
 from jax.sharding import PartitionSpec as P
 
 HEADS = 48
 KV_HEADS = 8
 HEAD_DIM = 128
+GROUP = HEADS // KV_HEADS
+
+VMEM = pltpu.VMEM
+MIB = 1 << 20
 
 
 def fresh_terms(queries, new_kv):
@@ -54,7 +62,7 @@
     return (weighted, totals)
 
 
-def per_device(
+def per_device_wide(
     queries,
     new_kv,
     prefix_kv,
@@ -118,6 +126,357 @@
     return (attn_out, moe_out)
 
 
+def call(body, outs, in_spaces, name, scratch=(), limit=16 * MIB, cost=None):
+    spaces = {"v": VMEM, "s": pltpu.SMEM, "a": pl.ANY}
+    single = not isinstance(outs, (list, tuple))
+    shapes = [outs] if single else list(outs)
+    specs = [pl.BlockSpec(memory_space=VMEM) for _ in shapes]
+    return pl.pallas_call(
+        body,
+        out_shape=shapes[0] if single else tuple(shapes),
+        in_specs=[pl.BlockSpec(memory_space=spaces[s]) for s in in_spaces],
+        out_specs=specs[0] if single else tuple(specs),
+        scratch_shapes=list(scratch),
+        compiler_params=pltpu.CompilerParams(vmem_limit_bytes=limit),
+        cost_estimate=cost,
+        name=name,
+    )
+
+
+class Plan:
+    def __init__(self, queries, new_kv, prefix_kv):
+        self.steps, self.conts, self.half = queries.shape
+        self.kv_local = new_kv.shape[-1] // HEAD_DIM
+        self.prompts, self.positions = prefix_kv.shape[:2]
+        self.tokens = self.steps * self.conts
+        self.block = self.prompts * self.positions * 2
+        self.fresh = self.block
+        self.query = self.fresh + 2 * self.tokens
+        self.resid = self.query + GROUP * self.tokens
+        self.prompt = self.resid + GROUP * self.tokens
+        self.rows = -(-(self.prompt + self.tokens) // 16) * 16
+
+
+def pack_body(plan, prompt_ref, q_ref, new_ref, prefix_ref, resid_ref, out_ref):
+    t, c = plan.tokens, plan.conts
+    base = lax.axis_index("experts") * plan.prompts
+    row = lax.broadcasted_iota(jnp.int32, (c, HEAD_DIM), 0)
+    local = jnp.zeros((c, HEAD_DIM), jnp.float32)
+    for i in range(c):
+        local = jnp.where(row == i, (prompt_ref[i] - base).astype(jnp.float32), local)
+    local = local.astype(jnp.bfloat16)
+    for h in range(plan.kv_local):
+        lanes = pl.ds(h * HEAD_DIM, HEAD_DIM)
+        for p in range(plan.prompts):
+            for k in range(plan.positions):
+                out_ref[h, pl.ds((p * plan.positions + k) * 2, 2), :] = prefix_ref[p, k, :, lanes]
+        for s in range(plan.steps):
+            for i in range(c):
+                out_ref[h, pl.ds(plan.fresh + (s * c + i) * 2, 2), :] = new_ref[s, i, :, lanes]
+            for g in range(GROUP):
+                head = pl.ds((h * GROUP + g) * HEAD_DIM, HEAD_DIM)
+                out_ref[h, pl.ds(plan.query + g * t + s * c, c), :] = q_ref[s, :, head]
+                out_ref[h, pl.ds(plan.resid + g * t + s * c, c), :] = resid_ref[s, :, head]
+            out_ref[h, pl.ds(plan.prompt + s * c, c), :] = local
+
+
+def attend_body(plan, rows, got_ref, gain_ref, x_ref, attn_ref, q_s, r_s, kv_s, p_s):
+    t, c = plan.tokens, plan.conts
+    total = rows * t
+    f32 = jnp.float32
+    for src in range(rows):
+        kv_s[pl.ds(src * plan.block, plan.block), :] = got_ref[src, pl.ds(0, plan.block), :]
+        kv_s[pl.ds(rows * plan.block + src * 2 * t, 2 * t), :] = got_ref[src, pl.ds(plan.fresh, 2 * t), :]
+        p_s[pl.ds(src * t, t), :] = got_ref[src, pl.ds(plan.prompt, t), :]
+        for g in range(GROUP):
+            q_s[pl.ds(g * total + src * t, t), :] = got_ref[src, pl.ds(plan.query + g * t, t), :]
+            r_s[pl.ds(g * total + src * t, t), :] = got_ref[src, pl.ds(plan.resid + g * t, t), :]
+    used = rows * plan.block + rows * 2 * t
+    spare = kv_s.shape[0] - used
+    if spare:
+        kv_s[pl.ds(used, spare), :] = jnp.zeros((spare, HEAD_DIM), jnp.bfloat16)
+    kv = kv_s[...]
+    scores = lax.dot_general(
+        q_s[...], kv, (((1,), (1,)), ((), ())), preferred_element_type=f32
+    ) * HEAD_DIM ** (-0.5)
+    shape = scores.shape
+    row = lax.broadcasted_iota(jnp.int32, shape, 0) % total
+    col = lax.broadcasted_iota(jnp.int32, shape, 1)
+    prompt = p_s[...].astype(f32)[:, :1]
+    prompt = jnp.concatenate([prompt] * GROUP, axis=0).astype(jnp.int32)
+    in_prefix = (col < rows * plan.block) & ((col % plan.block) // (2 * plan.positions) == prompt)
+    late = col - rows * plan.block
+    same = (late // (2 * t) == row // t) & (((late // 2) % t) % c == row % c)
+    seen = ((late // 2) % t) // c <= (row % t) // c
+    in_fresh = (late >= 0) & (col < used) & same & seen
+    live = (col % 2 == 0) & (in_prefix | in_fresh)
+    scores = jnp.where(live, scores, -jnp.inf)
+    highest = jnp.max(scores, axis=-1, keepdims=True)
+    expo = jnp.exp(scores - highest)
+    totals = jnp.sum(expo, axis=-1, keepdims=True)
+    weights = pltpu.roll(expo, 1, 1).astype(jnp.bfloat16)
+    out = jnp.dot(weights, kv, preferred_element_type=f32) / totals
+    attn = out.astype(jnp.bfloat16)
+    combined = attn.astype(f32) + r_s[...].astype(f32)
+    square = jnp.zeros((total, HEAD_DIM), f32)
+    pieces = x_ref.shape[0]
+    for g in range(GROUP):
+        part = combined[g * total : (g + 1) * total]
+        square = square + part * part
+        lanes = pl.ds(g * HEAD_DIM, HEAD_DIM)
+        gained = (part * gain_ref[:, lanes].astype(f32)).astype(jnp.bfloat16)
+        for piece in range(pieces):
+            x_ref[piece, :, lanes] = gained
+        attn_ref[:, lanes] = attn[g * total : (g + 1) * total]
+    square = jnp.sum(square, axis=-1, keepdims=True)
+    high = square.astype(jnp.bfloat16)
+    low = (square - high.astype(f32)).astype(jnp.bfloat16)
+    lane = lax.broadcasted_iota(jnp.int32, (total, HEAD_DIM), 1)
+    extra = jnp.where(lane == 0, high.astype(f32), jnp.where(lane == 1, low.astype(f32), 0.0))
+    extra = extra.astype(jnp.bfloat16)
+    for piece in range(pieces):
+        x_ref[piece, :, pl.ds(GROUP * HEAD_DIM, HEAD_DIM)] = extra
+
+
+def gate_up_half(offset, x_ref, gate_hbm, up_hbm, gate_buf, up_buf, sems, init):
+    chunks, _, width = x_ref.shape
+    depth = width - HEAD_DIM
+    copies = []
+    for k in range(chunks):
+        rows = pl.ds(offset + k * depth, depth)
+        pair = (
+            pltpu.make_async_copy(gate_hbm.at[0, rows], gate_buf.at[k], sems.at[0, k]),
+            pltpu.make_async_copy(up_hbm.at[0, rows], up_buf.at[k], sems.at[1, k]),
+        )
+        for copy in pair:
+            copy.start()
+        copies.append(pair)
+    gate, up = init
+    for k in range(chunks):
+        x = x_ref[k, :, pl.ds(0, depth)]
+        copies[k][0].wait()
+        part = jnp.dot(x, gate_buf[k], preferred_element_type=jnp.float32)
+        gate = part if gate is None else gate + part
+        copies[k][1].wait()
+        part = jnp.dot(x, up_buf[k], preferred_element_type=jnp.float32)
+        up = part if up is None else up + part
+    return gate, up
+
+
+def first_half_body(x_ref, gate_hbm, up_hbm, gate_ref, up_ref, gate_buf, up_buf, sems):
+    chunks, _, width = x_ref.shape
+    offset = lax.axis_index("heads") * (chunks * (width - HEAD_DIM))
+    gate, up = gate_up_half(offset, x_ref, gate_hbm, up_hbm, gate_buf, up_buf, sems, (None, None))
+    gate_ref[...] = gate
+    up_ref[...] = up
+
+
+def second_half_body(
+    x_ref, own_ref, gate_in, up_in, gate_hbm, up_hbm, hidden_ref, gate_buf, up_buf, sems
+):
+    chunks, _, width = x_ref.shape
+    depth = width - HEAD_DIM
+    half = chunks * depth
+    offset = (1 - lax.axis_index("heads")) * half
+    square = jnp.zeros((x_ref.shape[1], 1), jnp.float32)
+    for ref in (own_ref, x_ref):
+        for k in range(chunks):
+            extra = ref[k, :, pl.ds(depth, HEAD_DIM)].astype(jnp.float32)
+            square = square + jnp.sum(extra, axis=-1, keepdims=True)
+    scale = lax.rsqrt(square / (2 * half) + 1e-05)
+    gate, up = gate_up_half(
+        offset, x_ref, gate_hbm, up_hbm, gate_buf, up_buf, sems, (gate_in[...], up_in[...])
+    )
+    gate = gate * scale
+    up = up * scale
+    hidden_ref[...] = (gate / (1.0 + jnp.exp(-gate)) * up).astype(jnp.bfloat16)
+
+
+def down_first_body(hidden_ref, down_hbm, out_ref, buf, sems):
+    depth = hidden_ref.shape[1]
+    out_ref[...] = down_half(lax.axis_index("heads") * depth, hidden_ref, down_hbm, buf, sems)
+
+
+def down_half(offset, hidden_ref, down_hbm, buf, sems):
+    parts, depth, _ = buf.shape
+    copies = []
+    for k in range(parts):
+        rows = pl.ds(offset + k * depth, depth)
+        copy = pltpu.make_async_copy(down_hbm.at[0, rows], buf.at[k], sems.at[k])
+        copy.start()
+        copies.append(copy)
+    total = None
+    for k in range(parts):
+        copies[k].wait()
+        part = jnp.dot(
+            hidden_ref[:, pl.ds(k * depth, depth)], buf[k], preferred_element_type=jnp.float32
+        )
+        total = part if total is None else total + part
+    return total
+
+
+def down_second_body(rows, hidden_ref, own_ref, attn_ref, down_hbm, out_ref, buf, sems):
+    depth = hidden_ref.shape[1]
+    other = (1 - lax.axis_index("heads")) * depth
+    total = own_ref[...] + down_half(other, hidden_ref, down_hbm, buf, sems)
+    result = total.astype(jnp.bfloat16)
+    pieces, t, width = out_ref.shape
+    experts = pieces // rows
+    half = result.shape[1]
+    for r in range(rows):
+        attn = attn_ref[pl.ds(r * t, t), :]
+        for e in range(experts):
+            first = (e * rows + r) * t
+            out_ref[r * experts + e, :, pl.ds(0, half)] = result[first : first + t]
+            out_ref[r * experts + e, :, pl.ds(half, width - half)] = attn
+
+
+def mix_body(rows, routes_ref, gates_ref, got_ref, attn_ref, moe_ref):
+    pieces, t, width = got_ref.shape
+    experts = pieces // rows
+    steps, conts, half = moe_ref.shape
+    own = lax.axis_index("experts")
+    row = lax.broadcasted_iota(jnp.int32, (t, 1), 0)
+    mixture = jnp.zeros((t, half), jnp.float32)
+    for e in range(experts):
+        summed = jnp.zeros((t, half), jnp.float32)
+        for r in range(rows):
+            summed = summed + got_ref[r * experts + e, :, pl.ds(0, half)].astype(jnp.float32)
+        share = jnp.zeros((t, 1), jnp.float32)
+        for s in range(steps):
+            for c in range(conts):
+                amount = jnp.float32(0.0)
+                for k in range(routes_ref.shape[2]):
+                    amount = amount + jnp.where(routes_ref[s, c, k] == e, gates_ref[s, c, k], 0.0)
+                share = jnp.where(row == s * conts + c, amount, share)
+        mixture = mixture + share * summed.astype(jnp.bfloat16).astype(jnp.float32)
+    mixture = mixture.astype(jnp.bfloat16)
+    piece = width - half
+    for s in range(steps):
+        moe_ref[s] = mixture[s * conts : (s + 1) * conts]
+        for r in range(rows):
+            attn_ref[s, :, pl.ds(r * piece, piece)] = got_ref[
+                r * experts + own, pl.ds(s * conts, conts), pl.ds(half, piece)
+            ]
+
+
+def per_device(
+    queries,
+    new_kv,
+    prefix_kv,
+    cont_prompt,
+    resid,
+    norm_gain,
+    w_gate,
+    w_up,
+    w_down,
+    routes,
+    route_gates,
+):
+    rows, experts = lax.axis_size("rows"), lax.axis_size("experts")
+    plan = Plan(queries, new_kv, prefix_kv)
+    bf16, f32 = jnp.bfloat16, jnp.float32
+    shape = jax.ShapeDtypeStruct
+    piece = GROUP * HEAD_DIM
+    total = rows * plan.tokens
+    tokens = experts * total
+
+    packed = call(
+        functools.partial(pack_body, plan),
+        shape((rows, plan.rows, HEAD_DIM), bf16),
+        "svvvv",
+        "pack",
+    )(cont_prompt, queries, new_kv, prefix_kv, resid)
+    got = lax.all_to_all(packed, "rows", split_axis=0, concat_axis=0, tiled=True)
+
+    start = lax.axis_index("heads") * plan.half + lax.axis_index("rows") * piece
+    gain = lax.dynamic_slice_in_dim(norm_gain, start, piece).reshape(1, piece)
+    keys = -(-(rows * (plan.block + 2 * plan.tokens)) // 128) * 128
+    x, attn = call(
+        functools.partial(attend_body, plan, rows),
+        (shape((rows * experts, total, piece + HEAD_DIM), bf16), shape((total, piece), bf16)),
+        "vv",
+        "attend",
+        scratch=(
+            VMEM((GROUP * total, HEAD_DIM), bf16),
+            VMEM((GROUP * total, HEAD_DIM), bf16),
+            VMEM((keys, HEAD_DIM), bf16),
+            VMEM((total, HEAD_DIM), bf16),
+        ),
+    )(got, gain)
+    x = lax.all_to_all(x, ("rows", "experts"), split_axis=0, concat_axis=0, tiled=True)
+    own = x.reshape(rows, tokens, piece + HEAD_DIM)
+    swap = [(0, 1), (1, 0)]
+    other = lax.ppermute(own, "heads", swap)
+
+    hbm = functools.partial(pltpu.with_memory_space_constraint, memory_space=pltpu.HBM)
+    w_gate, w_up, w_down = hbm(w_gate), hbm(w_up), hbm(w_down)
+    units = w_gate.shape[2]
+    buffers = (
+        VMEM((rows, piece, units), bf16),
+        VMEM((rows, piece, units), bf16),
+        pltpu.SemaphoreType.DMA((2, rows)),
+    )
+    cost = pl.CostEstimate(
+        flops=4 * tokens * plan.half * units,
+        bytes_accessed=4 * plan.half * units,
+        transcendentals=0,
+    )
+    gate, up = call(
+        first_half_body,
+        (shape((tokens, units), f32), shape((tokens, units), f32)),
+        "vaa",
+        "first_half",
+        scratch=buffers,
+        limit=32 * MIB,
+        cost=cost,
+    )(own, w_gate, w_up)
+    hidden = call(
+        second_half_body,
+        shape((tokens, units), bf16),
+        "vvvvaa",
+        "second_half",
+        scratch=buffers,
+        limit=32 * MIB,
+        cost=cost,
+    )(other, own, gate, up, w_gate, w_up)
+    other_hidden = lax.ppermute(hidden, "heads", swap)
+    parts = 4
+    buffers = (
+        VMEM((parts, units // parts, plan.half), bf16),
+        pltpu.SemaphoreType.DMA((parts,)),
+    )
+    cost = pl.CostEstimate(
+        flops=2 * tokens * plan.half * units,
+        bytes_accessed=2 * plan.half * units,
+        transcendentals=0,
+    )
+    partial = call(
+        down_first_body,
+        shape((tokens, plan.half), f32),
+        "va",
+        "down_first",
+        scratch=buffers,
+        limit=32 * MIB,
+        cost=cost,
+    )(hidden, w_down)
+    blocks = call(
+        functools.partial(down_second_body, rows),
+        shape((rows * experts, plan.tokens, plan.half + piece), bf16),
+        "vvva",
+        "down_second",
+        scratch=buffers,
+        limit=32 * MIB,
+        cost=cost,
+    )(other_hidden, partial, attn, w_down)
+    blocks = lax.all_to_all(blocks, ("rows", "experts"), split_axis=0, concat_axis=0, tiled=True)
+    out = shape(queries.shape, bf16)
+    attn_out, moe_out = call(functools.partial(mix_body, rows), (out, out), "ssv", "mix")(
+        routes, route_gates, blocks
+    )
+    return (attn_out, moe_out)
+
+
 def solution(mesh):
     placed = (
         P(None, ("groups", "rows", "experts"), "heads"),
@@ -132,8 +491,10 @@
         P(None, ("groups", "rows", "experts"), None),
         P(None, ("groups", "rows", "experts"), None),
     )
+    sizes = mesh.shape
+    by_head = sizes["heads"] == 2 and sizes["rows"] * sizes["heads"] == KV_HEADS
     return jax.shard_map(
-        per_device,
+        per_device if by_head else per_device_wide,
         mesh=mesh,
         in_specs=placed,
         out_specs=(

time: 114 us -> 62.8 us (0.55)
  blocking collectives: 44.7 us -> 23.3 us
  Pallas kernels: 0 us -> 20.1 us
  matrix products: 18.1 us -> 0 us
  waiting for transfers between devices: 24.1 us -> 6.74 us
  between operations: 14.2 us -> 0.71 us
  starting transfers between devices: 3.31 us -> 6.92 us
  local copies, waits for them, and re-layouts: 6.88 us -> 4.5 us
  other arithmetic: 2.32 us -> 0 us
    all_gather x5 -> x0, blocking collectives: 37.8 us -> none  [the longest x1 17.4 us: attend_gathered(): cache = lax.all_gather(prefix_kv, 'rows', axis=1, tiled=True)]
    reduce_scatter x1 -> x0, waiting for transfers between devices: 20.3 us -> none  [per_device(): lax.psum_scatter(jnp.dot(segment, down_rows, preferred_element_type=jnp.f...]
    pallas_call x0 -> x7, Pallas kernels: none -> 20.1 us  [the longest x1 5.1 us: per_device(): call(second_half_body, shape((tokens, units), bf16), 'vvvvaa', 'second_ha...]
    dot_general x8 -> x0, matrix products: 18.1 us -> none  [the longest x1 7 us: per_device(): up_part = jnp.dot(segment, up_weights, preferred_element_type=jnp.float32)]
    all_to_all x1 -> x2, blocking collectives: 6.86 us -> 23.3 us  [the longest x1 11.9 us: per_device(): lax.all_to_all(blocks, ('rows', 'experts'), split_axis=0, concat_axis=0,...]
    all_to_all x1, starting transfers between devices: 3.28 us -> 6.35 us  [per_device(): lax.all_to_all(packed, 'rows', split_axis=0, concat_axis=0, tiled=True)]
    all_to_all x1, waiting for transfers between devices: 3.71 us -> 6.74 us  [per_device(): lax.all_to_all(packed, 'rows', split_axis=0, concat_axis=0, tiled=True)]
    reshape x5 -> x1, local copies, waits for them, and re-layouts: 2.89 us -> 0.01 us  [per_device(): gain = lax.dynamic_slice_in_dim(norm_gain, start, piece).reshape(1, piece)]
  transfers between devices with their start and end apart: 2 -> 3, of which waited for: 2 -> 1; matrix products, arithmetic and copies ran while one was open for 0% -> 1% of each run, Pallas kernels for 0% -> 13%
where the time goes in v1:
time: 62.8 us; the launch traced here: 62.3 us
  blocking collectives  23.3 us (37%)
  Pallas kernels  20.1 us (32%)
  starting transfers between devices  6.92 us (11%)
  waiting for transfers between devices  6.74 us (11%)
  local copies, waits for them, and re-layouts  4.5 us (7%)
  between operations  0.71 us (1%)
    all_to_all x1, blocking collectives, per_device(): lax.all_to_all(blocks, ('rows', 'experts'), split_axis=0, concat_axis=0,...  11.9 us
    all_to_all x1, blocking collectives, per_device(): lax.all_to_all(x, ('rows', 'experts'), split_axis=0, concat_axis=0, tiled...  11.4 us
    all_to_all x1, waiting for transfers between devices, per_device(): lax.all_to_all(packed, 'rows', split_axis=0, concat_axis=0, tiled=True)  6.74 us
    all_to_all x1, starting transfers between devices, per_device(): lax.all_to_all(packed, 'rows', split_axis=0, concat_axis=0, tiled=True)  6.35 us
    pallas_call x1, Pallas kernels, per_device(): call(second_half_body, shape((tokens, units), bf16), 'vvvvaa', 'second_ha...  5.1 us
    pallas_call x1, Pallas kernels, per_device(): call(first_half_body, (shape((tokens, units), f32), shape((tokens, units)...  5.08 us
    unnamed x14, local copies, waits for them, and re-layouts  3.73 us
    pallas_call x1, Pallas kernels, per_device(): call(functools.partial(down_second_body, rows), shape((rows * experts, pl...  3.26 us
  transfers between devices with their start and end apart: 3, of which 1 were waited for; matrix products, arithmetic and copies ran while one was open for 1% of the time, Pallas kernels for 13%

profile of v1, /device:TPU:0, one launch (start us, length us, event | category | flops | bytes accessed | tf_op | source)
XLA Modules:
  0.0 62.3 jit_solution(14359602998573908040)
XLA Ops:
  0.6 0.0 copy-start
  0.6 0.9 %copy-done = bf16[2,32,2,512]{3,2,1,0:T(2,128)(2,1)S(1)} copy-done((bf16[2,32,2,512]{3,2,1,0:T(2,128)(2,1)S(1)}, bf16[2,32,2,512]{3,2,1,0:T(2,128)(2,1)}, u32[]{:S(2)}) %copy-start) | copy-done | bytes 131096
  1.5 0.0 copy-start.1
  1.5 0.7 %copy-done.1 = bf16[2,2,3072]{2,1,0:T(2,128)(2,1)S(1)} copy-done((bf16[2,2,3072]{2,1,0:T(2,128)(2,1)S(1)}, bf16[2,2,3072]{2,1,0:T(2,128)(2,1)}, u32[]{:S(2)}) %copy-start.1) | copy-done | bytes 24600
  2.3 0.0 copy-start.2
  2.3 0.7 %copy-done.2 = bf16[2,2,3072]{2,1,0:T(2,128)(2,1)S(1)} copy-done((bf16[2,2,3072]{2,1,0:T(2,128)(2,1)S(1)}, bf16[2,2,3072]{2,1,0:T(2,128)(2,1)}, u32[]{:S(2)}) %copy-start.2) | copy-done | bytes 24600
  3.0 0.0 copy-start.3
  3.0 0.7 %copy-done.3 = bf16[2,2,2,512]{3,2,1,0:T(2,128)(2,1)S(1)} copy-done((bf16[2,2,2,512]{3,2,1,0:T(2,128)(2,1)S(1)}, bf16[2,2,2,512]{3,2,1,0:T(2,128)(2,1)}, u32[]{:S(2)}) %copy-start.3) | copy-done | bytes 8216
  3.7 0.0 copy-start.6
  3.7 0.7 %copy-done.6 = s32[2]{0:T(128)S(1)} copy-done((s32[2]{0:T(128)S(1)}, s32[2]{0:T(128)}, u32[]{:S(2)}) %copy-start.6) | copy-done | bytes 32
  4.4 1.5 %pack.1 = bf16[4,192,128]{2,1,0:T(8,128)(2,1)} custom-call(s32[2]{0:T(128)S(1)} %copy-done.6, bf16[2,2,3072]{2,1,0:T(2,128)(2,1)S(1)} %copy-done.1, bf16[2,2,2,512]{3,2,1,0:T(2,128)(2,1)S(1)} %copy-done.3, bf16[2,32,2,512]{3,2,1,0:T(2,128)(2,1)S(1)} %copy-done, bf16[2,2,3072]{2,1,0:T(2,128)(2,1)S(1)} %copy-done.2), custom_call_target="tpu_custom_call" | custom-call | tf_op jit(solution)/shard_map/pack/pallas_call | solution.py:384
  5.8 6.3 %all-to-all-start = ((bf16[4,192,128]{2,1,0:T(8,128)(2,1)}), bf16[4,192,128]{2,1,0:T(8,128)(2,1)S(1)}, u32[]{:S(2)}, u32[]{:S(2)}) async-start(bf16[4,192,128]{2,1,0:T(8,128)(2,1)} %pack.1), calls=%async_computation | async-start | bytes 393216 | tf_op jit(solution)/shard_map/all_to_all | solution.py:390
  12.2 0.8 %dynamic_slice.3 = bf16[768]{0:T(1024)(128)(2,1)S(1)} dynamic-slice(bf16[6144]{0:T(1024)(128)(2,1)} %param.16, s32[]{:T(128)S(6)} %select_n.3), dynamic_slice_sizes={768} | dynamic-slice | bytes 3076 | tf_op jit(solution)/shard_map/dynamic_slice | solution.py:393
  12.9 6.7 %all-to-all-done.got_ref = bf16[4,192,128]{2,1,0:T(8,128)(2,1)S(1)} async-done(((bf16[4,192,128]{2,1,0:T(8,128)(2,1)}), bf16[4,192,128]{2,1,0:T(8,128)(2,1)S(1)}, u32[]{:S(2)}, u32[]{:S(2)}) %all-to-all-start) | async-done | bytes 196640 | tf_op jit(solution)/shard_map/all_to_all | solution.py:390
  19.7 0.6 %attend.1 = (bf16[8,16,896]{2,1,0:T(8,128)(2,1)S(1)}, bf16[16,768]{1,0:T(8,128)(2,1)S(1)}) custom-call(bf16[4,192,128]{2,1,0:T(8,128)(2,1)S(1)} %all-to-all-done.got_ref, bf16[1,768]{1,0:T(2,128)(2,1)S(1)} %reshape.10.gain_ref), custom_call_target="tpu_custom_call" | custom-call | tf_op jit(solution)/shard_map/attend/pallas_call | solution.py:395
  20.3 11.4 %all_to_all.15 = bf16[8,16,896]{2,1,0:T(8,128)(2,1)S(1)} all-to-all(bf16[8,16,896]{2,1,0:T(8,128)(2,1)S(1)} %get-tuple-element.6), channel_id=1, replica_groups=mesh['groups'=2,'rows'=4,'experts'=2,'heads'=2] {'rows','experts'}, dimensions={0} | all-to-all | bytes 458752 | tf_op jit(solution)/shard_map/all_to_all | solution.py:407
  31.7 0.0 collective-permute-start
  31.7 5.1 %first_half.1 = (f32[32,1024]{1,0:T(8,128)S(1)}, f32[32,1024]{1,0:T(8,128)S(1)}) custom-call(bf16[4,32,896]{2,1,0:T(8,128)(2,1)S(1)} %bitcast.2, bf16[1,6144,1024]{2,1,0:T(8,128)(2,1)} %gate_hbm.3, bf16[1,6144,1024]{2,1,0:T(8,128)(2,1)} %up_hbm.3), custom_call_target="tpu_custom_call" | custom-call | flops 402653184 | bytes 12582912 | tf_op jit(solution)/shard_map/first_half/pallas_call | solution.py:425
  36.8 0.0 collective-permute-done.x_ref
  36.8 5.1 %second_half.1.hidden_ref = bf16[32,1024]{1,0:T(8,128)(2,1)S(1)} custom-call(bf16[4,32,896]{2,1,0:T(8,128)(2,1)S(1)} %collective-permute-done.x_ref, bf16[4,32,896]{2,1,0:T(8,128)(2,1)S(1)} %bitcast.3, f32[32,1024]{1,0:T(8,128)S(1)} %get-tuple-element.7.gate_in, f32[32,1024]{1,0:T(8,128)S(1)} %get-tuple-element.8.up_in, bf16[1,6144,1024]{2,1,0:T(8,128)(2,1)} %gate_hbm.3, ...), custom_call_target="tpu_custom_call" | custom-call | flops 402653184 | bytes 12582912 | tf_op jit(solution)/shard_map/second_half/pallas_call | solution.py:434
  42.0 0.0 copy-start.4
  42.0 0.0 copy-start.5
  42.0 0.6 collective-permute-start.1
  42.6 3.2 %down_first.1.own_ref = f32[32,3072]{1,0:T(8,128)S(1)} custom-call(bf16[32,1024]{1,0:T(8,128)(2,1)S(1)} %second_half.1.hidden_ref, bf16[1,2048,3072]{2,1,0:T(8,128)(2,1)} %down_hbm.3), custom_call_target="tpu_custom_call" | custom-call | flops 201326592 | bytes 6291456 | tf_op jit(solution)/shard_map/down_first/pallas_call | solution.py:454
  45.8 0.0 collective-permute-done.1.hidden_ref
  45.8 3.3 %down_second.1 = bf16[8,4,3840]{2,1,0:T(4,128)(2,1)S(1)} custom-call(bf16[32,1024]{1,0:T(8,128)(2,1)S(1)} %collective-permute-done.1.hidden_ref, f32[32,3072]{1,0:T(8,128)S(1)} %down_first.1.own_ref, bf16[16,768]{1,0:T(8,128)(2,1)S(1)} %get-tuple-element.9.attn_ref, bf16[1,2048,3072]{2,1,0:T(8,128)(2,1)} %down_hbm.3), custom_call_target="tpu_custom_call" | custom-call | flops 201326592 | bytes 6291456 | tf_op jit(solution)/shard_map/down_second/pallas_call | solution.py:463
  49.1 11.9 %all_to_all.16.got_ref = bf16[8,4,3840]{2,1,0:T(4,128)(2,1)S(1)} all-to-all(bf16[8,4,3840]{2,1,0:T(4,128)(2,1)S(1)} %down_second.1), channel_id=1, replica_groups=mesh['groups'=2,'rows'=4,'experts'=2,'heads'=2] {'rows','experts'}, dimensions={0} | all-to-all | bytes 491520 | tf_op jit(solution)/shard_map/all_to_all | solution.py:472
  61.0 0.0 copy-done.4
  61.0 0.0 copy-done.5
  61.0 1.3 %mix.1 = (bf16[2,2,3072]{2,1,0:T(2,128)(2,1)}, bf16[2,2,3072]{2,1,0:T(2,128)(2,1)}) custom-call(s32[2,2,2]{2,1,0:T(2,128)S(1)} %copy-done.4, f32[2,2,2]{2,1,0:T(2,128)S(1)} %copy-done.5, bf16[8,4,3840]{2,1,0:T(4,128)(2,1)S(1)} %all_to_all.16.got_ref), custom_call_target="tpu_custom_call" | custom-call | tf_op jit(solution)/shard_map/mix/pallas_call | solution.py:474
  (1 shorter events, 0.0 us)
Async XLA Ops:
  0.6 0.9 %copy-start = (bf16[2,32,2,512]{3,2,1,0:T(2,128)(2,1)S(1)}, bf16[2,32,2,512]{3,2,1,0:T(2,128)(2,1)}, u32[]{:S(2)}) copy-start(bf16[2,32,2,512]{3,2,1,0:T(2,128)(2,1)} %prefix_ref.1) | copy-start | bytes 393220
  1.5 0.7 %copy-start.1 = (bf16[2,2,3072]{2,1,0:T(2,128)(2,1)S(1)}, bf16[2,2,3072]{2,1,0:T(2,128)(2,1)}, u32[]{:S(2)}) copy-start(bf16[2,2,3072]{2,1,0:T(2,128)(2,1)} %q_ref.1) | copy-start | bytes 73732
  2.3 0.7 %copy-start.2 = (bf16[2,2,3072]{2,1,0:T(2,128)(2,1)S(1)}, bf16[2,2,3072]{2,1,0:T(2,128)(2,1)}, u32[]{:S(2)}) copy-start(bf16[2,2,3072]{2,1,0:T(2,128)(2,1)} %resid_ref.1) | copy-start | bytes 73732
  3.0 0.7 %copy-start.3 = (bf16[2,2,2,512]{3,2,1,0:T(2,128)(2,1)S(1)}, bf16[2,2,2,512]{3,2,1,0:T(2,128)(2,1)}, u32[]{:S(2)}) copy-start(bf16[2,2,2,512]{3,2,1,0:T(2,128)(2,1)} %new_ref.1) | copy-start | bytes 24580
  3.7 0.7 %copy-start.6 = (s32[2]{0:T(128)S(1)}, s32[2]{0:T(128)}, u32[]{:S(2)}) copy-start(s32[2]{0:T(128)} %prompt_ref.1) | copy-start | bytes 28
  5.8 13.9 %all-to-all-start = ((bf16[4,192,128]{2,1,0:T(8,128)(2,1)}), bf16[4,192,128]{2,1,0:T(8,128)(2,1)S(1)}, u32[]{:S(2)}, u32[]{:S(2)}) async-start(bf16[4,192,128]{2,1,0:T(8,128)(2,1)} %pack.1), calls=%async_computation | async-start | bytes 393216 | tf_op jit(solution)/shard_map/all_to_all | solution.py:390
  31.7 5.1 %collective-permute-start = (bf16[4,32,896]{2,1,0:T(8,128)(2,1)S(1)}, bf16[4,32,896]{2,1,0:T(8,128)(2,1)S(1)}, u32[]{:S(2)}, u32[]{:S(2)}) collective-permute-start(bf16[4,32,896]{2,1,0:T(8,128)(2,1)S(1)} %bitcast.1), channel_id=1, source_target_pairs={{0,1},{1,0},{2,3},{3,2},{4,5},{5,4},{6,7},{7,6},{8,9},{9,8},{10,11... | collective-permute-start | bytes 688136 | tf_op jit(solution)/shard_map/ppermute | solution.py:410
  42.0 19.1 %copy-start.4 = (s32[2,2,2]{2,1,0:T(2,128)S(1)}, s32[2,2,2]{2,1,0:T(2,128)}, u32[]{:S(2)}) copy-start(s32[2,2,2]{2,1,0:T(2,128)} %routes_ref.1) | copy-start | bytes 100
  42.0 19.0 %copy-start.5 = (f32[2,2,2]{2,1,0:T(2,128)S(1)}, f32[2,2,2]{2,1,0:T(2,128)}, u32[]{:S(2)}) copy-start(f32[2,2,2]{2,1,0:T(2,128)} %gates_ref.1) | copy-start | bytes 100
  42.0 3.8 %collective-permute-start.1 = (bf16[32,1024]{1,0:T(8,128)(2,1)S(1)}, bf16[32,1024]{1,0:T(8,128)(2,1)S(1)}, u32[]{:S(2)}, u32[]{:S(2)}) collective-permute-start(bf16[32,1024]{1,0:T(8,128)(2,1)S(1)} %second_half.1.hidden_ref), channel_id=1, source_target_pairs={{0,1},{1,0},{2,3},{3,2},{4,5},{5,4},{6,7},{7,6},{8,9},{9,8},{10,11... | collective-permute-start | bytes 196616 | tf_op jit(solution)/shard_map/ppermute | solution.py:443

commit v2 on v1

--- a/solution.py
+++ b/solution.py
@@ -126,7 +126,7 @@
     return (attn_out, moe_out)
 
 
-def call(body, outs, in_spaces, name, scratch=(), limit=16 * MIB, cost=None):
+def call(body, outs, in_spaces, name, scratch=(), limit=4 * MIB, cost=None):
     spaces = {"v": VMEM, "s": pltpu.SMEM, "a": pl.ANY}
     single = not isinstance(outs, (list, tuple))
     shapes = [outs] if single else list(outs)
@@ -157,7 +157,17 @@
         self.rows = -(-(self.prompt + self.tokens) // 16) * 16
 
 
-def pack_body(plan, prompt_ref, q_ref, new_ref, prefix_ref, resid_ref, out_ref):
+def pack_body(plan, prompt_hbm, q_hbm, new_hbm, prefix_hbm, resid_hbm, *rest):
+    outs, buffers, sems = rest[: plan.kv_local], rest[plan.kv_local : -1], rest[-1]
+    sources = (prompt_hbm, q_hbm, new_hbm, prefix_hbm, resid_hbm)
+    copies = []
+    for i, (source, buffer) in enumerate(zip(sources, buffers)):
+        copy = pltpu.make_async_copy(source, buffer, sems.at[i])
+        copy.start()
+        copies.append(copy)
+    for copy in copies:
+        copy.wait()
+    prompt_ref, q_ref, new_ref, prefix_ref, resid_ref = buffers
     t, c = plan.tokens, plan.conts
     base = lax.axis_index("experts") * plan.prompts
     row = lax.broadcasted_iota(jnp.int32, (c, HEAD_DIM), 0)
@@ -165,32 +175,42 @@
     for i in range(c):
         local = jnp.where(row == i, (prompt_ref[i] - base).astype(jnp.float32), local)
     local = local.astype(jnp.bfloat16)
-    for h in range(plan.kv_local):
-        lanes = pl.ds(h * HEAD_DIM, HEAD_DIM)
+    own = lax.axis_index("rows")
+    for k, out_ref in enumerate(outs):
+        h = own ^ k
+        lanes = pl.ds(pl.multiple_of(h * HEAD_DIM, HEAD_DIM), HEAD_DIM)
         for p in range(plan.prompts):
-            for k in range(plan.positions):
-                out_ref[h, pl.ds((p * plan.positions + k) * 2, 2), :] = prefix_ref[p, k, :, lanes]
+            for i in range(plan.positions):
+                out_ref[pl.ds((p * plan.positions + i) * 2, 2), :] = prefix_ref[p, i, :, lanes]
         for s in range(plan.steps):
             for i in range(c):
-                out_ref[h, pl.ds(plan.fresh + (s * c + i) * 2, 2), :] = new_ref[s, i, :, lanes]
+                out_ref[pl.ds(plan.fresh + (s * c + i) * 2, 2), :] = new_ref[s, i, :, lanes]
             for g in range(GROUP):
-                head = pl.ds((h * GROUP + g) * HEAD_DIM, HEAD_DIM)
-                out_ref[h, pl.ds(plan.query + g * t + s * c, c), :] = q_ref[s, :, head]
-                out_ref[h, pl.ds(plan.resid + g * t + s * c, c), :] = resid_ref[s, :, head]
-            out_ref[h, pl.ds(plan.prompt + s * c, c), :] = local
-
-
-def attend_body(plan, rows, got_ref, gain_ref, x_ref, attn_ref, q_s, r_s, kv_s, p_s):
+                head = pl.ds(pl.multiple_of((h * GROUP + g) * HEAD_DIM, HEAD_DIM), HEAD_DIM)
+                out_ref[pl.ds(plan.query + g * t + s * c, c), :] = q_ref[s, :, head]
+                out_ref[pl.ds(plan.resid + g * t + s * c, c), :] = resid_ref[s, :, head]
+            out_ref[pl.ds(plan.prompt + s * c, c), :] = local
+
+
+def attend_body(plan, rows, *refs):
+    pieces, (gain_ref, _, x_ref, attn_ref, q_s, r_s, kv_s, p_s) = refs[:rows], refs[rows:]
     t, c = plan.tokens, plan.conts
     total = rows * t
     f32 = jnp.float32
-    for src in range(rows):
-        kv_s[pl.ds(src * plan.block, plan.block), :] = got_ref[src, pl.ds(0, plan.block), :]
-        kv_s[pl.ds(rows * plan.block + src * 2 * t, 2 * t), :] = got_ref[src, pl.ds(plan.fresh, 2 * t), :]
-        p_s[pl.ds(src * t, t), :] = got_ref[src, pl.ds(plan.prompt, t), :]
-        for g in range(GROUP):
-            q_s[pl.ds(g * total + src * t, t), :] = got_ref[src, pl.ds(plan.query + g * t, t), :]
-            r_s[pl.ds(g * total + src * t, t), :] = got_ref[src, pl.ds(plan.resid + g * t, t), :]
+
+    def place(own):
+        for k, got_ref in enumerate(pieces):
+            src = own ^ k
+            kv_s[pl.ds(src * plan.block, plan.block), :] = got_ref[pl.ds(0, plan.block), :]
+            late = pl.ds(rows * plan.block + src * 2 * t, 2 * t)
+            kv_s[late, :] = got_ref[pl.ds(plan.fresh, 2 * t), :]
+            p_s[pl.ds(src * t, t), :] = got_ref[pl.ds(plan.prompt, t), :]
+            for g in range(GROUP):
+                q_s[pl.ds(g * total + src * t, t), :] = got_ref[pl.ds(plan.query + g * t, t), :]
+                r_s[pl.ds(g * total + src * t, t), :] = got_ref[pl.ds(plan.resid + g * t, t), :]
+
+    for own in range(rows):
+        pl.when(lax.axis_index("rows") == own)(functools.partial(place, own))
     used = rows * plan.block + rows * 2 * t
     spare = kv_s.shape[0] - used
     if spare:
@@ -238,87 +258,85 @@
         x_ref[piece, :, pl.ds(GROUP * HEAD_DIM, HEAD_DIM)] = extra
 
 
-def gate_up_half(offset, x_ref, gate_hbm, up_hbm, gate_buf, up_buf, sems, init):
+def stream(source, target, sems):
+    core = lax.axis_index("heads")
+    half = source.shape[1] // 2
+    parts = sems.shape[1]
+    step = half // parts
+    copies = []
+    for side in range(2):
+        first = (core if side == 0 else 1 - core) * half
+        copies.append(
+            [
+                pltpu.make_async_copy(
+                    source.at[0, pl.ds(first + k * step, step)],
+                    target.at[side, pl.ds(k * step, step)],
+                    sems.at[side, k],
+                )
+                for k in range(parts)
+            ]
+        )
+    for copy in copies[0] + copies[1]:
+        copy.start()
+    return copies
+
+
+def load_body(_, source, target, sems):
+    copies = stream(source, target, sems)
+    for copy in copies[0] + copies[1]:
+        copy.wait()
+
+
+def half_products(side, x_ref, weight, total, ready=None):
     chunks, _, width = x_ref.shape
     depth = width - HEAD_DIM
-    copies = []
     for k in range(chunks):
-        rows = pl.ds(offset + k * depth, depth)
-        pair = (
-            pltpu.make_async_copy(gate_hbm.at[0, rows], gate_buf.at[k], sems.at[0, k]),
-            pltpu.make_async_copy(up_hbm.at[0, rows], up_buf.at[k], sems.at[1, k]),
+        if ready is not None:
+            ready[k].wait()
+        part = jnp.dot(
+            x_ref[k, :, pl.ds(0, depth)],
+            weight[side, pl.ds(k * depth, depth)],
+            preferred_element_type=jnp.float32,
         )
-        for copy in pair:
-            copy.start()
-        copies.append(pair)
-    gate, up = init
-    for k in range(chunks):
-        x = x_ref[k, :, pl.ds(0, depth)]
-        copies[k][0].wait()
-        part = jnp.dot(x, gate_buf[k], preferred_element_type=jnp.float32)
-        gate = part if gate is None else gate + part
-        copies[k][1].wait()
-        part = jnp.dot(x, up_buf[k], preferred_element_type=jnp.float32)
-        up = part if up is None else up + part
-    return gate, up
-
-
-def first_half_body(x_ref, gate_hbm, up_hbm, gate_ref, up_ref, gate_buf, up_buf, sems):
-    chunks, _, width = x_ref.shape
-    offset = lax.axis_index("heads") * (chunks * (width - HEAD_DIM))
-    gate, up = gate_up_half(offset, x_ref, gate_hbm, up_hbm, gate_buf, up_buf, sems, (None, None))
-    gate_ref[...] = gate
-    up_ref[...] = up
+        total = part if total is None else total + part
+    return total
+
+
+def first_half_body(x_ref, gate_w, up_hbm, gate_ref, up_ref, up_w, sems):
+    copies = stream(up_hbm, up_w, sems)
+    gate_ref[...] = half_products(0, x_ref, gate_w, None)
+    up_ref[...] = half_products(0, x_ref, up_w, None, copies[0])
+    for copy in copies[1]:
+        copy.wait()
 
 
 def second_half_body(
-    x_ref, own_ref, gate_in, up_in, gate_hbm, up_hbm, hidden_ref, gate_buf, up_buf, sems
+    x_ref, own_ref, gate_in, up_in, gate_w, up_w, down_hbm, hidden_ref, down_w, sems
 ):
+    copies = stream(down_hbm, down_w, sems)
     chunks, _, width = x_ref.shape
     depth = width - HEAD_DIM
-    half = chunks * depth
-    offset = (1 - lax.axis_index("heads")) * half
     square = jnp.zeros((x_ref.shape[1], 1), jnp.float32)
     for ref in (own_ref, x_ref):
         for k in range(chunks):
             extra = ref[k, :, pl.ds(depth, HEAD_DIM)].astype(jnp.float32)
             square = square + jnp.sum(extra, axis=-1, keepdims=True)
-    scale = lax.rsqrt(square / (2 * half) + 1e-05)
-    gate, up = gate_up_half(
-        offset, x_ref, gate_hbm, up_hbm, gate_buf, up_buf, sems, (gate_in[...], up_in[...])
-    )
-    gate = gate * scale
-    up = up * scale
+    scale = lax.rsqrt(square / (2 * chunks * depth) + 1e-05)
+    gate = half_products(1, x_ref, gate_w, gate_in[...]) * scale
+    up = half_products(1, x_ref, up_w, up_in[...]) * scale
     hidden_ref[...] = (gate / (1.0 + jnp.exp(-gate)) * up).astype(jnp.bfloat16)
-
-
-def down_first_body(hidden_ref, down_hbm, out_ref, buf, sems):
-    depth = hidden_ref.shape[1]
-    out_ref[...] = down_half(lax.axis_index("heads") * depth, hidden_ref, down_hbm, buf, sems)
-
-
-def down_half(offset, hidden_ref, down_hbm, buf, sems):
-    parts, depth, _ = buf.shape
-    copies = []
-    for k in range(parts):
-        rows = pl.ds(offset + k * depth, depth)
-        copy = pltpu.make_async_copy(down_hbm.at[0, rows], buf.at[k], sems.at[k])
-        copy.start()
-        copies.append(copy)
-    total = None
-    for k in range(parts):
-        copies[k].wait()
-        part = jnp.dot(
-            hidden_ref[:, pl.ds(k * depth, depth)], buf[k], preferred_element_type=jnp.float32
-        )
-        total = part if total is None else total + part
-    return total
-
-
-def down_second_body(rows, hidden_ref, own_ref, attn_ref, down_hbm, out_ref, buf, sems):
-    depth = hidden_ref.shape[1]
-    other = (1 - lax.axis_index("heads")) * depth
-    total = own_ref[...] + down_half(other, hidden_ref, down_hbm, buf, sems)
+    for copy in copies[0] + copies[1]:
+        copy.wait()
+
+
+def down_first_body(hidden_ref, down_w, out_ref):
+    out_ref[...] = jnp.dot(hidden_ref[...], down_w[0], preferred_element_type=jnp.float32)
+
+
+def down_second_body(rows, hidden_ref, own_ref, attn_ref, down_w, out_ref):
+    total = own_ref[...] + jnp.dot(
+        hidden_ref[...], down_w[1], preferred_element_type=jnp.float32
+    )
     result = total.astype(jnp.bfloat16)
     pieces, t, width = out_ref.shape
     experts = pieces // rows
@@ -381,13 +399,33 @@
     total = rows * plan.tokens
     tokens = experts * total
 
+    hbm = functools.partial(pltpu.with_memory_space_constraint, memory_space=pltpu.HBM)
+    vmem = functools.partial(pltpu.with_memory_space_constraint, memory_space=VMEM)
+    sources = (cont_prompt, queries, new_kv, prefix_kv, resid)
     packed = call(
         functools.partial(pack_body, plan),
-        shape((rows, plan.rows, HEAD_DIM), bf16),
-        "svvvv",
+        (shape((plan.rows, HEAD_DIM), bf16),) * rows,
+        "aaaaa",
         "pack",
-    )(cont_prompt, queries, new_kv, prefix_kv, resid)
-    got = lax.all_to_all(packed, "rows", split_axis=0, concat_axis=0, tiled=True)
+        scratch=(pltpu.SMEM(cont_prompt.shape, jnp.int32),)
+        + tuple(VMEM(source.shape, bf16) for source in sources[1:])
+        + (pltpu.SemaphoreType.DMA((len(sources),)),),
+    )(*map(hbm, sources))
+    got = [
+        lax.ppermute(packed[k], "rows", [(i, i ^ k) for i in range(rows)]) if k else packed[0]
+        for k in range(rows)
+    ]
+
+    def resident(weight):
+        return VMEM((2, weight.shape[1] // 2, weight.shape[2]), bf16)
+
+    def reading(weight):
+        return pl.CostEstimate(flops=0, bytes_accessed=2 * weight.size, transcendentals=0)
+
+    sems = pltpu.SemaphoreType.DMA((2, rows))
+    gate_w = call(
+        load_body, resident(w_gate), "va", "load_gate", (sems,), MIB, reading(w_gate)
+    )(packed[0], hbm(w_gate))
 
     start = lax.axis_index("heads") * plan.half + lax.axis_index("rows") * piece
     gain = lax.dynamic_slice_in_dim(norm_gain, start, piece).reshape(1, piece)
@@ -395,7 +433,7 @@
     x, attn = call(
         functools.partial(attend_body, plan, rows),
         (shape((rows * experts, total, piece + HEAD_DIM), bf16), shape((total, piece), bf16)),
-        "vv",
+        "v" * (rows + 2),
         "attend",
         scratch=(
             VMEM((GROUP * total, HEAD_DIM), bf16),
@@ -403,72 +441,44 @@
             VMEM((keys, HEAD_DIM), bf16),
             VMEM((total, HEAD_DIM), bf16),
         ),
-    )(got, gain)
+    )(*got, gain, vmem(gate_w))
     x = lax.all_to_all(x, ("rows", "experts"), split_axis=0, concat_axis=0, tiled=True)
     own = x.reshape(rows, tokens, piece + HEAD_DIM)
     swap = [(0, 1), (1, 0)]
     other = lax.ppermute(own, "heads", swap)
 
-    hbm = functools.partial(pltpu.with_memory_space_constraint, memory_space=pltpu.HBM)
-    w_gate, w_up, w_down = hbm(w_gate), hbm(w_up), hbm(w_down)
     units = w_gate.shape[2]
-    buffers = (
-        VMEM((rows, piece, units), bf16),
-        VMEM((rows, piece, units), bf16),
-        pltpu.SemaphoreType.DMA((2, rows)),
-    )
-    cost = pl.CostEstimate(
-        flops=4 * tokens * plan.half * units,
-        bytes_accessed=4 * plan.half * units,
-        transcendentals=0,
-    )
-    gate, up = call(
+    gate, up, up_w = call(
         first_half_body,
-        (shape((tokens, units), f32), shape((tokens, units), f32)),
-        "vaa",
+        (shape((tokens, units), f32), shape((tokens, units), f32), resident(w_up)),
+        "vva",
         "first_half",
-        scratch=buffers,
-        limit=32 * MIB,
-        cost=cost,
-    )(own, w_gate, w_up)
-    hidden = call(
+        (sems,),
+        cost=reading(w_up),
+    )(own, vmem(gate_w), hbm(w_up))
+    hidden, down_w = call(
         second_half_body,
-        shape((tokens, units), bf16),
-        "vvvvaa",
+        (shape((tokens, units), bf16), resident(w_down)),
+        "vvvvvva",
         "second_half",
-        scratch=buffers,
-        limit=32 * MIB,
-        cost=cost,
-    )(other, own, gate, up, w_gate, w_up)
+        (sems,),
+        cost=reading(w_down),
+    )(other, own, gate, up, vmem(gate_w), vmem(up_w), hbm(w_down))
     other_hidden = lax.ppermute(hidden, "heads", swap)
-    parts = 4
-    buffers = (
-        VMEM((parts, units // parts, plan.half), bf16),
-        pltpu.SemaphoreType.DMA((parts,)),
-    )
-    cost = pl.CostEstimate(
-        flops=2 * tokens * plan.half * units,
-        bytes_accessed=2 * plan.half * units,
-        transcendentals=0,
-    )
     partial = call(
         down_first_body,
         shape((tokens, plan.half), f32),
-        "va",
+        "vv",
         "down_first",
-        scratch=buffers,
-        limit=32 * MIB,
-        cost=cost,
-    )(hidden, w_down)
+        cost=reading(w_down),
+    )(hidden, vmem(down_w))
     blocks = call(
         functools.partial(down_second_body, rows),
         shape((rows * experts, plan.tokens, plan.half + piece), bf16),
-        "vvva",
+        "vvvv",
         "down_second",
-        scratch=buffers,
-        limit=32 * MIB,
-        cost=cost,
-    )(other_hidden, partial, attn, w_down)
+        cost=reading(w_down),
+    )(other_hidden, partial, attn, vmem(down_w))
     blocks = lax.all_to_all(blocks, ("rows", "experts"), split_axis=0, concat_axis=0, tiled=True)
     out = shape(queries.shape, bf16)
     attn_out, moe_out = call(functools.partial(mix_body, rows), (out, out), "ssv", "mix")(

time: 62.8 us -> 55.6 us (0.89)
  waiting for transfers between devices: 6.74 us -> 0.4 us
  local copies, waits for them, and re-layouts: 4.5 us -> 0.78 us
  Pallas kernels: 20.1 us -> 22 us
  blocking collectives: 23.3 us -> 25.2 us
  starting transfers between devices: 6.92 us -> 6.28 us
    all_to_all x1 -> x0, waiting for transfers between devices: 6.74 us -> none  [per_device(): lax.all_to_all(packed, 'rows', split_axis=0, concat_axis=0, tiled=True)]
    all_to_all x1 -> x0, starting transfers between devices: 6.35 us -> none  [per_device(): lax.all_to_all(packed, 'rows', split_axis=0, concat_axis=0, tiled=True)]
    ppermute x0 -> x3, starting transfers between devices: none -> 5.71 us  [per_device(): lax.ppermute(packed[k], 'rows', [(i, i ^ k) for i in range(rows)])]
    pallas_call x3 -> x4, Pallas kernels: 9.81 us -> 13.9 us  [the longest x1 6.84 us: per_device(): call(second_half_body, (shape((tokens, units), bf16), resident(w_down)),...]
    unnamed x14 -> x4, local copies, waits for them, and re-layouts: 3.73 us -> 0.01 us
    pallas_call x1, Pallas kernels: 3.26 us -> 1.2 us  [per_device(): call(functools.partial(down_second_body, rows), shape((rows * experts, pl...]
    all_to_all x1, blocking collectives: 11.4 us -> 13.5 us  [per_device(): lax.all_to_all(x, ('rows', 'experts'), split_axis=0, concat_axis=0, tiled...]
  transfers between devices with their start and end apart: 3 -> 5, of which waited for: 1 -> 1; matrix products, arithmetic and copies ran while one was open for 1% -> 1% of each run, Pallas kernels for 13% -> 20%
where the time goes in v2:
time: 55.6 us; the launch traced here: 55.3 us
  blocking collectives  25.2 us (45%)
  Pallas kernels  22 us (40%)
  starting transfers between devices  6.28 us (11%)
  local copies, waits for them, and re-layouts  0.78 us (1%)
  between operations  0.7 us (1%)
    all_to_all x1, blocking collectives, per_device(): lax.all_to_all(x, ('rows', 'experts'), split_axis=0, concat_axis=0, tiled...  13.5 us
    all_to_all x1, blocking collectives, per_device(): lax.all_to_all(blocks, ('rows', 'experts'), split_axis=0, concat_axis=0,...  11.7 us
    pallas_call x1, Pallas kernels, per_device(): call(second_half_body, (shape((tokens, units), bf16), resident(w_down)),...  6.84 us
    ppermute x3, starting transfers between devices, per_device(): lax.ppermute(packed[k], 'rows', [(i, i ^ k) for i in range(rows)])  5.71 us
    pallas_call x1, Pallas kernels, per_device(): call(first_half_body, (shape((tokens, units), f32), shape((tokens, units)...  4.94 us
    pallas_call x1, Pallas kernels, per_device(): call(load_body, resident(w_gate), 'va', 'load_gate', (sems,), MIB, readin...  4.7 us
    pallas_call x1, Pallas kernels, per_device(): call(functools.partial(mix_body, rows), (out, out), 'ssv', 'mix')  1.27 us
    pallas_call x1, Pallas kernels, per_device(): call(functools.partial(pack_body, plan), (shape((plan.rows, HEAD_DIM), bf...  1.23 us
  transfers between devices with their start and end apart: 5, of which 1 were waited for; matrix products, arithmetic and copies ran while one was open for 1% of the time, Pallas kernels for 20%

profile of v2, /device:TPU:0, one launch (start us, length us, event | category | flops | bytes accessed | tf_op | source)
XLA Modules:
  0.0 55.3 jit_solution(3440684791923806409)
XLA Ops:
  0.6 1.2 %pack.1 = (bf16[192,128]{1,0:T(8,128)(2,1)S(1)}, bf16[192,128]{1,0:T(8,128)(2,1)S(1)}, bf16[192,128]{1,0:T(8,128)(2,1)S(1)}, bf16[192,128]{1,0:T(8,128)(2,1)S(1)}) custom-call(s32[2]{0:T(128)} %prompt_hbm.1, bf16[2,2,3072]{2,1,0:T(2,128)(2,1)} %q_hbm.1, bf16[2,2,2,512]{3,2,1,0:T(2,128)(2,1)} %new_hbm.1, bf16[2,32,2,512]{3,2,1,0:T(2,128)(2,1)} %prefix_hbm.1, ...), custom_call_target="tpu_custom_call" | custom-call | tf_op jit(solution)/shard_map/pack/pallas_call | solution.py:405
  1.9 3.1 %collective-permute-start = (bf16[192,128]{1,0:T(8,128)(2,1)S(1)}, bf16[192,128]{1,0:T(8,128)(2,1)S(1)}, u32[]{:S(2)}, u32[]{:S(2)}) collective-permute-start(bf16[192,128]{1,0:T(8,128)(2,1)S(1)} %get-tuple-element.14), channel_id=1, source_target_pairs={{0,4},{4,0},{8,12},{12,8},{1,5},{5,1},{9,13},{13,9},{2,6},{6,2},{1... | collective-permute-start | bytes 147464 | tf_op jit(solution)/shard_map/ppermute | solution.py:415
  5.0 2.6 %collective-permute-start.1 = (bf16[192,128]{1,0:T(8,128)(2,1)S(1)}, bf16[192,128]{1,0:T(8,128)(2,1)S(1)}, u32[]{:S(2)}, u32[]{:S(2)}) collective-permute-start(bf16[192,128]{1,0:T(8,128)(2,1)S(1)} %get-tuple-element.15), channel_id=1, source_target_pairs={{0,8},{4,12},{8,0},{12,4},{1,9},{5,13},{9,1},{13,5},{2,10},{6,14},... | collective-permute-start | bytes 147464 | tf_op jit(solution)/shard_map/ppermute | solution.py:415
  7.6 0.0 collective-permute-start.2
  7.6 0.8 %dynamic_slice.3 = bf16[768]{0:T(1024)(128)(2,1)S(1)} dynamic-slice(bf16[6144]{0:T(1024)(128)(2,1)} %param.16, s32[]{:T(128)S(6)} %select_n.3), dynamic_slice_sizes={768} | dynamic-slice | bytes 3076 | tf_op jit(solution)/shard_map/dynamic_slice | solution.py:431
  8.3 4.7 %load_gate.1.refs_5_.gate_w = bf16[2,3072,1024]{2,1,0:T(8,128)(2,1)S(1)} custom-call(bf16[192,128]{1,0:T(8,128)(2,1)S(1)} %get-tuple-element.13._.refs_0_, bf16[1,6144,1024]{2,1,0:T(8,128)(2,1)} %source.1), custom_call_target="tpu_custom_call" | custom-call | bytes 12582912 | tf_op jit(solution)/shard_map/load_gate/pallas_call | solution.py:426
  13.1 0.0 collective-permute-done.refs_1_
  13.1 0.0 collective-permute-done.1.refs_2_
  13.1 0.4 collective-permute-done.2.refs_3_
  13.5 0.7 %attend.1 = (bf16[8,16,896]{2,1,0:T(8,128)(2,1)S(1)}, bf16[16,768]{1,0:T(8,128)(2,1)S(1)}) custom-call(bf16[192,128]{1,0:T(8,128)(2,1)S(1)} %get-tuple-element.13._.refs_0_, bf16[192,128]{1,0:T(8,128)(2,1)S(1)} %collective-permute-done.refs_1_, bf16[192,128]{1,0:T(8,128)(2,1)S(1)} %collective-permute-done.1.refs_2_, ...), custom_call_target="tpu_custom_call" | custom-call | tf_op jit(solution)/shard_map/attend/pallas_call | solution.py:433
  14.1 13.5 %all_to_all.10 = bf16[8,16,896]{2,1,0:T(8,128)(2,1)S(1)} all-to-all(bf16[8,16,896]{2,1,0:T(8,128)(2,1)S(1)} %get-tuple-element.17), channel_id=1, replica_groups=mesh['groups'=2,'rows'=4,'experts'=2,'heads'=2] {'rows','experts'}, dimensions={0} | all-to-all | bytes 458752 | tf_op jit(solution)/shard_map/all_to_all | solution.py:445
  27.6 0.0 collective-permute-start.3
  27.6 4.9 %first_half.1 = (f32[32,1024]{1,0:T(8,128)S(1)}, f32[32,1024]{1,0:T(8,128)S(1)}, bf16[2,3072,1024]{2,1,0:T(8,128)(2,1)S(1)}) custom-call(bf16[4,32,896]{2,1,0:T(8,128)(2,1)S(1)} %bitcast.2, bf16[2,3072,1024]{2,1,0:T(8,128)(2,1)S(1)} %load_gate.1.refs_5_.gate_w, bf16[1,6144,1024]{2,1,0:T(8,128)(2,1)} %up_hbm.1), custom_call_target="tpu_custom_call" | custom-call | bytes 12582912 | tf_op jit(solution)/shard_map/first_half/pallas_call | solution.py:451
  32.5 0.0 collective-permute-done.3.x_ref
  32.5 6.8 %second_half.1 = (bf16[32,1024]{1,0:T(8,128)(2,1)S(1)}, bf16[2,1024,3072]{2,1,0:T(8,128)(2,1)S(1)}) custom-call(bf16[4,32,896]{2,1,0:T(8,128)(2,1)S(1)} %collective-permute-done.3.x_ref, bf16[4,32,896]{2,1,0:T(8,128)(2,1)S(1)} %bitcast.3, f32[32,1024]{1,0:T(8,128)S(1)} %get-tuple-element.18.gate_in, f32[32,1024]{1,0:T(8,128)S(1)} %get-tuple-element.19.up_in, ...), custom_call_target="tpu_custom_call" | custom-call | bytes 12582912 | tf_op jit(solution)/shard_map/second_half/pallas_call | solution.py:459
  39.4 0.6 %collective-permute-start.4 = (bf16[32,1024]{1,0:T(8,128)(2,1)S(1)}, bf16[32,1024]{1,0:T(8,128)(2,1)S(1)}, u32[]{:S(2)}, u32[]{:S(2)}) collective-permute-start(bf16[32,1024]{1,0:T(8,128)(2,1)S(1)} %get-tuple-element.21.hidden_ref), channel_id=1, source_target_pairs={{0,1},{1,0},{2,3},{3,2},{4,5},{5,4},{6,7},{7,6},{8,9},{9,8},{10,11... | collective-permute-start | bytes 196616 | tf_op jit(solution)/shard_map/ppermute | solution.py:467
  40.0 0.0 copy-start
  40.0 0.0 copy-start.1
  40.0 1.2 %down_first.1.own_ref = f32[32,3072]{1,0:T(8,128)S(1)} custom-call(bf16[32,1024]{1,0:T(8,128)(2,1)S(1)} %get-tuple-element.21.hidden_ref, bf16[2,1024,3072]{2,1,0:T(8,128)(2,1)S(1)} %get-tuple-element.22.down_w), custom_call_target="tpu_custom_call" | custom-call | bytes 12582912 | tf_op jit(solution)/shard_map/down_first/pallas_call | solution.py:468
  41.1 0.0 collective-permute-done.4.hidden_ref
  41.1 1.2 %down_second.1 = bf16[8,4,3840]{2,1,0:T(4,128)(2,1)S(1)} custom-call(bf16[32,1024]{1,0:T(8,128)(2,1)S(1)} %collective-permute-done.4.hidden_ref, f32[32,3072]{1,0:T(8,128)S(1)} %down_first.1.own_ref, bf16[16,768]{1,0:T(8,128)(2,1)S(1)} %get-tuple-element.23.attn_ref, bf16[2,1024,3072]{2,1,0:T(8,128)(2,1)S(1)} %get-tuple-element.22.down_w), custom_call_target="tpu_custom_call" | custom-call | bytes 12582912 | tf_op jit(solution)/shard_map/down_second/pallas_call | solution.py:475
  42.4 11.7 %all_to_all.11.got_ref = bf16[8,4,3840]{2,1,0:T(4,128)(2,1)S(1)} all-to-all(bf16[8,4,3840]{2,1,0:T(4,128)(2,1)S(1)} %down_second.1), channel_id=1, replica_groups=mesh['groups'=2,'rows'=4,'experts'=2,'heads'=2] {'rows','experts'}, dimensions={0} | all-to-all | bytes 491520 | tf_op jit(solution)/shard_map/all_to_all | solution.py:482
  54.1 0.0 copy-done
  54.1 0.0 copy-done.1
  54.1 1.3 %mix.1 = (bf16[2,2,3072]{2,1,0:T(2,128)(2,1)}, bf16[2,2,3072]{2,1,0:T(2,128)(2,1)}) custom-call(s32[2,2,2]{2,1,0:T(2,128)S(1)} %copy-done, f32[2,2,2]{2,1,0:T(2,128)S(1)} %copy-done.1, bf16[8,4,3840]{2,1,0:T(4,128)(2,1)S(1)} %all_to_all.11.got_ref), custom_call_target="tpu_custom_call" | custom-call | tf_op jit(solution)/shard_map/mix/pallas_call | solution.py:484
  (1 shorter events, 0.0 us)
Async XLA Ops:
  1.9 11.2 %collective-permute-start = (bf16[192,128]{1,0:T(8,128)(2,1)S(1)}, bf16[192,128]{1,0:T(8,128)(2,1)S(1)}, u32[]{:S(2)}, u32[]{:S(2)}) collective-permute-start(bf16[192,128]{1,0:T(8,128)(2,1)S(1)} %get-tuple-element.14), channel_id=1, source_target_pairs={{0,4},{4,0},{8,12},{12,8},{1,5},{5,1},{9,13},{13,9},{2,6},{6,2},{1... | collective-permute-start | bytes 147464 | tf_op jit(solution)/shard_map/ppermute | solution.py:415
  5.0 8.1 %collective-permute-start.1 = (bf16[192,128]{1,0:T(8,128)(2,1)S(1)}, bf16[192,128]{1,0:T(8,128)(2,1)S(1)}, u32[]{:S(2)}, u32[]{:S(2)}) collective-permute-start(bf16[192,128]{1,0:T(8,128)(2,1)S(1)} %get-tuple-element.15), channel_id=1, source_target_pairs={{0,8},{4,12},{8,0},{12,4},{1,9},{5,13},{9,1},{13,5},{2,10},{6,14},... | collective-permute-start | bytes 147464 | tf_op jit(solution)/shard_map/ppermute | solution.py:415
  7.6 5.9 %collective-permute-start.2 = (bf16[192,128]{1,0:T(8,128)(2,1)S(1)}, bf16[192,128]{1,0:T(8,128)(2,1)S(1)}, u32[]{:S(2)}, u32[]{:S(2)}) collective-permute-start(bf16[192,128]{1,0:T(8,128)(2,1)S(1)} %get-tuple-element.16), channel_id=1, source_target_pairs={{0,12},{4,8},{8,4},{12,0},{1,13},{5,9},{9,5},{13,1},{2,14},{6,10},... | collective-permute-start | bytes 147464 | tf_op jit(solution)/shard_map/ppermute | solution.py:415
  27.6 5.0 %collective-permute-start.3 = (bf16[4,32,896]{2,1,0:T(8,128)(2,1)S(1)}, bf16[4,32,896]{2,1,0:T(8,128)(2,1)S(1)}, u32[]{:S(2)}, u32[]{:S(2)}) collective-permute-start(bf16[4,32,896]{2,1,0:T(8,128)(2,1)S(1)} %bitcast.1), channel_id=1, source_target_pairs={{0,1},{1,0},{2,3},{3,2},{4,5},{5,4},{6,7},{7,6},{8,9},{9,8},{10,11... | collective-permute-start | bytes 688136 | tf_op jit(solution)/shard_map/ppermute | solution.py:448
  39.4 1.8 %collective-permute-start.4 = (bf16[32,1024]{1,0:T(8,128)(2,1)S(1)}, bf16[32,1024]{1,0:T(8,128)(2,1)S(1)}, u32[]{:S(2)}, u32[]{:S(2)}) collective-permute-start(bf16[32,1024]{1,0:T(8,128)(2,1)S(1)} %get-tuple-element.21.hidden_ref), channel_id=1, source_target_pairs={{0,1},{1,0},{2,3},{3,2},{4,5},{5,4},{6,7},{7,6},{8,9},{9,8},{10,11... | collective-permute-start | bytes 196616 | tf_op jit(solution)/shard_map/ppermute | solution.py:467
  40.0 14.1 %copy-start = (s32[2,2,2]{2,1,0:T(2,128)S(1)}, s32[2,2,2]{2,1,0:T(2,128)}, u32[]{:S(2)}) copy-start(s32[2,2,2]{2,1,0:T(2,128)} %routes_ref.1) | copy-start | bytes 100
  40.0 14.1 %copy-start.1 = (f32[2,2,2]{2,1,0:T(2,128)S(1)}, f32[2,2,2]{2,1,0:T(2,128)}, u32[]{:S(2)}) copy-start(f32[2,2,2]{2,1,0:T(2,128)} %gates_ref.1) | copy-start | bytes 100

commit v3 on v2

--- a/solution.py
+++ b/solution.py
@@ -239,81 +239,102 @@
     attn = out.astype(jnp.bfloat16)
     combined = attn.astype(f32) + r_s[...].astype(f32)
     square = jnp.zeros((total, HEAD_DIM), f32)
-    pieces = x_ref.shape[0]
     for g in range(GROUP):
         part = combined[g * total : (g + 1) * total]
         square = square + part * part
         lanes = pl.ds(g * HEAD_DIM, HEAD_DIM)
-        gained = (part * gain_ref[:, lanes].astype(f32)).astype(jnp.bfloat16)
-        for piece in range(pieces):
-            x_ref[piece, :, lanes] = gained
+        x_ref[:, lanes] = (part * gain_ref[:, lanes].astype(f32)).astype(jnp.bfloat16)
         attn_ref[:, lanes] = attn[g * total : (g + 1) * total]
     square = jnp.sum(square, axis=-1, keepdims=True)
     high = square.astype(jnp.bfloat16)
     low = (square - high.astype(f32)).astype(jnp.bfloat16)
     lane = lax.broadcasted_iota(jnp.int32, (total, HEAD_DIM), 1)
     extra = jnp.where(lane == 0, high.astype(f32), jnp.where(lane == 1, low.astype(f32), 0.0))
-    extra = extra.astype(jnp.bfloat16)
-    for piece in range(pieces):
-        x_ref[piece, :, pl.ds(GROUP * HEAD_DIM, HEAD_DIM)] = extra
-
-
-def stream(source, target, sems):
+    x_ref[:, pl.ds(GROUP * HEAD_DIM, HEAD_DIM)] = extra.astype(jnp.bfloat16)
+
+
+def other_half(side):
     core = lax.axis_index("heads")
-    half = source.shape[1] // 2
-    parts = sems.shape[1]
-    step = half // parts
-    copies = []
-    for side in range(2):
-        first = (core if side == 0 else 1 - core) * half
-        copies.append(
-            [
-                pltpu.make_async_copy(
-                    source.at[0, pl.ds(first + k * step, step)],
-                    target.at[side, pl.ds(k * step, step)],
-                    sems.at[side, k],
-                )
-                for k in range(parts)
-            ]
+    return 1 - core if side else core
+
+
+def stream(source, side, target, sems):
+    parts = sems.shape[0]
+    step = source.shape[1] // 2 // parts
+    first = other_half(side) * (step * parts)
+    copies = [
+        pltpu.make_async_copy(
+            source.at[0, pl.ds(first + k * step, step)], target.at[pl.ds(k * step, step)], sems.at[k]
         )
-    for copy in copies[0] + copies[1]:
+        for k in range(parts)
+    ]
+    for copy in copies:
         copy.start()
     return copies
 
 
-def load_body(_, source, target, sems):
-    copies = stream(source, target, sems)
-    for copy in copies[0] + copies[1]:
+def finish(copies):
+    for copy in copies:
         copy.wait()
 
 
-def half_products(side, x_ref, weight, total, ready=None):
+def load_body(sides, _, source, *rest):
+    targets, sems = rest[:-1], rest[-1]
+    copies = [stream(source, side, target, sems.at[side]) for side, target in zip(sides, targets)]
+    for each in copies:
+        finish(each)
+
+
+def merge_body(own_ref, peer_ref, _, out_ref):
+    total = own_ref.shape[0]
+    out_ref[pl.ds(0, total), :] = own_ref[...]
+    out_ref[pl.ds(total, total), :] = peer_ref[...]
+
+
+def stack_body(*refs):
+    *pieces, _, out_ref = refs
+    for k, ref in enumerate(pieces):
+        out_ref[k] = ref[...]
+
+
+def products(x, weight, src, total):
+    depth = x.shape[1]
+    part = jnp.dot(
+        x,
+        weight[pl.ds(pl.multiple_of(src * depth, depth), depth)],
+        preferred_element_type=jnp.float32,
+    )
+    return part if total is None else total + part
+
+
+def own_chunk_body(x_ref, gate_w, up_w, up_hbm, gate_ref, up_ref, up_other, sems):
+    copies = stream(up_hbm, 1, up_other, sems.at[0])
+    depth = x_ref.shape[1] - HEAD_DIM
+    x = x_ref[:, pl.ds(0, depth)]
+    own = lax.axis_index("rows")
+    gate_ref[...] = products(x, gate_w, own, None)
+    up_ref[...] = products(x, up_w, own, None)
+    finish(copies)
+
+
+def first_half_body(x_ref, gate_in, up_in, gate_w, up_w, down_hbm, gate_ref, up_ref, down_w, sems):
+    copies = stream(down_hbm, 0, down_w, sems.at[0])
     chunks, _, width = x_ref.shape
-    depth = width - HEAD_DIM
-    for k in range(chunks):
-        if ready is not None:
-            ready[k].wait()
-        part = jnp.dot(
-            x_ref[k, :, pl.ds(0, depth)],
-            weight[side, pl.ds(k * depth, depth)],
-            preferred_element_type=jnp.float32,
-        )
-        total = part if total is None else total + part
-    return total
-
-
-def first_half_body(x_ref, gate_w, up_hbm, gate_ref, up_ref, up_w, sems):
-    copies = stream(up_hbm, up_w, sems)
-    gate_ref[...] = half_products(0, x_ref, gate_w, None)
-    up_ref[...] = half_products(0, x_ref, up_w, None, copies[0])
-    for copy in copies[1]:
-        copy.wait()
+    own = lax.axis_index("rows")
+    gate, up = gate_in[...], up_in[...]
+    for k in range(1, chunks):
+        x = x_ref[k, :, pl.ds(0, width - HEAD_DIM)]
+        gate = products(x, gate_w, own ^ k, gate)
+        up = products(x, up_w, own ^ k, up)
+    gate_ref[...] = gate
+    up_ref[...] = up
+    finish(copies)
 
 
 def second_half_body(
     x_ref, own_ref, gate_in, up_in, gate_w, up_w, down_hbm, hidden_ref, down_w, sems
 ):
-    copies = stream(down_hbm, down_w, sems)
+    copies = stream(down_hbm, 1, down_w, sems.at[0])
     chunks, _, width = x_ref.shape
     depth = width - HEAD_DIM
     square = jnp.zeros((x_ref.shape[1], 1), jnp.float32)
@@ -322,31 +343,37 @@
             extra = ref[k, :, pl.ds(depth, HEAD_DIM)].astype(jnp.float32)
             square = square + jnp.sum(extra, axis=-1, keepdims=True)
     scale = lax.rsqrt(square / (2 * chunks * depth) + 1e-05)
-    gate = half_products(1, x_ref, gate_w, gate_in[...]) * scale
-    up = half_products(1, x_ref, up_w, up_in[...]) * scale
+    own = lax.axis_index("rows")
+    gate, up = gate_in[...], up_in[...]
+    for k in range(chunks):
+        x = x_ref[k, :, pl.ds(0, depth)]
+        gate = products(x, gate_w, own ^ k, gate)
+        up = products(x, up_w, own ^ k, up)
+    gate = gate * scale
+    up = up * scale
     hidden_ref[...] = (gate / (1.0 + jnp.exp(-gate)) * up).astype(jnp.bfloat16)
-    for copy in copies[0] + copies[1]:
-        copy.wait()
+    finish(copies)
 
 
 def down_first_body(hidden_ref, down_w, out_ref):
-    out_ref[...] = jnp.dot(hidden_ref[...], down_w[0], preferred_element_type=jnp.float32)
+    out_ref[...] = jnp.dot(hidden_ref[...], down_w[...], preferred_element_type=jnp.float32)
 
 
 def down_second_body(rows, hidden_ref, own_ref, attn_ref, down_w, out_ref):
     total = own_ref[...] + jnp.dot(
-        hidden_ref[...], down_w[1], preferred_element_type=jnp.float32
+        hidden_ref[...], down_w[...], preferred_element_type=jnp.float32
     )
     result = total.astype(jnp.bfloat16)
     pieces, t, width = out_ref.shape
     experts = pieces // rows
     half = result.shape[1]
+    own = lax.axis_index("experts")
     for r in range(rows):
         attn = attn_ref[pl.ds(r * t, t), :]
         for e in range(experts):
             first = (e * rows + r) * t
-            out_ref[r * experts + e, :, pl.ds(0, half)] = result[first : first + t]
-            out_ref[r * experts + e, :, pl.ds(half, width - half)] = attn
+            out_ref[r * experts + (own ^ e), :, pl.ds(0, half)] = result[first : first + t]
+            out_ref[r * experts + (own ^ e), :, pl.ds(half, width - half)] = attn
 
 
 def mix_body(rows, routes_ref, gates_ref, got_ref, attn_ref, moe_ref):
@@ -416,23 +443,36 @@
         for k in range(rows)
     ]
 
-    def resident(weight):
-        return VMEM((2, weight.shape[1] // 2, weight.shape[2]), bf16)
-
-    def reading(weight):
-        return pl.CostEstimate(flops=0, bytes_accessed=2 * weight.size, transcendentals=0)
+    def half_of(weight):
+        return VMEM((weight.shape[1] // 2, weight.shape[2]), bf16)
+
+    def reading(weight, halves=1):
+        return pl.CostEstimate(
+            flops=tokens * weight.size * halves,
+            bytes_accessed=weight.size * halves,
+            transcendentals=0,
+        )
 
     sems = pltpu.SemaphoreType.DMA((2, rows))
-    gate_w = call(
-        load_body, resident(w_gate), "va", "load_gate", (sems,), MIB, reading(w_gate)
-    )(packed[0], hbm(w_gate))
+    gate_own, gate_other = map(
+        vmem,
+        call(
+            functools.partial(load_body, (0, 1)),
+            (half_of(w_gate), half_of(w_gate)),
+            "va",
+            "load_gate",
+            (sems,),
+            MIB,
+            reading(w_gate, 2),
+        )(packed[0], hbm(w_gate)),
+    )
 
     start = lax.axis_index("heads") * plan.half + lax.axis_index("rows") * piece
     gain = lax.dynamic_slice_in_dim(norm_gain, start, piece).reshape(1, piece)
     keys = -(-(rows * (plan.block + 2 * plan.tokens)) // 128) * 128
     x, attn = call(
         functools.partial(attend_body, plan, rows),
-        (shape((rows * experts, total, piece + HEAD_DIM), bf16), shape((total, piece), bf16)),
+        (shape((total, piece + HEAD_DIM), bf16), shape((total, piece), bf16)),
         "v" * (rows + 2),
         "attend",
         scratch=(
@@ -441,29 +481,60 @@
             VMEM((keys, HEAD_DIM), bf16),
             VMEM((total, HEAD_DIM), bf16),
         ),
-    )(*got, gain, vmem(gate_w))
-    x = lax.all_to_all(x, ("rows", "experts"), split_axis=0, concat_axis=0, tiled=True)
-    own = x.reshape(rows, tokens, piece + HEAD_DIM)
+    )(*got, gain, gate_own)
     swap = [(0, 1), (1, 0)]
+    peer = lax.ppermute(x, "experts", swap)
+    up_own = vmem(
+        call(
+            functools.partial(load_body, (0,)),
+            half_of(w_up),
+            "va",
+            "load_up",
+            (sems,),
+            MIB,
+            reading(w_up),
+        )(x, hbm(w_up))
+    )
+    merged = call(merge_body, shape((tokens, piece + HEAD_DIM), bf16), "vvv", "merge")(
+        x, peer, up_own
+    )
+    chunks = [
+        lax.ppermute(merged, "rows", [(i, i ^ k) for i in range(rows)]) if k else merged
+        for k in range(rows)
+    ]
+    units = w_gate.shape[2]
+    products_of = shape((tokens, units), f32)
+    gate, up, up_other = call(
+        own_chunk_body,
+        (products_of, products_of, half_of(w_up)),
+        "vvva",
+        "own_chunk",
+        (sems,),
+        cost=reading(w_up),
+    )(merged, gate_own, up_own, hbm(w_up))
+    own = call(
+        stack_body,
+        shape((rows, tokens, piece + HEAD_DIM), bf16),
+        "v" * (rows + 1),
+        "stack",
+    )(*chunks, vmem(up_other))
     other = lax.ppermute(own, "heads", swap)
-
-    units = w_gate.shape[2]
-    gate, up, up_w = call(
+    gate, up, down_own = call(
         first_half_body,
-        (shape((tokens, units), f32), shape((tokens, units), f32), resident(w_up)),
-        "vva",
+        (products_of, products_of, half_of(w_down)),
+        "vvvvva",
         "first_half",
         (sems,),
-        cost=reading(w_up),
-    )(own, vmem(gate_w), hbm(w_up))
-    hidden, down_w = call(
+        cost=reading(w_down),
+    )(own, gate, up, gate_own, up_own, hbm(w_down))
+    hidden, down_other = call(
         second_half_body,
-        (shape((tokens, units), bf16), resident(w_down)),
+        (shape((tokens, units), bf16), half_of(w_down)),
         "vvvvvva",
         "second_half",
         (sems,),
         cost=reading(w_down),
-    )(other, own, gate, up, vmem(gate_w), vmem(up_w), hbm(w_down))
+    )(other, own, gate, up, gate_other, vmem(up_other), hbm(w_down))
     other_hidden = lax.ppermute(hidden, "heads", swap)
     partial = call(
         down_first_body,
@@ -471,14 +542,14 @@
         "vv",
         "down_first",
         cost=reading(w_down),
-    )(hidden, vmem(down_w))
+    )(hidden, vmem(down_own))
     blocks = call(
         functools.partial(down_second_body, rows),
         shape((rows * experts, plan.tokens, plan.half + piece), bf16),
         "vvvv",
         "down_second",
         cost=reading(w_down),
-    )(other_hidden, partial, attn, vmem(down_w))
+    )(other_hidden, partial, attn, vmem(down_other))
     blocks = lax.all_to_all(blocks, ("rows", "experts"), split_axis=0, concat_axis=0, tiled=True)
     out = shape(queries.shape, bf16)
     attn_out, moe_out = call(functools.partial(mix_body, rows), (out, out), "ssv", "mix")(
@@ -502,7 +573,12 @@
         P(None, ("groups", "rows", "experts"), None),
     )
     sizes = mesh.shape
-    by_head = sizes["heads"] == 2 and sizes["rows"] * sizes["heads"] == KV_HEADS
+    by_head = (
+        sizes["heads"] == 2
+        and sizes["experts"] == 2
+        and sizes["rows"] == 4
+        and sizes["rows"] * sizes["heads"] == KV_HEADS
+    )
     return jax.shard_map(
         per_device if by_head else per_device_wide,
         mesh=mesh,

time: 55.6 us -> 54.1 us (0.973)
  blocking collectives: 25.2 us -> 13.1 us
  starting transfers between devices: 6.28 us -> 12.3 us
  Pallas kernels: 22 us -> 25.9 us
  waiting for transfers between devices: 0.4 us -> 1.12 us
    all_to_all x1 -> x0, blocking collectives: 13.5 us -> none  [per_device(): lax.all_to_all(x, ('rows', 'experts'), split_axis=0, concat_axis=0, tiled...]
    ppermute x0 -> x4, starting transfers between devices: none -> 5.95 us  [the longest x3 4.45 us: per_device(): lax.ppermute(merged, 'rows', [(i, i ^ k) for i in range(rows)])]
    pallas_call x4 -> x8, Pallas kernels: 17.1 us -> 21 us  [the longest x1 5.05 us: per_device(): call(second_half_body, (shape((tokens, units), bf16), half_of(w_down)), '...]
    all_to_all x1, blocking collectives: 11.7 us -> 13.1 us  [per_device(): lax.all_to_all(blocks, ('rows', 'experts'), split_axis=0, concat_axis=0,...]
    ppermute x0 -> x4, waiting for transfers between devices: none -> 0.72 us  [the longest x3 0.72 us: per_device(): lax.ppermute(merged, 'rows', [(i, i ^ k) for i in range(rows)])]
  transfers between devices with their start and end apart: 5 -> 9, of which waited for: 1 -> 2; matrix products, arithmetic and copies ran while one was open for 1% -> 1% of each run, Pallas kernels for 20% -> 31%
where the time goes in v3:
time: 54.1 us; the launch traced here: 53.9 us
  Pallas kernels  25.9 us (48%)
  blocking collectives  13.1 us (24%)
  starting transfers between devices  12.3 us (23%)
  waiting for transfers between devices  1.12 us (2%)
  local copies, waits for them, and re-layouts  0.78 us (1%)
  between operations  0.76 us (1%)
    all_to_all x1, blocking collectives, per_device(): lax.all_to_all(blocks, ('rows', 'experts'), split_axis=0, concat_axis=0,...  13.1 us
    ppermute x3, starting transfers between devices, per_device(): lax.ppermute(packed[k], 'rows', [(i, i ^ k) for i in range(rows)])  5.71 us
    pallas_call x1, Pallas kernels, per_device(): call(second_half_body, (shape((tokens, units), bf16), half_of(w_down)), '...  5.05 us
    pallas_call x1, Pallas kernels, per_device(): call(functools.partial(load_body, (0, 1)), (half_of(w_gate), half_of(w_ga...  4.7 us
    ppermute x3, starting transfers between devices, per_device(): lax.ppermute(merged, 'rows', [(i, i ^ k) for i in range(rows)])  4.45 us
    pallas_call x1, Pallas kernels, per_device(): call(first_half_body, (products_of, products_of, half_of(w_down)), 'vvvvv...  4.28 us
    pallas_call x1, Pallas kernels, per_device(): call(own_chunk_body, (products_of, products_of, half_of(w_up)), 'vvva', '...  3.42 us
    pallas_call x1, Pallas kernels, per_device(): call(functools.partial(load_body, (0,)), half_of(w_up), 'va', 'load_up',...  2.9 us
  transfers between devices with their start and end apart: 9, of which 2 were waited for; matrix products, arithmetic and copies ran while one was open for 1% of the time, Pallas kernels for 31%

profile of v3, /device:TPU:0, one launch (start us, length us, event | category | flops | bytes accessed | tf_op | source)
XLA Modules:
  0.0 53.9 jit_solution(6449717982832494487)
XLA Ops:
  0.6 1.2 %pack.1 = (bf16[192,128]{1,0:T(8,128)(2,1)S(1)}, bf16[192,128]{1,0:T(8,128)(2,1)S(1)}, bf16[192,128]{1,0:T(8,128)(2,1)S(1)}, bf16[192,128]{1,0:T(8,128)(2,1)S(1)}) custom-call(s32[2]{0:T(128)} %prompt_hbm.1, bf16[2,2,3072]{2,1,0:T(2,128)(2,1)} %q_hbm.1, bf16[2,2,2,512]{3,2,1,0:T(2,128)(2,1)} %new_hbm.1, bf16[2,32,2,512]{3,2,1,0:T(2,128)(2,1)} %prefix_hbm.1, ...), custom_call_target="tpu_custom_call" | custom-call | tf_op jit(solution)/shard_map/pack/pallas_call | solution.py:432
  1.9 3.1 %collective-permute-start = (bf16[192,128]{1,0:T(8,128)(2,1)S(1)}, bf16[192,128]{1,0:T(8,128)(2,1)S(1)}, u32[]{:S(2)}, u32[]{:S(2)}) collective-permute-start(bf16[192,128]{1,0:T(8,128)(2,1)S(1)} %get-tuple-element.19), channel_id=1, source_target_pairs={{0,4},{4,0},{8,12},{12,8},{1,5},{5,1},{9,13},{13,9},{2,6},{6,2},{1... | collective-permute-start | bytes 147464 | tf_op jit(solution)/shard_map/ppermute | solution.py:442
  5.0 2.6 %collective-permute-start.1 = (bf16[192,128]{1,0:T(8,128)(2,1)S(1)}, bf16[192,128]{1,0:T(8,128)(2,1)S(1)}, u32[]{:S(2)}, u32[]{:S(2)}) collective-permute-start(bf16[192,128]{1,0:T(8,128)(2,1)S(1)} %get-tuple-element.20), channel_id=1, source_target_pairs={{0,8},{4,12},{8,0},{12,4},{1,9},{5,13},{9,1},{13,5},{2,10},{6,14},... | collective-permute-start | bytes 147464 | tf_op jit(solution)/shard_map/ppermute | solution.py:442
  7.6 0.0 collective-permute-start.2
  7.6 0.8 %dynamic_slice.3 = bf16[768]{0:T(1024)(128)(2,1)S(1)} dynamic-slice(bf16[6144]{0:T(1024)(128)(2,1)} %param.16, s32[]{:T(128)S(6)} %select_n.3), dynamic_slice_sizes={768} | dynamic-slice | bytes 3076 | tf_op jit(solution)/shard_map/dynamic_slice | solution.py:471
  8.3 4.7 %load_gate.1 = (bf16[3072,1024]{1,0:T(8,128)(2,1)S(1)}, bf16[3072,1024]{1,0:T(8,128)(2,1)S(1)}) custom-call(bf16[192,128]{1,0:T(8,128)(2,1)S(1)} %get-tuple-element.18._.refs_0_, bf16[1,6144,1024]{2,1,0:T(8,128)(2,1)} %source.2), custom_call_target="tpu_custom_call" | custom-call | flops 402653184 | bytes 12582912 | tf_op jit(solution)/shard_map/load_gate/pallas_call | solution.py:459
  13.1 0.0 collective-permute-done.refs_1_
  13.1 0.0 collective-permute-done.1.refs_2_
  13.1 0.4 collective-permute-done.2.refs_3_
  13.5 0.7 %attend.1 = (bf16[16,896]{1,0:T(8,128)(2,1)S(1)}, bf16[16,768]{1,0:T(8,128)(2,1)S(1)}) custom-call(bf16[192,128]{1,0:T(8,128)(2,1)S(1)} %get-tuple-element.18._.refs_0_, bf16[192,128]{1,0:T(8,128)(2,1)S(1)} %collective-permute-done.refs_1_, bf16[192,128]{1,0:T(8,128)(2,1)S(1)} %collective-permute-done.1.refs_2_, ...), custom_call_target="tpu_custom_call" | custom-call | tf_op jit(solution)/shard_map/attend/pallas_call | solution.py:473
  14.1 1.5 %collective-permute-start.3 = (bf16[16,896]{1,0:T(8,128)(2,1)S(1)}, bf16[16,896]{1,0:T(8,128)(2,1)S(1)}, u32[]{:S(2)}, u32[]{:S(2)}) collective-permute-start(bf16[16,896]{1,0:T(8,128)(2,1)S(1)} %get-tuple-element.23._.own_ref), channel_id=1, source_target_pairs={{0,2},{2,0},{1,3},{3,1},{4,6},{6,4},{5,7},{7,5},{8,10},{10,8},{9,1... | collective-permute-start | bytes 86024 | tf_op jit(solution)/shard_map/ppermute | solution.py:486
  15.6 2.9 %load_up.1._.up_w = bf16[3072,1024]{1,0:T(8,128)(2,1)S(1)} custom-call(bf16[16,896]{1,0:T(8,128)(2,1)S(1)} %get-tuple-element.23._.own_ref, bf16[1,6144,1024]{2,1,0:T(8,128)(2,1)} %up_hbm.1), custom_call_target="tpu_custom_call" | custom-call | flops 201326592 | bytes 6291456 | tf_op jit(solution)/shard_map/load_up/pallas_call | solution.py:488
  18.5 0.0 collective-permute-done.3.peer_ref
  18.6 3.5 %collective-permute-start.6 = (bf16[32,896]{1,0:T(8,128)(2,1)S(1)}, bf16[32,896]{1,0:T(8,128)(2,1)S(1)}, u32[]{:S(2)}, u32[]{:S(2)}) collective-permute-start(bf16[32,896]{1,0:T(8,128)(2,1)S(1)} %merge.1.x_ref.refs_0_), channel_id=1, source_target_pairs={{0,12},{4,8},{8,4},{12,0},{1,13},{5,9},{9,5},{13,1},{2,14},{6,10},... | collective-permute-start | bytes 172040 | tf_op jit(solution)/shard_map/ppermute | solution.py:502
  22.1 0.0 collective-permute-start.5
  22.1 0.9 %collective-permute-start.4 = (bf16[32,896]{1,0:T(8,128)(2,1)S(1)}, bf16[32,896]{1,0:T(8,128)(2,1)S(1)}, u32[]{:S(2)}, u32[]{:S(2)}) collective-permute-start(bf16[32,896]{1,0:T(8,128)(2,1)S(1)} %merge.1.x_ref.refs_0_), channel_id=1, source_target_pairs={{0,4},{4,0},{8,12},{12,8},{1,5},{5,1},{9,13},{13,9},{2,6},{6,2},{1... | collective-permute-start | bytes 172040 | tf_op jit(solution)/shard_map/ppermute | solution.py:502
  23.0 3.4 %own_chunk.1 = (f32[32,1024]{1,0:T(8,128)S(1)}, f32[32,1024]{1,0:T(8,128)S(1)}, bf16[3072,1024]{1,0:T(8,128)(2,1)S(1)}) custom-call(bf16[32,896]{1,0:T(8,128)(2,1)S(1)} %merge.1.x_ref.refs_0_, bf16[3072,1024]{1,0:T(8,128)(2,1)S(1)} %get-tuple-element.22.refs_5_.gate_w, bf16[3072,1024]{1,0:T(8,128)(2,1)S(1)} %load_up.1._.up_w, bf16[1,6144,1024]{2,1,0:T(8,128)(2,1)} %up_hbm.1), custom_call_target="tpu_custom_call" | custom-call | flops 201326592 | bytes 6291456 | tf_op jit(solution)/shard_map/own_chunk/pallas_call | solution.py:507
  26.4 0.0 collective-permute-done.6.refs_3_
  26.4 0.7 %collective-permute-done.5.refs_2_ = bf16[32,896]{1,0:T(8,128)(2,1)S(1)} collective-permute-done((bf16[32,896]{1,0:T(8,128)(2,1)S(1)}, bf16[32,896]{1,0:T(8,128)(2,1)S(1)}, u32[]{:S(2)}, u32[]{:S(2)}) %collective-permute-start.5) | collective-permute-done | bytes 57376 | tf_op jit(solution)/shard_map/ppermute | solution.py:502
  27.2 0.0 collective-permute-done.4.refs_1_
  27.2 0.1 collective-permute-start.7
  27.3 4.3 %first_half.1 = (f32[32,1024]{1,0:T(8,128)S(1)}, f32[32,1024]{1,0:T(8,128)S(1)}, bf16[1024,3072]{1,0:T(8,128)(2,1)S(1)}) custom-call(bf16[4,32,896]{2,1,0:T(8,128)(2,1)S(1)} %stack.1.x_ref.own_ref, f32[32,1024]{1,0:T(8,128)S(1)} %get-tuple-element.25.gate_in, f32[32,1024]{1,0:T(8,128)S(1)} %get-tuple-element.26.up_in, ...), custom_call_target="tpu_custom_call" | custom-call | flops 201326592 | bytes 6291456 | tf_op jit(solution)/shard_map/first_half/pallas_call | solution.py:522
  31.5 0.0 collective-permute-done.7.x_ref
  31.6 5.0 %second_half.1 = (bf16[32,1024]{1,0:T(8,128)(2,1)S(1)}, bf16[1024,3072]{1,0:T(8,128)(2,1)S(1)}) custom-call(bf16[4,32,896]{2,1,0:T(8,128)(2,1)S(1)} %collective-permute-done.7.x_ref, bf16[4,32,896]{2,1,0:T(8,128)(2,1)S(1)} %stack.1.x_ref.own_ref, f32[32,1024]{1,0:T(8,128)S(1)} %get-tuple-element.27.gate_in, f32[32,1024]{1,0:T(8,128)S(1)} %get-tuple-element.28.up_in, ...), custom_call_target="tpu_custom_call" | custom-call | flops 201326592 | bytes 6291456 | tf_op jit(solution)/shard_map/second_half/pallas_call | solution.py:530
  36.6 0.5 %collective-permute-start.8 = (bf16[32,1024]{1,0:T(8,128)(2,1)S(1)}, bf16[32,1024]{1,0:T(8,128)(2,1)S(1)}, u32[]{:S(2)}, u32[]{:S(2)}) collective-permute-start(bf16[32,1024]{1,0:T(8,128)(2,1)S(1)} %get-tuple-element.30.hidden_ref), channel_id=1, source_target_pairs={{0,1},{1,0},{2,3},{3,2},{4,5},{5,4},{6,7},{7,6},{8,9},{9,8},{10,11... | collective-permute-start | bytes 196616 | tf_op jit(solution)/shard_map/ppermute | solution.py:538
  37.2 1.2 %down_first.1.own_ref = f32[32,3072]{1,0:T(8,128)S(1)} custom-call(bf16[32,1024]{1,0:T(8,128)(2,1)S(1)} %get-tuple-element.30.hidden_ref, bf16[1024,3072]{1,0:T(8,128)(2,1)S(1)} %get-tuple-element.31.down_w), custom_call_target="tpu_custom_call" | custom-call | flops 201326592 | bytes 6291456 | tf_op jit(solution)/shard_map/down_first/pallas_call | solution.py:539
  38.3 0.0 collective-permute-done.8.hidden_ref
  38.3 1.2 %down_second.1 = bf16[8,4,3840]{2,1,0:T(4,128)(2,1)S(1)} custom-call(bf16[32,1024]{1,0:T(8,128)(2,1)S(1)} %collective-permute-done.8.hidden_ref, f32[32,3072]{1,0:T(8,128)S(1)} %down_first.1.own_ref, bf16[16,768]{1,0:T(8,128)(2,1)S(1)} %get-tuple-element.32.attn_ref, bf16[1024,3072]{1,0:T(8,128)(2,1)S(1)} %get-tuple-element.33.down_w), custom_call_target="tpu_custom_call" | custom-call | flops 201326592 | bytes 6291456 | tf_op jit(solution)/shard_map/down_second/pallas_call | solution.py:546
  39.6 13.1 %all_to_all.5.got_ref = bf16[8,4,3840]{2,1,0:T(4,128)(2,1)S(1)} all-to-all(bf16[8,4,3840]{2,1,0:T(4,128)(2,1)S(1)} %down_second.1), channel_id=1, replica_groups=mesh['groups'=2,'rows'=4,'experts'=2,'heads'=2] {'rows','experts'}, dimensions={0} | all-to-all | bytes 491520 | tf_op jit(solution)/shard_map/all_to_all | solution.py:553
  52.6 0.0 copy-done
  52.6 0.0 copy-done.1
  52.6 1.3 %mix.1 = (bf16[2,2,3072]{2,1,0:T(2,128)(2,1)}, bf16[2,2,3072]{2,1,0:T(2,128)(2,1)}) custom-call(s32[2,2,2]{2,1,0:T(2,128)S(1)} %copy-done, f32[2,2,2]{2,1,0:T(2,128)S(1)} %copy-done.1, bf16[8,4,3840]{2,1,0:T(4,128)(2,1)S(1)} %all_to_all.5.got_ref), custom_call_target="tpu_custom_call" | custom-call | tf_op jit(solution)/shard_map/mix/pallas_call | solution.py:555
  (5 shorter events, 0.0 us)
Async XLA Ops:
  1.9 11.2 %collective-permute-start = (bf16[192,128]{1,0:T(8,128)(2,1)S(1)}, bf16[192,128]{1,0:T(8,128)(2,1)S(1)}, u32[]{:S(2)}, u32[]{:S(2)}) collective-permute-start(bf16[192,128]{1,0:T(8,128)(2,1)S(1)} %get-tuple-element.19), channel_id=1, source_target_pairs={{0,4},{4,0},{8,12},{12,8},{1,5},{5,1},{9,13},{13,9},{2,6},{6,2},{1... | collective-permute-start | bytes 147464 | tf_op jit(solution)/shard_map/ppermute | solution.py:442
  5.0 8.1 %collective-permute-start.1 = (bf16[192,128]{1,0:T(8,128)(2,1)S(1)}, bf16[192,128]{1,0:T(8,128)(2,1)S(1)}, u32[]{:S(2)}, u32[]{:S(2)}) collective-permute-start(bf16[192,128]{1,0:T(8,128)(2,1)S(1)} %get-tuple-element.20), channel_id=1, source_target_pairs={{0,8},{4,12},{8,0},{12,4},{1,9},{5,13},{9,1},{13,5},{2,10},{6,14},... | collective-permute-start | bytes 147464 | tf_op jit(solution)/shard_map/ppermute | solution.py:442
  7.6 5.9 %collective-permute-start.2 = (bf16[192,128]{1,0:T(8,128)(2,1)S(1)}, bf16[192,128]{1,0:T(8,128)(2,1)S(1)}, u32[]{:S(2)}, u32[]{:S(2)}) collective-permute-start(bf16[192,128]{1,0:T(8,128)(2,1)S(1)} %get-tuple-element.21), channel_id=1, source_target_pairs={{0,12},{4,8},{8,4},{12,0},{1,13},{5,9},{9,5},{13,1},{2,14},{6,10},... | collective-permute-start | bytes 147464 | tf_op jit(solution)/shard_map/ppermute | solution.py:442
  14.1 4.4 %collective-permute-start.3 = (bf16[16,896]{1,0:T(8,128)(2,1)S(1)}, bf16[16,896]{1,0:T(8,128)(2,1)S(1)}, u32[]{:S(2)}, u32[]{:S(2)}) collective-permute-start(bf16[16,896]{1,0:T(8,128)(2,1)S(1)} %get-tuple-element.23._.own_ref), channel_id=1, source_target_pairs={{0,2},{2,0},{1,3},{3,1},{4,6},{6,4},{5,7},{7,5},{8,10},{10,8},{9,1... | collective-permute-start | bytes 86024 | tf_op jit(solution)/shard_map/ppermute | solution.py:486
  18.6 7.9 %collective-permute-start.6 = (bf16[32,896]{1,0:T(8,128)(2,1)S(1)}, bf16[32,896]{1,0:T(8,128)(2,1)S(1)}, u32[]{:S(2)}, u32[]{:S(2)}) collective-permute-start(bf16[32,896]{1,0:T(8,128)(2,1)S(1)} %merge.1.x_ref.refs_0_), channel_id=1, source_target_pairs={{0,12},{4,8},{8,4},{12,0},{1,13},{5,9},{9,5},{13,1},{2,14},{6,10},... | collective-permute-start | bytes 172040 | tf_op jit(solution)/shard_map/ppermute | solution.py:502
  22.1 5.1 %collective-permute-start.5 = (bf16[32,896]{1,0:T(8,128)(2,1)S(1)}, bf16[32,896]{1,0:T(8,128)(2,1)S(1)}, u32[]{:S(2)}, u32[]{:S(2)}) collective-permute-start(bf16[32,896]{1,0:T(8,128)(2,1)S(1)} %merge.1.x_ref.refs_0_), channel_id=1, source_target_pairs={{0,8},{4,12},{8,0},{12,4},{1,9},{5,13},{9,1},{13,5},{2,10},{6,14},... | collective-permute-start | bytes 172040 | tf_op jit(solution)/shard_map/ppermute | solution.py:502
  22.1 5.1 %collective-permute-start.4 = (bf16[32,896]{1,0:T(8,128)(2,1)S(1)}, bf16[32,896]{1,0:T(8,128)(2,1)S(1)}, u32[]{:S(2)}, u32[]{:S(2)}) collective-permute-start(bf16[32,896]{1,0:T(8,128)(2,1)S(1)} %merge.1.x_ref.refs_0_), channel_id=1, source_target_pairs={{0,4},{4,0},{8,12},{12,8},{1,5},{5,1},{9,13},{13,9},{2,6},{6,2},{1... | collective-permute-start | bytes 172040 | tf_op jit(solution)/shard_map/ppermute | solution.py:502
  27.2 4.4 %collective-permute-start.7 = (bf16[4,32,896]{2,1,0:T(8,128)(2,1)S(1)}, bf16[4,32,896]{2,1,0:T(8,128)(2,1)S(1)}, u32[]{:S(2)}, u32[]{:S(2)}) collective-permute-start(bf16[4,32,896]{2,1,0:T(8,128)(2,1)S(1)} %stack.1.x_ref.own_ref), channel_id=1, source_target_pairs={{0,1},{1,0},{2,3},{3,2},{4,5},{5,4},{6,7},{7,6},{8,9},{9,8},{10,11... | collective-permute-start | bytes 688136 | tf_op jit(solution)/shard_map/ppermute | solution.py:521
  36.6 1.7 %collective-permute-start.8 = (bf16[32,1024]{1,0:T(8,128)(2,1)S(1)}, bf16[32,1024]{1,0:T(8,128)(2,1)S(1)}, u32[]{:S(2)}, u32[]{:S(2)}) collective-permute-start(bf16[32,1024]{1,0:T(8,128)(2,1)S(1)} %get-tuple-element.30.hidden_ref), channel_id=1, source_target_pairs={{0,1},{1,0},{2,3},{3,2},{4,5},{5,4},{6,7},{7,6},{8,9},{9,8},{10,11... | collective-permute-start | bytes 196616 | tf_op jit(solution)/shard_map/ppermute | solution.py:538
  37.2 15.5 %copy-start = (s32[2,2,2]{2,1,0:T(2,128)S(1)}, s32[2,2,2]{2,1,0:T(2,128)}, u32[]{:S(2)}) copy-start(s32[2,2,2]{2,1,0:T(2,128)} %routes_ref.1) | copy-start | bytes 100
  37.2 15.5 %copy-start.1 = (f32[2,2,2]{2,1,0:T(2,128)S(1)}, f32[2,2,2]{2,1,0:T(2,128)}, u32[]{:S(2)}) copy-start(f32[2,2,2]{2,1,0:T(2,128)} %gates_ref.1) | copy-start | bytes 100

commit v4 on v2

--- a/solution.py
+++ b/solution.py
@@ -14,6 +14,16 @@
 
 VMEM = pltpu.VMEM
 MIB = 1 << 20
+PACK_COVER = 40 * MIB
+FLOPS = 1000
+OWN_COVER = 40 * MIB
+FIRST_COVER = 8 * MIB
+SECOND_COVER = 8 * MIB
+FIRST_LIMIT = 4 * MIB
+SECOND_LIMIT = 24 * MIB
+DOWN_LIMIT = 40 * MIB
+ATTEND_COVER = MIB
+MERGE_COVER = MIB
 
 
 def fresh_terms(queries, new_kv):
@@ -157,24 +167,28 @@
         self.rows = -(-(self.prompt + self.tokens) // 16) * 16
 
 
-def pack_body(plan, prompt_hbm, q_hbm, new_hbm, prefix_hbm, resid_hbm, *rest):
-    outs, buffers, sems = rest[: plan.kv_local], rest[plan.kv_local : -1], rest[-1]
-    sources = (prompt_hbm, q_hbm, new_hbm, prefix_hbm, resid_hbm)
-    copies = []
-    for i, (source, buffer) in enumerate(zip(sources, buffers)):
-        copy = pltpu.make_async_copy(source, buffer, sems.at[i])
+def fetch_body(plan, *refs):
+    count = (len(refs) - 2) // 2
+    sources, targets, (prompts, sems) = refs[:count], refs[count : 2 * count], refs[2 * count :]
+    copies = [
+        pltpu.make_async_copy(source, target, sems.at[i])
+        for i, (source, target) in enumerate(zip(sources, (prompts,) + targets[1:]))
+    ]
+    for copy in copies:
         copy.start()
-        copies.append(copy)
     for copy in copies:
         copy.wait()
-    prompt_ref, q_ref, new_ref, prefix_ref, resid_ref = buffers
-    t, c = plan.tokens, plan.conts
+    c = plan.conts
     base = lax.axis_index("experts") * plan.prompts
     row = lax.broadcasted_iota(jnp.int32, (c, HEAD_DIM), 0)
     local = jnp.zeros((c, HEAD_DIM), jnp.float32)
     for i in range(c):
-        local = jnp.where(row == i, (prompt_ref[i] - base).astype(jnp.float32), local)
-    local = local.astype(jnp.bfloat16)
+        local = jnp.where(row == i, (prompts[i] - base).astype(jnp.float32), local)
+    targets[0][...] = local.astype(jnp.bfloat16)
+
+
+def pack_body(plan, local_ref, q_ref, new_ref, prefix_ref, resid_ref, *outs):
+    t, c = plan.tokens, plan.conts
     own = lax.axis_index("rows")
     for k, out_ref in enumerate(outs):
         h = own ^ k
@@ -189,11 +203,11 @@
                 head = pl.ds(pl.multiple_of((h * GROUP + g) * HEAD_DIM, HEAD_DIM), HEAD_DIM)
                 out_ref[pl.ds(plan.query + g * t + s * c, c), :] = q_ref[s, :, head]
                 out_ref[pl.ds(plan.resid + g * t + s * c, c), :] = resid_ref[s, :, head]
-            out_ref[pl.ds(plan.prompt + s * c, c), :] = local
+            out_ref[pl.ds(plan.prompt + s * c, c), :] = local_ref[...]
 
 
 def attend_body(plan, rows, *refs):
-    pieces, (gain_ref, _, x_ref, attn_ref, q_s, r_s, kv_s, p_s) = refs[:rows], refs[rows:]
+    pieces, (gain_ref, x_ref, attn_ref, q_s, r_s, kv_s, p_s, gain_s) = refs[:rows], refs[rows:]
     t, c = plan.tokens, plan.conts
     total = rows * t
     f32 = jnp.float32
@@ -237,129 +251,161 @@
     weights = pltpu.roll(expo, 1, 1).astype(jnp.bfloat16)
     out = jnp.dot(weights, kv, preferred_element_type=f32) / totals
     attn = out.astype(jnp.bfloat16)
+    attn_ref[...] = attn
+    gain_s[...] = gain_ref[...].astype(f32)
+    first = (lax.axis_index("heads") * rows + lax.axis_index("rows")) * GROUP
     combined = attn.astype(f32) + r_s[...].astype(f32)
     square = jnp.zeros((total, HEAD_DIM), f32)
-    pieces = x_ref.shape[0]
     for g in range(GROUP):
         part = combined[g * total : (g + 1) * total]
         square = square + part * part
-        lanes = pl.ds(g * HEAD_DIM, HEAD_DIM)
-        gained = (part * gain_ref[:, lanes].astype(f32)).astype(jnp.bfloat16)
-        for piece in range(pieces):
-            x_ref[piece, :, lanes] = gained
-        attn_ref[:, lanes] = attn[g * total : (g + 1) * total]
+        gained = part * gain_s[pl.ds(first + g, 1), :]
+        x_ref[:, pl.ds(g * HEAD_DIM, HEAD_DIM)] = gained.astype(jnp.bfloat16)
     square = jnp.sum(square, axis=-1, keepdims=True)
     high = square.astype(jnp.bfloat16)
     low = (square - high.astype(f32)).astype(jnp.bfloat16)
     lane = lax.broadcasted_iota(jnp.int32, (total, HEAD_DIM), 1)
     extra = jnp.where(lane == 0, high.astype(f32), jnp.where(lane == 1, low.astype(f32), 0.0))
-    extra = extra.astype(jnp.bfloat16)
-    for piece in range(pieces):
-        x_ref[piece, :, pl.ds(GROUP * HEAD_DIM, HEAD_DIM)] = extra
-
-
-def stream(source, target, sems):
+    x_ref[:, pl.ds(GROUP * HEAD_DIM, HEAD_DIM)] = extra.astype(jnp.bfloat16)
+
+
+def to_row(column, first, lanes):
+    shape = (column.shape[0], lanes)
+    hit = lax.broadcasted_iota(jnp.int32, shape, 1) == lax.broadcasted_iota(jnp.int32, shape, 0) + first
+    return jnp.sum(jnp.where(hit, column, 0.0), axis=0, keepdims=True)
+
+
+def to_column(row, count):
+    shape = (count, row.shape[1])
+    hit = lax.broadcasted_iota(jnp.int32, shape, 1) == lax.broadcasted_iota(jnp.int32, shape, 0)
+    return jnp.sum(jnp.where(hit, row, 0.0), axis=1, keepdims=True)
+
+
+def merge_body(plan, rows, own_ref, peer_ref, attn_ref, *outs):
+    t = plan.tokens
+    total, width = own_ref.shape
+    depth = width - HEAD_DIM
+    spare = pl.ds(depth, HEAD_DIM)
+    high, low = [], []
+    for i, ref in enumerate((own_ref, peer_ref)):
+        extra = ref[:, spare].astype(jnp.float32)
+        high.append(to_row(extra[:, 0:1], i * total, HEAD_DIM))
+        low.append(to_row(extra[:, 1:2], i * total, HEAD_DIM))
+    row = lax.broadcasted_iota(jnp.int32, (2 * total - GROUP * t, HEAD_DIM), 0)
+    squares = jnp.where(row == 0, high[0] + high[1], jnp.where(row == 1, low[0] + low[1], 0.0))
+    squares = squares.astype(jnp.bfloat16)
+    for out_ref in outs:
+        for i, ref in enumerate((own_ref, peer_ref)):
+            out_ref[pl.ds(i * total, total), pl.ds(0, depth)] = ref[:, pl.ds(0, depth)]
+        out_ref[pl.ds(GROUP * t, row.shape[0]), spare] = squares
+
+    def place(own):
+        for k, out_ref in enumerate(outs):
+            for g in range(GROUP):
+                part = attn_ref[pl.ds(g * total + (own ^ k) * t, t), :]
+                out_ref[pl.ds(g * t, t), spare] = part
+
+    for own in range(rows):
+        pl.when(lax.axis_index("rows") == own)(functools.partial(place, own))
+
+
+def stack_body(*refs):
+    *pieces, _, out_ref = refs
+    for k, ref in enumerate(pieces):
+        out_ref[k] = ref[...]
+
+
+def products(side, x, weight, k, total):
+    depth = x.shape[1]
     core = lax.axis_index("heads")
-    half = source.shape[1] // 2
-    parts = sems.shape[1]
-    step = half // parts
-    copies = []
-    for side in range(2):
-        first = (core if side == 0 else 1 - core) * half
-        copies.append(
-            [
-                pltpu.make_async_copy(
-                    source.at[0, pl.ds(first + k * step, step)],
-                    target.at[side, pl.ds(k * step, step)],
-                    sems.at[side, k],
-                )
-                for k in range(parts)
-            ]
-        )
-    for copy in copies[0] + copies[1]:
-        copy.start()
-    return copies
-
-
-def load_body(_, source, target, sems):
-    copies = stream(source, target, sems)
-    for copy in copies[0] + copies[1]:
-        copy.wait()
-
-
-def half_products(side, x_ref, weight, total, ready=None):
+    core = 1 - core if side else core
+    half = weight.shape[1] // 2
+    first = pl.multiple_of(core * half + (lax.axis_index("rows") ^ k) * depth, depth)
+    part = jnp.dot(x, weight[0, pl.ds(first, depth)], preferred_element_type=jnp.float32)
+    return part if total is None else total + part
+
+
+def own_chunk_body(x_ref, gate_w, up_w, gate_ref, up_ref):
+    x = x_ref[:, pl.ds(0, x_ref.shape[1] - HEAD_DIM)]
+    gate_ref[...] = products(0, x, gate_w, 0, None)
+    up_ref[...] = products(0, x, up_w, 0, None)
+
+
+def first_half_body(x_ref, gate_in, up_in, gate_w, up_w, gate_ref, up_ref):
     chunks, _, width = x_ref.shape
+    gate, up = gate_in[...], up_in[...]
+    for k in range(1, chunks):
+        x = x_ref[k, :, pl.ds(0, width - HEAD_DIM)]
+        gate = products(0, x, gate_w, k, gate)
+        up = products(0, x, up_w, k, up)
+    gate_ref[...] = gate
+    up_ref[...] = up
+
+
+def second_half_body(plan, x_ref, own_ref, gate_in, up_in, gate_w, up_w, hidden_ref):
+    chunks, tokens, width = x_ref.shape
     depth = width - HEAD_DIM
-    for k in range(chunks):
-        if ready is not None:
-            ready[k].wait()
-        part = jnp.dot(
-            x_ref[k, :, pl.ds(0, depth)],
-            weight[side, pl.ds(k * depth, depth)],
-            preferred_element_type=jnp.float32,
-        )
-        total = part if total is None else total + part
-    return total
-
-
-def first_half_body(x_ref, gate_w, up_hbm, gate_ref, up_ref, up_w, sems):
-    copies = stream(up_hbm, up_w, sems)
-    gate_ref[...] = half_products(0, x_ref, gate_w, None)
-    up_ref[...] = half_products(0, x_ref, up_w, None, copies[0])
-    for copy in copies[1]:
-        copy.wait()
-
-
-def second_half_body(
-    x_ref, own_ref, gate_in, up_in, gate_w, up_w, down_hbm, hidden_ref, down_w, sems
-):
-    copies = stream(down_hbm, down_w, sems)
-    chunks, _, width = x_ref.shape
-    depth = width - HEAD_DIM
-    square = jnp.zeros((x_ref.shape[1], 1), jnp.float32)
+    first = GROUP * plan.tokens
+    square = jnp.zeros((tokens - first, HEAD_DIM), jnp.float32)
     for ref in (own_ref, x_ref):
         for k in range(chunks):
-            extra = ref[k, :, pl.ds(depth, HEAD_DIM)].astype(jnp.float32)
-            square = square + jnp.sum(extra, axis=-1, keepdims=True)
+            extra = ref[k, pl.ds(first, tokens - first), pl.ds(depth, HEAD_DIM)]
+            square = square + extra.astype(jnp.float32)
+    square = to_column(square[0:1] + square[1:2], tokens)
     scale = lax.rsqrt(square / (2 * chunks * depth) + 1e-05)
-    gate = half_products(1, x_ref, gate_w, gate_in[...]) * scale
-    up = half_products(1, x_ref, up_w, up_in[...]) * scale
+    gate, up = gate_in[...], up_in[...]
+    for k in range(chunks):
+        x = x_ref[k, :, pl.ds(0, depth)]
+        gate = products(1, x, gate_w, k, gate)
+        up = products(1, x, up_w, k, up)
+    gate = gate * scale
+    up = up * scale
     hidden_ref[...] = (gate / (1.0 + jnp.exp(-gate)) * up).astype(jnp.bfloat16)
-    for copy in copies[0] + copies[1]:
-        copy.wait()
+
+
+def down_product(side, hidden_ref, down_w):
+    depth = hidden_ref.shape[1]
+    core = lax.axis_index("heads")
+    first = pl.multiple_of((1 - core if side else core) * depth, depth)
+    return jnp.dot(
+        hidden_ref[...], down_w[0, pl.ds(first, depth)], preferred_element_type=jnp.float32
+    )
 
 
 def down_first_body(hidden_ref, down_w, out_ref):
-    out_ref[...] = jnp.dot(hidden_ref[...], down_w[0], preferred_element_type=jnp.float32)
-
-
-def down_second_body(rows, hidden_ref, own_ref, attn_ref, down_w, out_ref):
-    total = own_ref[...] + jnp.dot(
-        hidden_ref[...], down_w[1], preferred_element_type=jnp.float32
-    )
-    result = total.astype(jnp.bfloat16)
-    pieces, t, width = out_ref.shape
+    out_ref[...] = down_product(0, hidden_ref, down_w)
+
+
+def down_second_body(rows, hidden_ref, own_ref, down_w, out_ref):
+    result = (own_ref[...] + down_product(1, hidden_ref, down_w)).astype(jnp.bfloat16)
+    pieces, t, _ = out_ref.shape
     experts = pieces // rows
-    half = result.shape[1]
+    own = lax.axis_index("experts")
     for r in range(rows):
-        attn = attn_ref[pl.ds(r * t, t), :]
         for e in range(experts):
             first = (e * rows + r) * t
-            out_ref[r * experts + e, :, pl.ds(0, half)] = result[first : first + t]
-            out_ref[r * experts + e, :, pl.ds(half, width - half)] = attn
-
-
-def mix_body(rows, routes_ref, gates_ref, got_ref, attn_ref, moe_ref):
-    pieces, t, width = got_ref.shape
+            out_ref[r * experts + (own ^ e)] = result[first : first + t]
+
+
+def mix_body(rows, routes_ref, gates_ref, got_ref, own_ref, attn_ref, moe_ref):
+    pieces, t, half = got_ref.shape
     experts = pieces // rows
-    steps, conts, half = moe_ref.shape
-    own = lax.axis_index("experts")
+    steps, conts, _ = moe_ref.shape
+    depth = own_ref.shape[2] - HEAD_DIM
+    for k in range(rows):
+        head = (lax.axis_index("rows") ^ k) * GROUP
+        for g in range(GROUP):
+            lanes = pl.ds(pl.multiple_of((head + g) * HEAD_DIM, HEAD_DIM), HEAD_DIM)
+            for s in range(steps):
+                attn_ref[s, :, lanes] = own_ref[
+                    k, pl.ds(g * t + s * conts, conts), pl.ds(depth, HEAD_DIM)
+                ]
     row = lax.broadcasted_iota(jnp.int32, (t, 1), 0)
     mixture = jnp.zeros((t, half), jnp.float32)
     for e in range(experts):
         summed = jnp.zeros((t, half), jnp.float32)
         for r in range(rows):
-            summed = summed + got_ref[r * experts + e, :, pl.ds(0, half)].astype(jnp.float32)
+            summed = summed + got_ref[r * experts + e].astype(jnp.float32)
         share = jnp.zeros((t, 1), jnp.float32)
         for s in range(steps):
             for c in range(conts):
@@ -369,13 +415,8 @@
                 share = jnp.where(row == s * conts + c, amount, share)
         mixture = mixture + share * summed.astype(jnp.bfloat16).astype(jnp.float32)
     mixture = mixture.astype(jnp.bfloat16)
-    piece = width - half
     for s in range(steps):
         moe_ref[s] = mixture[s * conts : (s + 1) * conts]
-        for r in range(rows):
-            attn_ref[s, :, pl.ds(r * piece, piece)] = got_ref[
-                r * experts + own, pl.ds(s * conts, conts), pl.ds(half, piece)
-            ]
 
 
 def per_device(
@@ -401,88 +442,112 @@
 
     hbm = functools.partial(pltpu.with_memory_space_constraint, memory_space=pltpu.HBM)
     vmem = functools.partial(pltpu.with_memory_space_constraint, memory_space=VMEM)
+    gate_w, up_w, down_w = w_gate, w_up, w_down
+
+    def cover(size):
+        return pl.CostEstimate(flops=FLOPS * size, bytes_accessed=size, transcendentals=0)
+
     sources = (cont_prompt, queries, new_kv, prefix_kv, resid)
+    fetched = call(
+        functools.partial(fetch_body, plan),
+        (VMEM((plan.conts, HEAD_DIM), bf16),)
+        + tuple(VMEM(source.shape, bf16) for source in sources[1:]),
+        "aaaaa",
+        "fetch",
+        scratch=(
+            pltpu.SMEM(cont_prompt.shape, jnp.int32),
+            pltpu.SemaphoreType.DMA((len(sources),)),
+        ),
+    )(*map(hbm, sources))
     packed = call(
         functools.partial(pack_body, plan),
         (shape((plan.rows, HEAD_DIM), bf16),) * rows,
-        "aaaaa",
+        "vvvvv",
         "pack",
-        scratch=(pltpu.SMEM(cont_prompt.shape, jnp.int32),)
-        + tuple(VMEM(source.shape, bf16) for source in sources[1:])
-        + (pltpu.SemaphoreType.DMA((len(sources),)),),
-    )(*map(hbm, sources))
-    got = [
-        lax.ppermute(packed[k], "rows", [(i, i ^ k) for i in range(rows)]) if k else packed[0]
-        for k in range(rows)
-    ]
-
-    def resident(weight):
-        return VMEM((2, weight.shape[1] // 2, weight.shape[2]), bf16)
-
-    def reading(weight):
-        return pl.CostEstimate(flops=0, bytes_accessed=2 * weight.size, transcendentals=0)
-
-    sems = pltpu.SemaphoreType.DMA((2, rows))
-    gate_w = call(
-        load_body, resident(w_gate), "va", "load_gate", (sems,), MIB, reading(w_gate)
-    )(packed[0], hbm(w_gate))
-
-    start = lax.axis_index("heads") * plan.half + lax.axis_index("rows") * piece
-    gain = lax.dynamic_slice_in_dim(norm_gain, start, piece).reshape(1, piece)
+        cost=cover(PACK_COVER),
+    )(*map(vmem, fetched))
+
+    def spread(pieces):
+        return [
+            lax.ppermute(pieces[k], "rows", [(i, i ^ k) for i in range(rows)]) if k else pieces[0]
+            for k in range(rows)
+        ]
+
     keys = -(-(rows * (plan.block + 2 * plan.tokens)) // 128) * 128
+    lanes = piece + HEAD_DIM
     x, attn = call(
         functools.partial(attend_body, plan, rows),
-        (shape((rows * experts, total, piece + HEAD_DIM), bf16), shape((total, piece), bf16)),
-        "v" * (rows + 2),
+        (shape((total, lanes), bf16), shape((GROUP * total, HEAD_DIM), bf16)),
+        "v" * (rows + 1),
         "attend",
         scratch=(
             VMEM((GROUP * total, HEAD_DIM), bf16),
             VMEM((GROUP * total, HEAD_DIM), bf16),
             VMEM((keys, HEAD_DIM), bf16),
             VMEM((total, HEAD_DIM), bf16),
+            VMEM((norm_gain.size // HEAD_DIM, HEAD_DIM), f32),
         ),
-    )(*got, gain, vmem(gate_w))
-    x = lax.all_to_all(x, ("rows", "experts"), split_axis=0, concat_axis=0, tiled=True)
-    own = x.reshape(rows, tokens, piece + HEAD_DIM)
+        cost=cover(ATTEND_COVER),
+    )(*spread(packed), norm_gain.reshape(-1, HEAD_DIM))
     swap = [(0, 1), (1, 0)]
+    peer = lax.ppermute(x, "experts", swap)
+    merged = call(
+        functools.partial(merge_body, plan, rows),
+        (shape((tokens, lanes), bf16),) * rows,
+        "vvv",
+        "merge",
+        cost=cover(MERGE_COVER),
+    )(x, peer, attn)
+    chunks = spread(merged)
+    units = w_gate.shape[2]
+    products_of = shape((tokens, units), f32)
+    gate, up = call(
+        own_chunk_body,
+        (products_of, products_of),
+        "vvv",
+        "own_chunk",
+        cost=cover(OWN_COVER),
+    )(merged[0], gate_w, up_w)
+    own = call(stack_body, shape((rows, tokens, lanes), bf16), "v" * (rows + 1), "stack")(
+        *chunks, gate
+    )
     other = lax.ppermute(own, "heads", swap)
-
-    units = w_gate.shape[2]
-    gate, up, up_w = call(
+    gate, up = call(
         first_half_body,
-        (shape((tokens, units), f32), shape((tokens, units), f32), resident(w_up)),
-        "vva",
+        (products_of, products_of),
+        "vvvvv",
         "first_half",
-        (sems,),
-        cost=reading(w_up),
-    )(own, vmem(gate_w), hbm(w_up))
-    hidden, down_w = call(
-        second_half_body,
-        (shape((tokens, units), bf16), resident(w_down)),
-        "vvvvvva",
+        limit=FIRST_LIMIT,
+        cost=cover(FIRST_COVER),
+    )(own, gate, up, gate_w, up_w)
+    hidden = call(
+        functools.partial(second_half_body, plan),
+        shape((tokens, units), bf16),
+        "vvvvvv",
         "second_half",
-        (sems,),
-        cost=reading(w_down),
-    )(other, own, gate, up, vmem(gate_w), vmem(up_w), hbm(w_down))
+        limit=SECOND_LIMIT,
+        cost=cover(SECOND_COVER),
+    )(other, own, gate, up, gate_w, up_w)
     other_hidden = lax.ppermute(hidden, "heads", swap)
     partial = call(
         down_first_body,
         shape((tokens, plan.half), f32),
         "vv",
         "down_first",
-        cost=reading(w_down),
-    )(hidden, vmem(down_w))
+        limit=DOWN_LIMIT,
+        cost=cover(2 * plan.half * units),
+    )(hidden, down_w)
     blocks = call(
         functools.partial(down_second_body, rows),
-        shape((rows * experts, plan.tokens, plan.half + piece), bf16),
-        "vvvv",
+        shape((rows * experts, plan.tokens, plan.half), bf16),
+        "vvv",
         "down_second",
-        cost=reading(w_down),
-    )(other_hidden, partial, attn, vmem(down_w))
+        cost=cover(2 * plan.half * units),
+    )(other_hidden, partial, down_w)
     blocks = lax.all_to_all(blocks, ("rows", "experts"), split_axis=0, concat_axis=0, tiled=True)
     out = shape(queries.shape, bf16)
-    attn_out, moe_out = call(functools.partial(mix_body, rows), (out, out), "ssv", "mix")(
-        routes, route_gates, blocks
+    attn_out, moe_out = call(functools.partial(mix_body, rows), (out, out), "ssvv", "mix")(
+        routes, route_gates, blocks, own
     )
     return (attn_out, moe_out)
 
@@ -502,7 +567,12 @@
         P(None, ("groups", "rows", "experts"), None),
     )
     sizes = mesh.shape
-    by_head = sizes["heads"] == 2 and sizes["rows"] * sizes["heads"] == KV_HEADS
+    by_head = (
+        sizes["heads"] == 2
+        and sizes["experts"] == 2
+        and sizes["rows"] == 4
+        and sizes["rows"] * sizes["heads"] == KV_HEADS
+    )
     return jax.shard_map(
         per_device if by_head else per_device_wide,
         mesh=mesh,

time: 55.6 us -> 61.1 us (1.099)
  local copies, waits for them, and re-layouts: 0.78 us -> 13.7 us
  blocking collectives: 25.2 us -> 13.2 us
  Pallas kernels: 22 us -> 10.3 us
  waiting for transfers between devices: 0.4 us -> 10.5 us
  starting transfers between devices: 6.28 us -> 12.3 us
    unnamed x4 -> x16, local copies, waits for them, and re-layouts: 0.01 us -> 13.7 us
    all_to_all x1 -> x0, blocking collectives: 13.5 us -> none  [per_device(): lax.all_to_all(x, ('rows', 'experts'), split_axis=0, concat_axis=0, tiled...]
    pallas_call x5 -> x8, Pallas kernels: 18.4 us -> 7.66 us  [the longest x1 2.25 us: per_device(): call(functools.partial(second_half_body, plan), shape((tokens, units), bf...]
    ppermute x3 -> x7, waiting for transfers between devices: 0.39 us -> 10.5 us  [the longest x6 8.11 us: spread(): lax.ppermute(pieces[k], 'rows', [(i, i ^ k) for i in range(rows)])]
    ppermute x3 -> x7, starting transfers between devices: 5.71 us -> 11.6 us  [the longest x6 10.2 us: spread(): lax.ppermute(pieces[k], 'rows', [(i, i ^ k) for i in range(rows)])]
    all_to_all x1, blocking collectives: 11.7 us -> 13.2 us  [per_device(): lax.all_to_all(blocks, ('rows', 'experts'), split_axis=0, concat_axis=0,...]
    pallas_call x1, Pallas kernels: 1.23 us -> 0.26 us  [per_device(): call(functools.partial(pack_body, plan), (shape((plan.rows, HEAD_DIM), bf...]
    dynamic_slice x1 -> x0, local copies, waits for them, and re-layouts: 0.76 us -> none  [per_device(): gain = lax.dynamic_slice_in_dim(norm_gain, start, piece).reshape(1, piece)]
  transfers between devices with their start and end apart: 5 -> 9, of which waited for: 1 -> 5; matrix products, arithmetic and copies ran while one was open for 1% -> 0% of each run, Pallas kernels for 20% -> 6%
where the time goes in v4:
time: 61.1 us; the launch traced here: 60.8 us
  local copies, waits for them, and re-layouts  13.7 us (22%)
  blocking collectives  13.2 us (22%)
  starting transfers between devices  12.3 us (20%)
  waiting for transfers between devices  10.5 us (17%)
  Pallas kernels  10.3 us (17%)
  between operations  0.76 us (1%)
    unnamed x16, local copies, waits for them, and re-layouts  13.7 us
    all_to_all x1, blocking collectives, per_device(): lax.all_to_all(blocks, ('rows', 'experts'), split_axis=0, concat_axis=0,...  13.2 us
    ppermute x6, starting transfers between devices, spread(): lax.ppermute(pieces[k], 'rows', [(i, i ^ k) for i in range(rows)])  10.2 us
    ppermute x6, waiting for transfers between devices, spread(): lax.ppermute(pieces[k], 'rows', [(i, i ^ k) for i in range(rows)])  8.11 us
    ppermute x1, waiting for transfers between devices, per_device(): peer = lax.ppermute(x, 'experts', swap)  2.38 us
    pallas_call x1, Pallas kernels, per_device(): call(functools.partial(second_half_body, plan), shape((tokens, units), bf...  2.25 us
    pallas_call x1, Pallas kernels, per_device(): call(first_half_body, (products_of, products_of), 'vvvvv', 'first_half',...  1.72 us
    ppermute x1, starting transfers between devices, per_device(): peer = lax.ppermute(x, 'experts', swap)  1.5 us
  transfers between devices with their start and end apart: 9, of which 5 were waited for; matrix products, arithmetic and copies ran while one was open for 0% of the time, Pallas kernels for 6%

profile of v4, /device:TPU:0, one launch (start us, length us, event | category | flops | bytes accessed | tf_op | source)
XLA Modules:
  0.0 60.8 jit_solution(17826157959378153223)
XLA Ops:
  0.6 1.0 %fetch.1 = (bf16[2,128]{1,0:T(2,128)(2,1)S(1)}, bf16[2,2,3072]{2,1,0:T(2,128)(2,1)S(1)}, bf16[2,2,2,512]{3,2,1,0:T(2,128)(2,1)S(1)}, bf16[2,32,2,512]{3,2,1,0:T(2,128)(2,1)S(1)}, bf16[2,2,3072]{2,1,0:T(2,128)(2,1)S(1)}) custom-call(s32[2]{0:T(128)} %refs_0_.1, bf16[2,2,3072]{2,1,0:T(2,128)(2,1)} %refs_1_.1, bf16[2,2,2,512]{3,2,1,0:T(2,128)(2,1)} %refs_2_.1, ...), custom_call_target="tpu_custom_call" | custom-call | tf_op jit(solution)/shard_map/fetch/pallas_call | solution.py:451
  1.6 0.0 copy-start.7
  1.6 0.0 copy-start.2
  1.7 0.0 copy-start.4
  1.7 0.3 pack.1
  1.9 3.1 %collective-permute-start = (bf16[192,128]{1,0:T(8,128)(2,1)S(1)}, bf16[192,128]{1,0:T(8,128)(2,1)S(1)}, u32[]{:S(2)}, u32[]{:S(2)}) collective-permute-start(bf16[192,128]{1,0:T(8,128)(2,1)S(1)} %get-tuple-element.27), channel_id=1, source_target_pairs={{0,4},{4,0},{8,12},{12,8},{1,5},{5,1},{9,13},{13,9},{2,6},{6,2},{1... | collective-permute-start | bytes 147464 | tf_op jit(solution)/shard_map/ppermute | solution.py:472
  5.0 2.6 %collective-permute-start.1 = (bf16[192,128]{1,0:T(8,128)(2,1)S(1)}, bf16[192,128]{1,0:T(8,128)(2,1)S(1)}, u32[]{:S(2)}, u32[]{:S(2)}) collective-permute-start(bf16[192,128]{1,0:T(8,128)(2,1)S(1)} %get-tuple-element.28), channel_id=1, source_target_pairs={{0,8},{4,12},{8,0},{12,4},{1,9},{5,13},{9,1},{13,5},{2,10},{6,14},... | collective-permute-start | bytes 147464 | tf_op jit(solution)/shard_map/ppermute | solution.py:472
  7.6 3.3 %collective-permute-done.1.refs_2_ = bf16[192,128]{1,0:T(8,128)(2,1)S(1)} collective-permute-done((bf16[192,128]{1,0:T(8,128)(2,1)S(1)}, bf16[192,128]{1,0:T(8,128)(2,1)S(1)}, u32[]{:S(2)}, u32[]{:S(2)}) %collective-permute-start.1) | collective-permute-done | bytes 49184 | tf_op jit(solution)/shard_map/ppermute | solution.py:472
  11.0 2.6 %collective-permute-done.2.refs_3_ = bf16[192,128]{1,0:T(8,128)(2,1)S(1)} collective-permute-done((bf16[192,128]{1,0:T(8,128)(2,1)S(1)}, bf16[192,128]{1,0:T(8,128)(2,1)S(1)}, u32[]{:S(2)}, u32[]{:S(2)}) %collective-permute-start.2) | collective-permute-done | bytes 49184 | tf_op jit(solution)/shard_map/ppermute | solution.py:472
  13.5 0.7 %attend.1 = (bf16[16,896]{1,0:T(8,128)(2,1)S(1)}, bf16[96,128]{1,0:T(8,128)(2,1)S(1)}) custom-call(bf16[192,128]{1,0:T(8,128)(2,1)S(1)} %get-tuple-element.26.refs_0_, bf16[192,128]{1,0:T(8,128)(2,1)S(1)} %collective-permute-done.refs_1_, bf16[192,128]{1,0:T(8,128)(2,1)S(1)} %collective-permute-done.1.refs_2_, ...), custom_call_target="tpu_custom_call" | custom-call | flops 1048576000 | bytes 1048576 | tf_op jit(solution)/shard_map/attend/pallas_call | solution.py:478
  14.2 1.5 %collective-permute-start.3 = (bf16[16,896]{1,0:T(8,128)(2,1)S(1)}, bf16[16,896]{1,0:T(8,128)(2,1)S(1)}, u32[]{:S(2)}, u32[]{:S(2)}) collective-permute-start(bf16[16,896]{1,0:T(8,128)(2,1)S(1)} %get-tuple-element.30.own_ref), channel_id=1, source_target_pairs={{0,2},{2,0},{1,3},{3,1},{4,6},{6,4},{5,7},{7,5},{8,10},{10,8},{9,1... | collective-permute-start | bytes 86024 | tf_op jit(solution)/shard_map/ppermute | solution.py:493
  15.7 2.4 %collective-permute-done.3.peer_ref = bf16[16,896]{1,0:T(8,128)(2,1)S(1)} collective-permute-done((bf16[16,896]{1,0:T(8,128)(2,1)S(1)}, bf16[16,896]{1,0:T(8,128)(2,1)S(1)}, u32[]{:S(2)}, u32[]{:S(2)}) %collective-permute-start.3) | collective-permute-done | bytes 28704 | tf_op jit(solution)/shard_map/ppermute | solution.py:493
  18.1 0.1 merge.1
  18.2 0.1 collective-permute-start.4
  18.2 1.3 %collective-permute-start.5 = (bf16[32,896]{1,0:T(8,128)(2,1)S(1)}, bf16[32,896]{1,0:T(8,128)(2,1)S(1)}, u32[]{:S(2)}, u32[]{:S(2)}) collective-permute-start(bf16[32,896]{1,0:T(8,128)(2,1)S(1)} %get-tuple-element.34), channel_id=1, source_target_pairs={{0,8},{4,12},{8,0},{12,4},{1,9},{5,13},{9,1},{13,5},{2,10},{6,14},... | collective-permute-start | bytes 172040 | tf_op jit(solution)/shard_map/ppermute | solution.py:472
  19.5 3.1 %collective-permute-start.6 = (bf16[32,896]{1,0:T(8,128)(2,1)S(1)}, bf16[32,896]{1,0:T(8,128)(2,1)S(1)}, u32[]{:S(2)}, u32[]{:S(2)}) collective-permute-start(bf16[32,896]{1,0:T(8,128)(2,1)S(1)} %get-tuple-element.35), channel_id=1, source_target_pairs={{0,12},{4,8},{8,4},{12,0},{1,13},{5,9},{9,5},{13,1},{2,14},{6,10},... | collective-permute-start | bytes 172040 | tf_op jit(solution)/shard_map/ppermute | solution.py:472
  22.6 0.6 %own_chunk.1 = (f32[32,1024]{1,0:T(8,128)S(1)}, f32[32,1024]{1,0:T(8,128)S(1)}) custom-call(bf16[32,896]{1,0:T(8,128)(2,1)S(1)} %get-tuple-element.32.x_ref.refs_0_, bf16[1,6144,1024]{2,1,0:T(8,128)(2,1)S(1)} %copy-done.2, bf16[1,6144,1024]{2,1,0:T(8,128)(2,1)S(1)} %copy-done.4), custom_call_target="tpu_custom_call" | custom-call | flops 41943040000 | bytes 41943040 | tf_op jit(solution)/shard_map/own_chunk/pallas_call | solution.py:504
  23.3 0.1 collective-permute-done.5.refs_2_
  23.4 2.1 %collective-permute-done.6.refs_3_ = bf16[32,896]{1,0:T(8,128)(2,1)S(1)} collective-permute-done((bf16[32,896]{1,0:T(8,128)(2,1)S(1)}, bf16[32,896]{1,0:T(8,128)(2,1)S(1)}, u32[]{:S(2)}, u32[]{:S(2)}) %collective-permute-start.6) | collective-permute-done | bytes 57376 | tf_op jit(solution)/shard_map/ppermute | solution.py:472
  25.5 0.1 collective-permute-start.7
  25.6 1.7 %first_half.1 = (f32[32,1024]{1,0:T(8,128)S(1)}, f32[32,1024]{1,0:T(8,128)S(1)}) custom-call(bf16[4,32,896]{2,1,0:T(8,128)(2,1)S(1)} %stack.1.x_ref.own_ref, f32[32,1024]{1,0:T(8,128)S(1)} %get-tuple-element.36.refs_4_.gate_in, f32[32,1024]{1,0:T(8,128)S(1)} %get-tuple-element.37.up_in, bf16[1,6144,1024]{2,1,0:T(8,128)(2,1)S(1)} %copy-done.2, ...), custom_call_target="tpu_custom_call" | custom-call | flops 8388608000 | bytes 8388608 | tf_op jit(solution)/shard_map/first_half/pallas_call | solution.py:515
  27.3 0.0 collective-permute-done.7.x_ref
  27.3 0.0 copy-start.3
  27.4 4.6 %copy-done.3 = bf16[1,6144,1024]{2,1,0:T(8,128)(2,1)S(1)} copy-done((bf16[1,6144,1024]{2,1,0:T(8,128)(2,1)S(1)}, bf16[1,6144,1024]{2,1,0:T(8,128)(2,1)}, u32[]{:S(2)}) %copy-start.3) | copy-done | bytes 12582936
  31.9 4.6 %copy-done.5 = bf16[1,6144,1024]{2,1,0:T(8,128)(2,1)S(1)} copy-done((bf16[1,6144,1024]{2,1,0:T(8,128)(2,1)S(1)}, bf16[1,6144,1024]{2,1,0:T(8,128)(2,1)}, u32[]{:S(2)}) %copy-start.5) | copy-done | bytes 12582936
  36.5 2.3 %second_half.1.hidden_ref = bf16[32,1024]{1,0:T(8,128)(2,1)S(1)} custom-call(bf16[4,32,896]{2,1,0:T(8,128)(2,1)S(1)} %collective-permute-done.7.x_ref, bf16[4,32,896]{2,1,0:T(8,128)(2,1)S(1)} %stack.1.x_ref.own_ref, f32[32,1024]{1,0:T(8,128)S(1)} %get-tuple-element.38.gate_in, f32[32,1024]{1,0:T(8,128)S(1)} %get-tuple-element.39.up_in, ...), custom_call_target="tpu_custom_call" | custom-call | flops 8388608000 | bytes 8388608 | tf_op jit(solution)/shard_map/second_half/pallas_call | solution.py:523
  38.8 0.5 collective-permute-start.8
  39.3 4.6 %copy-done.6 = bf16[1,2048,3072]{2,1,0:T(8,128)(2,1)S(1)} copy-done((bf16[1,2048,3072]{2,1,0:T(8,128)(2,1)S(1)}, bf16[1,2048,3072]{2,1,0:T(8,128)(2,1)}, u32[]{:S(2)}) %copy-start.6) | copy-done | bytes 12582936
  43.9 1.2 %down_first.1.own_ref = f32[32,3072]{1,0:T(8,128)S(1)} custom-call(bf16[32,1024]{1,0:T(8,128)(2,1)S(1)} %second_half.1.hidden_ref, bf16[1,2048,3072]{2,1,0:T(8,128)(2,1)S(1)} %copy-done.6), custom_call_target="tpu_custom_call" | custom-call | flops 6291456000 | bytes 6291456 | tf_op jit(solution)/shard_map/down_first/pallas_call | solution.py:532
  45.1 1.2 %down_second.1 = bf16[8,4,3072]{2,1,0:T(4,128)(2,1)S(1)} custom-call(bf16[32,1024]{1,0:T(8,128)(2,1)S(1)} %collective-permute-done.8.hidden_ref, f32[32,3072]{1,0:T(8,128)S(1)} %down_first.1.own_ref, bf16[1,2048,3072]{2,1,0:T(8,128)(2,1)S(1)} %copy-done.6), custom_call_target="tpu_custom_call" | custom-call | flops 6291456000 | bytes 6291456 | tf_op jit(solution)/shard_map/down_second/pallas_call | solution.py:540
  46.3 13.2 %all_to_all.5.got_ref = bf16[8,4,3072]{2,1,0:T(4,128)(2,1)S(1)} all-to-all(bf16[8,4,3072]{2,1,0:T(4,128)(2,1)S(1)} %down_second.1), channel_id=1, replica_groups=mesh['groups'=2,'rows'=4,'experts'=2,'heads'=2] {'rows','experts'}, dimensions={0} | all-to-all | bytes 393216 | tf_op jit(solution)/shard_map/all_to_all | solution.py:547
  59.6 1.3 %mix.1 = (bf16[2,2,3072]{2,1,0:T(2,128)(2,1)}, bf16[2,2,3072]{2,1,0:T(2,128)(2,1)}) custom-call(s32[2,2,2]{2,1,0:T(2,128)S(1)} %copy-done, f32[2,2,2]{2,1,0:T(2,128)S(1)} %copy-done.1, bf16[8,4,3072]{2,1,0:T(4,128)(2,1)S(1)} %all_to_all.5.got_ref, bf16[4,32,896]{2,1,0:T(8,128)(2,1)S(1)} %stack.1.x_ref.own_ref), custom_call_target="tpu_custom_call" | custom-call | tf_op jit(solution)/shard_map/mix/pallas_call | solution.py:549
  (14 shorter events, 0.0 us)
Async XLA Ops:
  1.6 11.9 %copy-start.7 = (bf16[6144]{0:T(1024)(128)(2,1)S(1)}, bf16[6144]{0:T(1024)(128)(2,1)}, u32[]{:S(2)}) copy-start(bf16[6144]{0:T(1024)(128)(2,1)} %param.16) | copy-start | bytes 36868
  1.6 21.0 %copy-start.2 = (bf16[1,6144,1024]{2,1,0:T(8,128)(2,1)S(1)}, bf16[1,6144,1024]{2,1,0:T(8,128)(2,1)}, u32[]{:S(2)}) copy-start(bf16[1,6144,1024]{2,1,0:T(8,128)(2,1)} %gate_w.5) | copy-start | bytes 37748740
  1.7 21.0 %copy-start.4 = (bf16[1,6144,1024]{2,1,0:T(8,128)(2,1)S(1)}, bf16[1,6144,1024]{2,1,0:T(8,128)(2,1)}, u32[]{:S(2)}) copy-start(bf16[1,6144,1024]{2,1,0:T(8,128)(2,1)} %up_w.5) | copy-start | bytes 37748740
  1.9 5.7 %collective-permute-start = (bf16[192,128]{1,0:T(8,128)(2,1)S(1)}, bf16[192,128]{1,0:T(8,128)(2,1)S(1)}, u32[]{:S(2)}, u32[]{:S(2)}) collective-permute-start(bf16[192,128]{1,0:T(8,128)(2,1)S(1)} %get-tuple-element.27), channel_id=1, source_target_pairs={{0,4},{4,0},{8,12},{12,8},{1,5},{5,1},{9,13},{13,9},{2,6},{6,2},{1... | collective-permute-start | bytes 147464 | tf_op jit(solution)/shard_map/ppermute | solution.py:472
  5.0 5.9 %collective-permute-start.1 = (bf16[192,128]{1,0:T(8,128)(2,1)S(1)}, bf16[192,128]{1,0:T(8,128)(2,1)S(1)}, u32[]{:S(2)}, u32[]{:S(2)}) collective-permute-start(bf16[192,128]{1,0:T(8,128)(2,1)S(1)} %get-tuple-element.28), channel_id=1, source_target_pairs={{0,8},{4,12},{8,0},{12,4},{1,9},{5,13},{9,1},{13,5},{2,10},{6,14},... | collective-permute-start | bytes 147464 | tf_op jit(solution)/shard_map/ppermute | solution.py:472
  7.6 5.9 %collective-permute-start.2 = (bf16[192,128]{1,0:T(8,128)(2,1)S(1)}, bf16[192,128]{1,0:T(8,128)(2,1)S(1)}, u32[]{:S(2)}, u32[]{:S(2)}) collective-permute-start(bf16[192,128]{1,0:T(8,128)(2,1)S(1)} %get-tuple-element.29), channel_id=1, source_target_pairs={{0,12},{4,8},{8,4},{12,0},{1,13},{5,9},{9,5},{13,1},{2,14},{6,10},... | collective-permute-start | bytes 147464 | tf_op jit(solution)/shard_map/ppermute | solution.py:472
  14.2 3.9 %collective-permute-start.3 = (bf16[16,896]{1,0:T(8,128)(2,1)S(1)}, bf16[16,896]{1,0:T(8,128)(2,1)S(1)}, u32[]{:S(2)}, u32[]{:S(2)}) collective-permute-start(bf16[16,896]{1,0:T(8,128)(2,1)S(1)} %get-tuple-element.30.own_ref), channel_id=1, source_target_pairs={{0,2},{2,0},{1,3},{3,1},{4,6},{6,4},{5,7},{7,5},{8,10},{10,8},{9,1... | collective-permute-start | bytes 86024 | tf_op jit(solution)/shard_map/ppermute | solution.py:493
  18.2 5.1 %collective-permute-start.4 = (bf16[32,896]{1,0:T(8,128)(2,1)S(1)}, bf16[32,896]{1,0:T(8,128)(2,1)S(1)}, u32[]{:S(2)}, u32[]{:S(2)}) collective-permute-start(bf16[32,896]{1,0:T(8,128)(2,1)S(1)} %get-tuple-element.33), channel_id=1, source_target_pairs={{0,4},{4,0},{8,12},{12,8},{1,5},{5,1},{9,13},{13,9},{2,6},{6,2},{1... | collective-permute-start | bytes 172040 | tf_op jit(solution)/shard_map/ppermute | solution.py:472
  18.2 5.1 %collective-permute-start.5 = (bf16[32,896]{1,0:T(8,128)(2,1)S(1)}, bf16[32,896]{1,0:T(8,128)(2,1)S(1)}, u32[]{:S(2)}, u32[]{:S(2)}) collective-permute-start(bf16[32,896]{1,0:T(8,128)(2,1)S(1)} %get-tuple-element.34), channel_id=1, source_target_pairs={{0,8},{4,12},{8,0},{12,4},{1,9},{5,13},{9,1},{13,5},{2,10},{6,14},... | collective-permute-start | bytes 172040 | tf_op jit(solution)/shard_map/ppermute | solution.py:472
  19.5 6.0 %collective-permute-start.6 = (bf16[32,896]{1,0:T(8,128)(2,1)S(1)}, bf16[32,896]{1,0:T(8,128)(2,1)S(1)}, u32[]{:S(2)}, u32[]{:S(2)}) collective-permute-start(bf16[32,896]{1,0:T(8,128)(2,1)S(1)} %get-tuple-element.35), channel_id=1, source_target_pairs={{0,12},{4,8},{8,4},{12,0},{1,13},{5,9},{9,5},{13,1},{2,14},{6,10},... | collective-permute-start | bytes 172040 | tf_op jit(solution)/shard_map/ppermute | solution.py:472
  25.5 1.8 %collective-permute-start.7 = (bf16[4,32,896]{2,1,0:T(8,128)(2,1)S(1)}, bf16[4,32,896]{2,1,0:T(8,128)(2,1)S(1)}, u32[]{:S(2)}, u32[]{:S(2)}) collective-permute-start(bf16[4,32,896]{2,1,0:T(8,128)(2,1)S(1)} %stack.1.x_ref.own_ref), channel_id=1, source_target_pairs={{0,1},{1,0},{2,3},{3,2},{4,5},{5,4},{6,7},{7,6},{8,9},{9,8},{10,11... | collective-permute-start | bytes 688136 | tf_op jit(solution)/shard_map/ppermute | solution.py:514
  27.3 4.6 %copy-start.3 = (bf16[1,6144,1024]{2,1,0:T(8,128)(2,1)S(1)}, bf16[1,6144,1024]{2,1,0:T(8,128)(2,1)}, u32[]{:S(2)}) copy-start(bf16[1,6144,1024]{2,1,0:T(8,128)(2,1)} %gate_w.5) | copy-start | bytes 37748740
  31.9 4.6 %copy-start.5 = (bf16[1,6144,1024]{2,1,0:T(8,128)(2,1)S(1)}, bf16[1,6144,1024]{2,1,0:T(8,128)(2,1)}, u32[]{:S(2)}) copy-start(bf16[1,6144,1024]{2,1,0:T(8,128)(2,1)} %up_w.5) | copy-start | bytes 37748740
  38.8 6.3 %collective-permute-start.8 = (bf16[32,1024]{1,0:T(8,128)(2,1)S(1)}, bf16[32,1024]{1,0:T(8,128)(2,1)S(1)}, u32[]{:S(2)}, u32[]{:S(2)}) collective-permute-start(bf16[32,1024]{1,0:T(8,128)(2,1)S(1)} %second_half.1.hidden_ref), channel_id=1, source_target_pairs={{0,1},{1,0},{2,3},{3,2},{4,5},{5,4},{6,7},{7,6},{8,9},{9,8},{10,11... | collective-permute-start | bytes 196616 | tf_op jit(solution)/shard_map/ppermute | solution.py:531
  39.3 4.6 %copy-start.6 = (bf16[1,2048,3072]{2,1,0:T(8,128)(2,1)S(1)}, bf16[1,2048,3072]{2,1,0:T(8,128)(2,1)}, u32[]{:S(2)}) copy-start(bf16[1,2048,3072]{2,1,0:T(8,128)(2,1)} %down_w.3) | copy-start | bytes 37748740
  45.1 14.5 %copy-start = (s32[2,2,2]{2,1,0:T(2,128)S(1)}, s32[2,2,2]{2,1,0:T(2,128)}, u32[]{:S(2)}) copy-start(s32[2,2,2]{2,1,0:T(2,128)} %routes_ref.1) | copy-start | bytes 100
  45.1 14.5 %copy-start.1 = (f32[2,2,2]{2,1,0:T(2,128)S(1)}, f32[2,2,2]{2,1,0:T(2,128)}, u32[]{:S(2)}) copy-start(f32[2,2,2]{2,1,0:T(2,128)} %gates_ref.1) | copy-start | bytes 100

commit v5 on v4

--- a/solution.py
+++ b/solution.py
@@ -17,11 +17,11 @@
 PACK_COVER = 40 * MIB
 FLOPS = 1000
 OWN_COVER = 40 * MIB
-FIRST_COVER = 8 * MIB
-SECOND_COVER = 8 * MIB
+FIRST_COVER = 1 * MIB
+SECOND_COVER = 1 * MIB
 FIRST_LIMIT = 4 * MIB
-SECOND_LIMIT = 24 * MIB
-DOWN_LIMIT = 40 * MIB
+SECOND_LIMIT = 4 * MIB
+DOWN_LIMIT = 4 * MIB
 ATTEND_COVER = MIB
 MERGE_COVER = MIB
 

time: 61.1 us -> 48.1 us (0.79)
  local copies, waits for them, and re-layouts: 13.7 us -> 0.33 us
    unnamed x16, local copies, waits for them, and re-layouts: 13.7 us -> 0.33 us
  transfers between devices with their start and end apart: 9 -> 9, of which waited for: 5 -> 5; matrix products, arithmetic and copies ran while one was open for 0% -> 0% of each run, Pallas kernels for 6% -> 7%
where the time goes in v5:
time: 48.1 us; the launch traced here: 47.9 us
  blocking collectives  13.7 us (28%)
  starting transfers between devices  12.2 us (25%)
  waiting for transfers between devices  10.5 us (22%)
  Pallas kernels  10.3 us (21%)
  between operations  0.78 us (2%)
    all_to_all x1, blocking collectives, per_device(): lax.all_to_all(blocks, ('rows', 'experts'), split_axis=0, concat_axis=0,...  13.7 us
    ppermute x6, starting transfers between devices, spread(): lax.ppermute(pieces[k], 'rows', [(i, i ^ k) for i in range(rows)])  10.2 us
    ppermute x6, waiting for transfers between devices, spread(): lax.ppermute(pieces[k], 'rows', [(i, i ^ k) for i in range(rows)])  8.12 us
    ppermute x1, waiting for transfers between devices, per_device(): peer = lax.ppermute(x, 'experts', swap)  2.38 us
    pallas_call x1, Pallas kernels, per_device(): call(functools.partial(second_half_body, plan), shape((tokens, units), bf...  2.27 us
    pallas_call x1, Pallas kernels, per_device(): call(first_half_body, (products_of, products_of), 'vvvvv', 'first_half',...  1.71 us
    ppermute x1, starting transfers between devices, per_device(): peer = lax.ppermute(x, 'experts', swap)  1.5 us
    pallas_call x1, Pallas kernels, per_device(): call(functools.partial(mix_body, rows), (out, out), 'ssvv', 'mix')  1.28 us
  transfers between devices with their start and end apart: 9, of which 5 were waited for; matrix products, arithmetic and copies ran while one was open for 0% of the time, Pallas kernels for 7%

profile of v5, /device:TPU:0, one launch (start us, length us, event | category | flops | bytes accessed | tf_op | source)
XLA Modules:
  0.0 47.9 jit_solution(5843825926964656899)
XLA Ops:
  0.6 1.0 %fetch.1 = (bf16[2,128]{1,0:T(2,128)(2,1)S(1)}, bf16[2,2,3072]{2,1,0:T(2,128)(2,1)S(1)}, bf16[2,2,2,512]{3,2,1,0:T(2,128)(2,1)S(1)}, bf16[2,32,2,512]{3,2,1,0:T(2,128)(2,1)S(1)}, bf16[2,2,3072]{2,1,0:T(2,128)(2,1)S(1)}) custom-call(s32[2]{0:T(128)} %refs_0_.1, bf16[2,2,3072]{2,1,0:T(2,128)(2,1)} %refs_1_.1, bf16[2,2,2,512]{3,2,1,0:T(2,128)(2,1)} %refs_2_.1, ...), custom_call_target="tpu_custom_call" | custom-call | tf_op jit(solution)/shard_map/fetch/pallas_call | solution.py:451
  1.6 0.0 copy-start.4
  1.6 0.0 copy-start
  1.7 0.0 copy-start.1
  1.7 0.3 pack.1
  1.9 3.1 %collective-permute-start = (bf16[192,128]{1,0:T(8,128)(2,1)S(1)}, bf16[192,128]{1,0:T(8,128)(2,1)S(1)}, u32[]{:S(2)}, u32[]{:S(2)}) collective-permute-start(bf16[192,128]{1,0:T(8,128)(2,1)S(1)} %get-tuple-element.27), channel_id=1, source_target_pairs={{0,4},{4,0},{8,12},{12,8},{1,5},{5,1},{9,13},{13,9},{2,6},{6,2},{1... | collective-permute-start | bytes 147464 | tf_op jit(solution)/shard_map/ppermute | solution.py:472
  5.0 2.6 %collective-permute-start.1 = (bf16[192,128]{1,0:T(8,128)(2,1)S(1)}, bf16[192,128]{1,0:T(8,128)(2,1)S(1)}, u32[]{:S(2)}, u32[]{:S(2)}) collective-permute-start(bf16[192,128]{1,0:T(8,128)(2,1)S(1)} %get-tuple-element.28), channel_id=1, source_target_pairs={{0,8},{4,12},{8,0},{12,4},{1,9},{5,13},{9,1},{13,5},{2,10},{6,14},... | collective-permute-start | bytes 147464 | tf_op jit(solution)/shard_map/ppermute | solution.py:472
  7.6 3.3 %collective-permute-done.1.refs_2_ = bf16[192,128]{1,0:T(8,128)(2,1)S(1)} collective-permute-done((bf16[192,128]{1,0:T(8,128)(2,1)S(1)}, bf16[192,128]{1,0:T(8,128)(2,1)S(1)}, u32[]{:S(2)}, u32[]{:S(2)}) %collective-permute-start.1) | collective-permute-done | bytes 49184 | tf_op jit(solution)/shard_map/ppermute | solution.py:472
  11.0 2.6 %collective-permute-done.2.refs_3_ = bf16[192,128]{1,0:T(8,128)(2,1)S(1)} collective-permute-done((bf16[192,128]{1,0:T(8,128)(2,1)S(1)}, bf16[192,128]{1,0:T(8,128)(2,1)S(1)}, u32[]{:S(2)}, u32[]{:S(2)}) %collective-permute-start.2) | collective-permute-done | bytes 49184 | tf_op jit(solution)/shard_map/ppermute | solution.py:472
  13.5 0.7 %attend.1 = (bf16[16,896]{1,0:T(8,128)(2,1)S(1)}, bf16[96,128]{1,0:T(8,128)(2,1)S(1)}) custom-call(bf16[192,128]{1,0:T(8,128)(2,1)S(1)} %get-tuple-element.26.refs_0_, bf16[192,128]{1,0:T(8,128)(2,1)S(1)} %collective-permute-done.refs_1_, bf16[192,128]{1,0:T(8,128)(2,1)S(1)} %collective-permute-done.1.refs_2_, ...), custom_call_target="tpu_custom_call" | custom-call | flops 1048576000 | bytes 1048576 | tf_op jit(solution)/shard_map/attend/pallas_call | solution.py:478
  14.2 1.5 %collective-permute-start.3 = (bf16[16,896]{1,0:T(8,128)(2,1)S(1)}, bf16[16,896]{1,0:T(8,128)(2,1)S(1)}, u32[]{:S(2)}, u32[]{:S(2)}) collective-permute-start(bf16[16,896]{1,0:T(8,128)(2,1)S(1)} %get-tuple-element.30.own_ref), channel_id=1, source_target_pairs={{0,2},{2,0},{1,3},{3,1},{4,6},{6,4},{5,7},{7,5},{8,10},{10,8},{9,1... | collective-permute-start | bytes 86024 | tf_op jit(solution)/shard_map/ppermute | solution.py:493
  15.7 2.4 %collective-permute-done.3.peer_ref = bf16[16,896]{1,0:T(8,128)(2,1)S(1)} collective-permute-done((bf16[16,896]{1,0:T(8,128)(2,1)S(1)}, bf16[16,896]{1,0:T(8,128)(2,1)S(1)}, u32[]{:S(2)}, u32[]{:S(2)}) %collective-permute-start.3) | collective-permute-done | bytes 28704 | tf_op jit(solution)/shard_map/ppermute | solution.py:493
  18.1 0.1 merge.1
  18.2 0.1 collective-permute-start.4
  18.2 1.3 %collective-permute-start.5 = (bf16[32,896]{1,0:T(8,128)(2,1)S(1)}, bf16[32,896]{1,0:T(8,128)(2,1)S(1)}, u32[]{:S(2)}, u32[]{:S(2)}) collective-permute-start(bf16[32,896]{1,0:T(8,128)(2,1)S(1)} %get-tuple-element.34), channel_id=1, source_target_pairs={{0,8},{4,12},{8,0},{12,4},{1,9},{5,13},{9,1},{13,5},{2,10},{6,14},... | collective-permute-start | bytes 172040 | tf_op jit(solution)/shard_map/ppermute | solution.py:472
  19.5 3.1 %collective-permute-start.6 = (bf16[32,896]{1,0:T(8,128)(2,1)S(1)}, bf16[32,896]{1,0:T(8,128)(2,1)S(1)}, u32[]{:S(2)}, u32[]{:S(2)}) collective-permute-start(bf16[32,896]{1,0:T(8,128)(2,1)S(1)} %get-tuple-element.35), channel_id=1, source_target_pairs={{0,12},{4,8},{8,4},{12,0},{1,13},{5,9},{9,5},{13,1},{2,14},{6,10},... | collective-permute-start | bytes 172040 | tf_op jit(solution)/shard_map/ppermute | solution.py:472
  22.6 0.6 %own_chunk.1 = (f32[32,1024]{1,0:T(8,128)S(1)}, f32[32,1024]{1,0:T(8,128)S(1)}) custom-call(bf16[32,896]{1,0:T(8,128)(2,1)S(1)} %get-tuple-element.32.x_ref.refs_0_, bf16[1,6144,1024]{2,1,0:T(8,128)(2,1)S(1)} %copy-done, bf16[1,6144,1024]{2,1,0:T(8,128)(2,1)S(1)} %copy-done.1), custom_call_target="tpu_custom_call" | custom-call | flops 41943040000 | bytes 41943040 | tf_op jit(solution)/shard_map/own_chunk/pallas_call | solution.py:504
  23.3 0.1 collective-permute-done.5.refs_2_
  23.4 2.1 %collective-permute-done.6.refs_3_ = bf16[32,896]{1,0:T(8,128)(2,1)S(1)} collective-permute-done((bf16[32,896]{1,0:T(8,128)(2,1)S(1)}, bf16[32,896]{1,0:T(8,128)(2,1)S(1)}, u32[]{:S(2)}, u32[]{:S(2)}) %collective-permute-start.6) | collective-permute-done | bytes 57376 | tf_op jit(solution)/shard_map/ppermute | solution.py:472
  25.5 0.1 collective-permute-start.7
  25.6 0.0 slice-start
  25.6 1.7 %first_half.1 = (f32[32,1024]{1,0:T(8,128)S(1)}, f32[32,1024]{1,0:T(8,128)S(1)}) custom-call(bf16[4,32,896]{2,1,0:T(8,128)(2,1)S(1)} %stack.1.x_ref.own_ref, f32[32,1024]{1,0:T(8,128)S(1)} %get-tuple-element.36.refs_4_.gate_in, f32[32,1024]{1,0:T(8,128)S(1)} %get-tuple-element.37.up_in, bf16[1,6144,1024]{2,1,0:T(8,128)(2,1)S(1)} %copy-done, ...), custom_call_target="tpu_custom_call" | custom-call | flops 1048576000 | bytes 1048576 | tf_op jit(solution)/shard_map/first_half/pallas_call | solution.py:515
  27.3 0.0 collective-permute-done.7.x_ref
  27.4 0.0 slice-start.2
  27.4 2.3 %second_half.1.hidden_ref = bf16[32,1024]{1,0:T(8,128)(2,1)S(1)} custom-call(bf16[4,32,896]{2,1,0:T(8,128)(2,1)S(1)} %collective-permute-done.7.x_ref, bf16[4,32,896]{2,1,0:T(8,128)(2,1)S(1)} %stack.1.x_ref.own_ref, f32[32,1024]{1,0:T(8,128)S(1)} %get-tuple-element.38.gate_in, f32[32,1024]{1,0:T(8,128)S(1)} %get-tuple-element.39.up_in, ...), custom_call_target="tpu_custom_call" | custom-call | flops 1048576000 | bytes 1048576 | tf_op jit(solution)/shard_map/second_half/pallas_call | solution.py:523
  29.7 0.5 %collective-permute-start.8 = (bf16[32,1024]{1,0:T(8,128)(2,1)S(1)}, bf16[32,1024]{1,0:T(8,128)(2,1)S(1)}, u32[]{:S(2)}, u32[]{:S(2)}) collective-permute-start(bf16[32,1024]{1,0:T(8,128)(2,1)S(1)} %second_half.1.hidden_ref), channel_id=1, source_target_pairs={{0,1},{1,0},{2,3},{3,2},{4,5},{5,4},{6,7},{7,6},{8,9},{9,8},{10,11... | collective-permute-start | bytes 196616 | tf_op jit(solution)/shard_map/ppermute | solution.py:531
  30.2 0.3 slice-done.2
  30.5 1.2 %down_first.1.own_ref = f32[32,3072]{1,0:T(8,128)S(1)} custom-call(bf16[32,1024]{1,0:T(8,128)(2,1)S(1)} %second_half.1.hidden_ref, bf16[1,2048,3072]{2,1,0:T(8,128)(2,1)S(1)} %bitcast.2), custom_call_target="tpu_custom_call" | custom-call | flops 6291456000 | bytes 6291456 | tf_op jit(solution)/shard_map/down_first/pallas_call | solution.py:532
  31.7 0.0 collective-permute-done.8.hidden_ref
  31.7 1.2 %down_second.1 = bf16[8,4,3072]{2,1,0:T(4,128)(2,1)S(1)} custom-call(bf16[32,1024]{1,0:T(8,128)(2,1)S(1)} %collective-permute-done.8.hidden_ref, f32[32,3072]{1,0:T(8,128)S(1)} %down_first.1.own_ref, bf16[1,2048,3072]{2,1,0:T(8,128)(2,1)S(1)} %bitcast.2), custom_call_target="tpu_custom_call" | custom-call | flops 6291456000 | bytes 6291456 | tf_op jit(solution)/shard_map/down_second/pallas_call | solution.py:540
  32.9 13.7 %all_to_all.5.got_ref = bf16[8,4,3072]{2,1,0:T(4,128)(2,1)S(1)} all-to-all(bf16[8,4,3072]{2,1,0:T(4,128)(2,1)S(1)} %down_second.1), channel_id=1, replica_groups=mesh['groups'=2,'rows'=4,'experts'=2,'heads'=2] {'rows','experts'}, dimensions={0} | all-to-all | bytes 393216 | tf_op jit(solution)/shard_map/all_to_all | solution.py:547
  46.6 1.3 %mix.1 = (bf16[2,2,3072]{2,1,0:T(2,128)(2,1)}, bf16[2,2,3072]{2,1,0:T(2,128)(2,1)}) custom-call(s32[2,2,2]{2,1,0:T(2,128)S(1)} %copy-done.2, f32[2,2,2]{2,1,0:T(2,128)S(1)} %copy-done.3, bf16[8,4,3072]{2,1,0:T(4,128)(2,1)S(1)} %all_to_all.5.got_ref, bf16[4,32,896]{2,1,0:T(8,128)(2,1)S(1)} %stack.1.x_ref.own_ref), custom_call_target="tpu_custom_call" | custom-call | tf_op jit(solution)/shard_map/mix/pallas_call | solution.py:549
  (15 shorter events, 0.0 us)
Async XLA Ops:
  1.6 11.9 %copy-start.4 = (bf16[6144]{0:T(1024)(128)(2,1)S(1)}, bf16[6144]{0:T(1024)(128)(2,1)}, u32[]{:S(2)}) copy-start(bf16[6144]{0:T(1024)(128)(2,1)} %param.16) | copy-start | bytes 36868
  1.6 21.0 %copy-start = (bf16[1,6144,1024]{2,1,0:T(8,128)(2,1)S(1)}, bf16[1,6144,1024]{2,1,0:T(8,128)(2,1)}, u32[]{:S(2)}) copy-start(bf16[1,6144,1024]{2,1,0:T(8,128)(2,1)} %gate_w.5) | copy-start | bytes 37748740
  1.7 21.0 %copy-start.1 = (bf16[1,6144,1024]{2,1,0:T(8,128)(2,1)S(1)}, bf16[1,6144,1024]{2,1,0:T(8,128)(2,1)}, u32[]{:S(2)}) copy-start(bf16[1,6144,1024]{2,1,0:T(8,128)(2,1)} %up_w.5) | copy-start | bytes 37748740
  1.9 5.7 %collective-permute-start = (bf16[192,128]{1,0:T(8,128)(2,1)S(1)}, bf16[192,128]{1,0:T(8,128)(2,1)S(1)}, u32[]{:S(2)}, u32[]{:S(2)}) collective-permute-start(bf16[192,128]{1,0:T(8,128)(2,1)S(1)} %get-tuple-element.27), channel_id=1, source_target_pairs={{0,4},{4,0},{8,12},{12,8},{1,5},{5,1},{9,13},{13,9},{2,6},{6,2},{1... | collective-permute-start | bytes 147464 | tf_op jit(solution)/shard_map/ppermute | solution.py:472
  5.0 5.9 %collective-permute-start.1 = (bf16[192,128]{1,0:T(8,128)(2,1)S(1)}, bf16[192,128]{1,0:T(8,128)(2,1)S(1)}, u32[]{:S(2)}, u32[]{:S(2)}) collective-permute-start(bf16[192,128]{1,0:T(8,128)(2,1)S(1)} %get-tuple-element.28), channel_id=1, source_target_pairs={{0,8},{4,12},{8,0},{12,4},{1,9},{5,13},{9,1},{13,5},{2,10},{6,14},... | collective-permute-start | bytes 147464 | tf_op jit(solution)/shard_map/ppermute | solution.py:472
  7.6 5.9 %collective-permute-start.2 = (bf16[192,128]{1,0:T(8,128)(2,1)S(1)}, bf16[192,128]{1,0:T(8,128)(2,1)S(1)}, u32[]{:S(2)}, u32[]{:S(2)}) collective-permute-start(bf16[192,128]{1,0:T(8,128)(2,1)S(1)} %get-tuple-element.29), channel_id=1, source_target_pairs={{0,12},{4,8},{8,4},{12,0},{1,13},{5,9},{9,5},{13,1},{2,14},{6,10},... | collective-permute-start | bytes 147464 | tf_op jit(solution)/shard_map/ppermute | solution.py:472
  14.2 3.9 %collective-permute-start.3 = (bf16[16,896]{1,0:T(8,128)(2,1)S(1)}, bf16[16,896]{1,0:T(8,128)(2,1)S(1)}, u32[]{:S(2)}, u32[]{:S(2)}) collective-permute-start(bf16[16,896]{1,0:T(8,128)(2,1)S(1)} %get-tuple-element.30.own_ref), channel_id=1, source_target_pairs={{0,2},{2,0},{1,3},{3,1},{4,6},{6,4},{5,7},{7,5},{8,10},{10,8},{9,1... | collective-permute-start | bytes 86024 | tf_op jit(solution)/shard_map/ppermute | solution.py:493
  18.2 5.1 %collective-permute-start.4 = (bf16[32,896]{1,0:T(8,128)(2,1)S(1)}, bf16[32,896]{1,0:T(8,128)(2,1)S(1)}, u32[]{:S(2)}, u32[]{:S(2)}) collective-permute-start(bf16[32,896]{1,0:T(8,128)(2,1)S(1)} %get-tuple-element.33), channel_id=1, source_target_pairs={{0,4},{4,0},{8,12},{12,8},{1,5},{5,1},{9,13},{13,9},{2,6},{6,2},{1... | collective-permute-start | bytes 172040 | tf_op jit(solution)/shard_map/ppermute | solution.py:472
  18.2 5.1 %collective-permute-start.5 = (bf16[32,896]{1,0:T(8,128)(2,1)S(1)}, bf16[32,896]{1,0:T(8,128)(2,1)S(1)}, u32[]{:S(2)}, u32[]{:S(2)}) collective-permute-start(bf16[32,896]{1,0:T(8,128)(2,1)S(1)} %get-tuple-element.34), channel_id=1, source_target_pairs={{0,8},{4,12},{8,0},{12,4},{1,9},{5,13},{9,1},{13,5},{2,10},{6,14},... | collective-permute-start | bytes 172040 | tf_op jit(solution)/shard_map/ppermute | solution.py:472
  19.5 6.0 %collective-permute-start.6 = (bf16[32,896]{1,0:T(8,128)(2,1)S(1)}, bf16[32,896]{1,0:T(8,128)(2,1)S(1)}, u32[]{:S(2)}, u32[]{:S(2)}) collective-permute-start(bf16[32,896]{1,0:T(8,128)(2,1)S(1)} %get-tuple-element.35), channel_id=1, source_target_pairs={{0,12},{4,8},{8,4},{12,0},{1,13},{5,9},{9,5},{13,1},{2,14},{6,10},... | collective-permute-start | bytes 172040 | tf_op jit(solution)/shard_map/ppermute | solution.py:472
  25.5 1.8 %collective-permute-start.7 = (bf16[4,32,896]{2,1,0:T(8,128)(2,1)S(1)}, bf16[4,32,896]{2,1,0:T(8,128)(2,1)S(1)}, u32[]{:S(2)}, u32[]{:S(2)}) collective-permute-start(bf16[4,32,896]{2,1,0:T(8,128)(2,1)S(1)} %stack.1.x_ref.own_ref), channel_id=1, source_target_pairs={{0,1},{1,0},{2,3},{3,2},{4,5},{5,4},{6,7},{7,6},{8,9},{9,8},{10,11... | collective-permute-start | bytes 688136 | tf_op jit(solution)/shard_map/ppermute | solution.py:514
  25.6 4.6 %slice-start = ((s8[12582912]{0:T(1024)(128)(4,1)}), s8[4194304]{0:T(1024)(128)(4,1)S(1)}, s32[]{:S(2)}) async-start(s8[12582912]{0:T(1024)(128)(4,1)} %bitcast.1), calls=%async_computation.1 | async-start | bytes 8388608
  25.6 4.6 %slice-start.1 = ((s8[12582912]{0:T(1024)(128)(4,1)}), s8[4194304]{0:T(1024)(128)(4,1)S(1)}, s32[]{:S(2)}) async-start(s8[12582912]{0:T(1024)(128)(4,1)} %bitcast.1), calls=%async_computation.2 | async-start | bytes 8388608
  27.4 3.1 %slice-start.2 = ((s8[12582912]{0:T(1024)(128)(4,1)}), s8[4194304]{0:T(1024)(128)(4,1)S(1)}, s32[]{:S(2)}) async-start(s8[12582912]{0:T(1024)(128)(4,1)} %bitcast.1), calls=%async_computation.3 | async-start | bytes 8388608
  29.7 2.0 %collective-permute-start.8 = (bf16[32,1024]{1,0:T(8,128)(2,1)S(1)}, bf16[32,1024]{1,0:T(8,128)(2,1)S(1)}, u32[]{:S(2)}, u32[]{:S(2)}) collective-permute-start(bf16[32,1024]{1,0:T(8,128)(2,1)S(1)} %second_half.1.hidden_ref), channel_id=1, source_target_pairs={{0,1},{1,0},{2,3},{3,2},{4,5},{5,4},{6,7},{7,6},{8,9},{9,8},{10,11... | collective-permute-start | bytes 196616 | tf_op jit(solution)/shard_map/ppermute | solution.py:531
  31.7 15.0 %copy-start.2 = (s32[2,2,2]{2,1,0:T(2,128)S(1)}, s32[2,2,2]{2,1,0:T(2,128)}, u32[]{:S(2)}) copy-start(s32[2,2,2]{2,1,0:T(2,128)} %routes_ref.1) | copy-start | bytes 100
  31.7 15.0 %copy-start.3 = (f32[2,2,2]{2,1,0:T(2,128)S(1)}, f32[2,2,2]{2,1,0:T(2,128)}, u32[]{:S(2)}) copy-start(f32[2,2,2]{2,1,0:T(2,128)} %gates_ref.1) | copy-start | bytes 100

commit v6 on v5

--- a/solution.py
+++ b/solution.py
@@ -376,47 +376,62 @@
     out_ref[...] = down_product(0, hidden_ref, down_w)
 
 
-def down_second_body(rows, hidden_ref, own_ref, down_w, out_ref):
-    result = (own_ref[...] + down_product(1, hidden_ref, down_w)).astype(jnp.bfloat16)
-    pieces, t, _ = out_ref.shape
-    experts = pieces // rows
-    own = lax.axis_index("experts")
-    for r in range(rows):
-        for e in range(experts):
-            first = (e * rows + r) * t
-            out_ref[r * experts + (own ^ e)] = result[first : first + t]
-
-
-def mix_body(rows, routes_ref, gates_ref, got_ref, own_ref, attn_ref, moe_ref):
-    pieces, t, half = got_ref.shape
-    experts = pieces // rows
-    steps, conts, _ = moe_ref.shape
+def down_second_body(plan, rows, hidden_ref, own_ref, down_w, *outs):
+    result = own_ref[...] + down_product(1, hidden_ref, down_w)
+    t = plan.tokens
+    total = rows * t
+
+    def place(own):
+        for k, out_ref in enumerate(outs):
+            first = (own ^ k) * t
+            pair = [result[i : i + t] for i in (first, first + total)]
+            out_ref[...] = jnp.concatenate(pair, axis=0).astype(jnp.bfloat16)
+
+    for own in range(rows):
+        pl.when(lax.axis_index("rows") == own)(functools.partial(place, own))
+
+
+def sum_body(*refs):
+    *pieces, own_ref, peer_ref = refs
+    total = pieces[0][...].astype(jnp.float32)
+    for ref in pieces[1:]:
+        total = total + ref[...].astype(jnp.float32)
+    t = own_ref.shape[0]
+    own_ref[...] = total[:t].astype(jnp.bfloat16)
+    peer_ref[...] = total[t:].astype(jnp.bfloat16)
+
+
+def attn_body(plan, rows, own_ref, _, attn_ref):
+    t = plan.tokens
     depth = own_ref.shape[2] - HEAD_DIM
     for k in range(rows):
         head = (lax.axis_index("rows") ^ k) * GROUP
         for g in range(GROUP):
             lanes = pl.ds(pl.multiple_of((head + g) * HEAD_DIM, HEAD_DIM), HEAD_DIM)
-            for s in range(steps):
+            for s in range(plan.steps):
                 attn_ref[s, :, lanes] = own_ref[
-                    k, pl.ds(g * t + s * conts, conts), pl.ds(depth, HEAD_DIM)
+                    k, pl.ds(g * t + s * plan.conts, plan.conts), pl.ds(depth, HEAD_DIM)
                 ]
-    row = lax.broadcasted_iota(jnp.int32, (t, 1), 0)
-    mixture = jnp.zeros((t, half), jnp.float32)
-    for e in range(experts):
-        summed = jnp.zeros((t, half), jnp.float32)
-        for r in range(rows):
-            summed = summed + got_ref[r * experts + e].astype(jnp.float32)
-        share = jnp.zeros((t, 1), jnp.float32)
-        for s in range(steps):
-            for c in range(conts):
+
+
+def mix_body(plan, routes_ref, gates_ref, own_ref, peer_ref, moe_ref):
+    own = lax.axis_index("experts")
+    row = lax.broadcasted_iota(jnp.int32, (plan.tokens, 1), 0)
+    mixture = None
+    for expert, ref in ((own, own_ref), (1 - own, peer_ref)):
+        share = jnp.zeros((plan.tokens, 1), jnp.float32)
+        for s in range(plan.steps):
+            for c in range(plan.conts):
                 amount = jnp.float32(0.0)
                 for k in range(routes_ref.shape[2]):
-                    amount = amount + jnp.where(routes_ref[s, c, k] == e, gates_ref[s, c, k], 0.0)
-                share = jnp.where(row == s * conts + c, amount, share)
-        mixture = mixture + share * summed.astype(jnp.bfloat16).astype(jnp.float32)
+                    chosen = routes_ref[s, c, k] == expert
+                    amount = amount + jnp.where(chosen, gates_ref[s, c, k], 0.0)
+                share = jnp.where(row == s * plan.conts + c, amount, share)
+        part = share * ref[...].astype(jnp.float32)
+        mixture = part if mixture is None else mixture + part
     mixture = mixture.astype(jnp.bfloat16)
-    for s in range(steps):
-        moe_ref[s] = mixture[s * conts : (s + 1) * conts]
+    for s in range(plan.steps):
+        moe_ref[s] = mixture[s * plan.conts : (s + 1) * plan.conts]
 
 
 def per_device(
@@ -538,16 +553,19 @@
         cost=cover(2 * plan.half * units),
     )(hidden, down_w)
     blocks = call(
-        functools.partial(down_second_body, rows),
-        shape((rows * experts, plan.tokens, plan.half), bf16),
+        functools.partial(down_second_body, plan, rows),
+        (shape((experts * plan.tokens, plan.half), bf16),) * rows,
         "vvv",
         "down_second",
         cost=cover(2 * plan.half * units),
     )(other_hidden, partial, down_w)
-    blocks = lax.all_to_all(blocks, ("rows", "experts"), split_axis=0, concat_axis=0, tiled=True)
+    output = shape((plan.tokens, plan.half), bf16)
+    mine, theirs = call(sum_body, (output, output), "v" * rows, "sum")(*spread(blocks))
+    returned = lax.ppermute(theirs, "experts", swap)
     out = shape(queries.shape, bf16)
-    attn_out, moe_out = call(functools.partial(mix_body, rows), (out, out), "ssvv", "mix")(
-        routes, route_gates, blocks, own
+    attn_out = call(functools.partial(attn_body, plan, rows), out, "vv", "attn")(own, theirs)
+    moe_out = call(functools.partial(mix_body, plan), out, "ssvv", "mix")(
+        routes, route_gates, mine, returned
     )
     return (attn_out, moe_out)
 

time: 48.1 us -> 47.9 us (level)
  blocking collectives: 13.7 us -> 0 us
  waiting for transfers between devices: 10.5 us -> 17.4 us
  starting transfers between devices: 12.2 us -> 18.2 us
  Pallas kernels: 10.3 us -> 11 us
    all_to_all x1 -> x0, blocking collectives: 13.7 us -> none  [per_device(): lax.all_to_all(blocks, ('rows', 'experts'), split_axis=0, concat_axis=0,...]
    ppermute x6 -> x9, waiting for transfers between devices: 8.12 us -> 13.3 us  [spread(): lax.ppermute(pieces[k], 'rows', [(i, i ^ k) for i in range(rows)])]
    ppermute x6 -> x9, starting transfers between devices: 10.2 us -> 14.6 us  [spread(): lax.ppermute(pieces[k], 'rows', [(i, i ^ k) for i in range(rows)])]
    ppermute x0 -> x1, waiting for transfers between devices: none -> 1.7 us  [per_device(): returned = lax.ppermute(theirs, 'experts', swap)]
    ppermute x0 -> x1, starting transfers between devices: none -> 1.56 us  [per_device(): returned = lax.ppermute(theirs, 'experts', swap)]
    pallas_call x2 -> x4, Pallas kernels: 2.49 us -> 3.16 us  [the longest x1 1.24 us: per_device(): call(functools.partial(down_second_body, plan, rows), (shape((experts * p...]
  transfers between devices with their start and end apart: 9 -> 13, of which waited for: 5 -> 8; matrix products, arithmetic and copies ran while one was open for 0% -> 0% of each run, Pallas kernels for 7% -> 9%
where the time goes in v6:
time: 47.9 us; the launch traced here: 47.7 us
  starting transfers between devices  18.2 us (38%)
  waiting for transfers between devices  17.4 us (36%)
  Pallas kernels  11 us (23%)
  between operations  0.79 us (2%)
    ppermute x9, starting transfers between devices, spread(): lax.ppermute(pieces[k], 'rows', [(i, i ^ k) for i in range(rows)])  14.6 us
    ppermute x9, waiting for transfers between devices, spread(): lax.ppermute(pieces[k], 'rows', [(i, i ^ k) for i in range(rows)])  13.3 us
    ppermute x1, waiting for transfers between devices, per_device(): peer = lax.ppermute(x, 'experts', swap)  2.38 us
    pallas_call x1, Pallas kernels, per_device(): call(functools.partial(second_half_body, plan), shape((tokens, units), bf...  2.27 us
    pallas_call x1, Pallas kernels, per_device(): call(first_half_body, (products_of, products_of), 'vvvvv', 'first_half',...  1.71 us
    ppermute x1, waiting for transfers between devices, per_device(): returned = lax.ppermute(theirs, 'experts', swap)  1.7 us
    ppermute x1, starting transfers between devices, per_device(): returned = lax.ppermute(theirs, 'experts', swap)  1.56 us
    ppermute x1, starting transfers between devices, per_device(): peer = lax.ppermute(x, 'experts', swap)  1.5 us
  transfers between devices with their start and end apart: 13, of which 8 were waited for; matrix products, arithmetic and copies ran while one was open for 0% of the time, Pallas kernels for 9%

profile of v6, /device:TPU:0, one launch (start us, length us, event | category | flops | bytes accessed | tf_op | source)
XLA Modules:
  0.0 47.7 jit_solution(3869739155662554704)
XLA Ops:
  0.6 1.0 %fetch.1 = (bf16[2,128]{1,0:T(2,128)(2,1)S(1)}, bf16[2,2,3072]{2,1,0:T(2,128)(2,1)S(1)}, bf16[2,2,2,512]{3,2,1,0:T(2,128)(2,1)S(1)}, bf16[2,32,2,512]{3,2,1,0:T(2,128)(2,1)S(1)}, bf16[2,2,3072]{2,1,0:T(2,128)(2,1)S(1)}) custom-call(s32[2]{0:T(128)} %refs_0_.1, bf16[2,2,3072]{2,1,0:T(2,128)(2,1)} %refs_1_.1, bf16[2,2,2,512]{3,2,1,0:T(2,128)(2,1)} %refs_2_.1, ...), custom_call_target="tpu_custom_call" | custom-call | tf_op jit(solution)/shard_map/fetch/pallas_call | solution.py:466
  1.7 0.3 pack.1
  1.9 3.1 %collective-permute-start = (bf16[192,128]{1,0:T(8,128)(2,1)S(1)}, bf16[192,128]{1,0:T(8,128)(2,1)S(1)}, u32[]{:S(2)}, u32[]{:S(2)}) collective-permute-start(bf16[192,128]{1,0:T(8,128)(2,1)S(1)} %get-tuple-element.33), channel_id=1, source_target_pairs={{0,4},{4,0},{8,12},{12,8},{1,5},{5,1},{9,13},{13,9},{2,6},{6,2},{1... | collective-permute-start | bytes 147464 | tf_op jit(solution)/shard_map/ppermute | solution.py:487
  5.0 2.6 %collective-permute-start.1 = (bf16[192,128]{1,0:T(8,128)(2,1)S(1)}, bf16[192,128]{1,0:T(8,128)(2,1)S(1)}, u32[]{:S(2)}, u32[]{:S(2)}) collective-permute-start(bf16[192,128]{1,0:T(8,128)(2,1)S(1)} %get-tuple-element.34), channel_id=1, source_target_pairs={{0,8},{4,12},{8,0},{12,4},{1,9},{5,13},{9,1},{13,5},{2,10},{6,14},... | collective-permute-start | bytes 147464 | tf_op jit(solution)/shard_map/ppermute | solution.py:487
  7.6 3.3 %collective-permute-done.1.refs_2_ = bf16[192,128]{1,0:T(8,128)(2,1)S(1)} collective-permute-done((bf16[192,128]{1,0:T(8,128)(2,1)S(1)}, bf16[192,128]{1,0:T(8,128)(2,1)S(1)}, u32[]{:S(2)}, u32[]{:S(2)}) %collective-permute-start.1) | collective-permute-done | bytes 49184 | tf_op jit(solution)/shard_map/ppermute | solution.py:487
  11.0 2.6 %collective-permute-done.2.refs_3_ = bf16[192,128]{1,0:T(8,128)(2,1)S(1)} collective-permute-done((bf16[192,128]{1,0:T(8,128)(2,1)S(1)}, bf16[192,128]{1,0:T(8,128)(2,1)S(1)}, u32[]{:S(2)}, u32[]{:S(2)}) %collective-permute-start.2) | collective-permute-done | bytes 49184 | tf_op jit(solution)/shard_map/ppermute | solution.py:487
  13.5 0.7 %attend.1 = (bf16[16,896]{1,0:T(8,128)(2,1)S(1)}, bf16[96,128]{1,0:T(8,128)(2,1)S(1)}) custom-call(bf16[192,128]{1,0:T(8,128)(2,1)S(1)} %get-tuple-element.32.refs_0_, bf16[192,128]{1,0:T(8,128)(2,1)S(1)} %collective-permute-done.refs_1_, bf16[192,128]{1,0:T(8,128)(2,1)S(1)} %collective-permute-done.1.refs_2_, ...), custom_call_target="tpu_custom_call" | custom-call | flops 1048576000 | bytes 1048576 | tf_op jit(solution)/shard_map/attend/pallas_call | solution.py:493
  14.2 1.5 %collective-permute-start.3 = (bf16[16,896]{1,0:T(8,128)(2,1)S(1)}, bf16[16,896]{1,0:T(8,128)(2,1)S(1)}, u32[]{:S(2)}, u32[]{:S(2)}) collective-permute-start(bf16[16,896]{1,0:T(8,128)(2,1)S(1)} %get-tuple-element.36.own_ref), channel_id=1, source_target_pairs={{0,2},{2,0},{1,3},{3,1},{4,6},{6,4},{5,7},{7,5},{8,10},{10,8},{9,1... | collective-permute-start | bytes 86024 | tf_op jit(solution)/shard_map/ppermute | solution.py:508
  15.7 2.4 %collective-permute-done.3.peer_ref = bf16[16,896]{1,0:T(8,128)(2,1)S(1)} collective-permute-done((bf16[16,896]{1,0:T(8,128)(2,1)S(1)}, bf16[16,896]{1,0:T(8,128)(2,1)S(1)}, u32[]{:S(2)}, u32[]{:S(2)}) %collective-permute-start.3) | collective-permute-done | bytes 28704 | tf_op jit(solution)/shard_map/ppermute | solution.py:508
  18.1 0.1 merge.1
  18.2 0.1 collective-permute-start.4
  18.2 1.3 %collective-permute-start.5 = (bf16[32,896]{1,0:T(8,128)(2,1)S(1)}, bf16[32,896]{1,0:T(8,128)(2,1)S(1)}, u32[]{:S(2)}, u32[]{:S(2)}) collective-permute-start(bf16[32,896]{1,0:T(8,128)(2,1)S(1)} %get-tuple-element.40), channel_id=1, source_target_pairs={{0,8},{4,12},{8,0},{12,4},{1,9},{5,13},{9,1},{13,5},{2,10},{6,14},... | collective-permute-start | bytes 172040 | tf_op jit(solution)/shard_map/ppermute | solution.py:487
  19.5 3.1 %collective-permute-start.6 = (bf16[32,896]{1,0:T(8,128)(2,1)S(1)}, bf16[32,896]{1,0:T(8,128)(2,1)S(1)}, u32[]{:S(2)}, u32[]{:S(2)}) collective-permute-start(bf16[32,896]{1,0:T(8,128)(2,1)S(1)} %get-tuple-element.41), channel_id=1, source_target_pairs={{0,12},{4,8},{8,4},{12,0},{1,13},{5,9},{9,5},{13,1},{2,14},{6,10},... | collective-permute-start | bytes 172040 | tf_op jit(solution)/shard_map/ppermute | solution.py:487
  22.6 0.6 %own_chunk.1 = (f32[32,1024]{1,0:T(8,128)S(1)}, f32[32,1024]{1,0:T(8,128)S(1)}) custom-call(bf16[32,896]{1,0:T(8,128)(2,1)S(1)} %get-tuple-element.38.x_ref.refs_0_, bf16[1,6144,1024]{2,1,0:T(8,128)(2,1)S(1)} %copy-done, bf16[1,6144,1024]{2,1,0:T(8,128)(2,1)S(1)} %copy-done.1), custom_call_target="tpu_custom_call" | custom-call | flops 41943040000 | bytes 41943040 | tf_op jit(solution)/shard_map/own_chunk/pallas_call | solution.py:519
  23.3 0.1 collective-permute-done.5.refs_2_
  23.4 2.1 %collective-permute-done.6.refs_3_ = bf16[32,896]{1,0:T(8,128)(2,1)S(1)} collective-permute-done((bf16[32,896]{1,0:T(8,128)(2,1)S(1)}, bf16[32,896]{1,0:T(8,128)(2,1)S(1)}, u32[]{:S(2)}, u32[]{:S(2)}) %collective-permute-start.6) | collective-permute-done | bytes 57376 | tf_op jit(solution)/shard_map/ppermute | solution.py:487
  25.5 0.1 collective-permute-start.7
  25.6 1.7 %first_half.1 = (f32[32,1024]{1,0:T(8,128)S(1)}, f32[32,1024]{1,0:T(8,128)S(1)}) custom-call(bf16[4,32,896]{2,1,0:T(8,128)(2,1)S(1)} %stack.1.x_ref.own_ref, f32[32,1024]{1,0:T(8,128)S(1)} %get-tuple-element.42.refs_4_.gate_in, f32[32,1024]{1,0:T(8,128)S(1)} %get-tuple-element.43.up_in, bf16[1,6144,1024]{2,1,0:T(8,128)(2,1)S(1)} %copy-done, ...), custom_call_target="tpu_custom_call" | custom-call | flops 1048576000 | bytes 1048576 | tf_op jit(solution)/shard_map/first_half/pallas_call | solution.py:530
  27.4 2.3 %second_half.1.hidden_ref = bf16[32,1024]{1,0:T(8,128)(2,1)S(1)} custom-call(bf16[4,32,896]{2,1,0:T(8,128)(2,1)S(1)} %collective-permute-done.7.x_ref, bf16[4,32,896]{2,1,0:T(8,128)(2,1)S(1)} %stack.1.x_ref.own_ref, f32[32,1024]{1,0:T(8,128)S(1)} %get-tuple-element.44.gate_in, f32[32,1024]{1,0:T(8,128)S(1)} %get-tuple-element.45.up_in, ...), custom_call_target="tpu_custom_call" | custom-call | flops 1048576000 | bytes 1048576 | tf_op jit(solution)/shard_map/second_half/pallas_call | solution.py:538
  29.7 0.5 %collective-permute-start.8 = (bf16[32,1024]{1,0:T(8,128)(2,1)S(1)}, bf16[32,1024]{1,0:T(8,128)(2,1)S(1)}, u32[]{:S(2)}, u32[]{:S(2)}) collective-permute-start(bf16[32,1024]{1,0:T(8,128)(2,1)S(1)} %second_half.1.hidden_ref), channel_id=1, source_target_pairs={{0,1},{1,0},{2,3},{3,2},{4,5},{5,4},{6,7},{7,6},{8,9},{9,8},{10,11... | collective-permute-start | bytes 196616 | tf_op jit(solution)/shard_map/ppermute | solution.py:546
  30.2 0.3 slice-done.2
  30.5 1.2 %down_first.1.own_ref = f32[32,3072]{1,0:T(8,128)S(1)} custom-call(bf16[32,1024]{1,0:T(8,128)(2,1)S(1)} %second_half.1.hidden_ref, bf16[1,2048,3072]{2,1,0:T(8,128)(2,1)S(1)} %bitcast.2), custom_call_target="tpu_custom_call" | custom-call | flops 6291456000 | bytes 6291456 | tf_op jit(solution)/shard_map/down_first/pallas_call | solution.py:547
  31.7 1.2 %down_second.1 = (bf16[8,3072]{1,0:T(8,128)(2,1)S(1)}, bf16[8,3072]{1,0:T(8,128)(2,1)S(1)}, bf16[8,3072]{1,0:T(8,128)(2,1)S(1)}, bf16[8,3072]{1,0:T(8,128)(2,1)S(1)}) custom-call(bf16[32,1024]{1,0:T(8,128)(2,1)S(1)} %collective-permute-done.8.hidden_ref, f32[32,3072]{1,0:T(8,128)S(1)} %down_first.1.own_ref, bf16[1,2048,3072]{2,1,0:T(8,128)(2,1)S(1)} %bitcast.2), custom_call_target="tpu_custom_call" | custom-call | flops 6291456000 | bytes 6291456 | tf_op jit(solution)/shard_map/down_second/pallas_call | solution.py:555
  32.9 0.1 collective-permute-start.9
  33.0 3.6 %collective-permute-start.10 = (bf16[8,3072]{1,0:T(8,128)(2,1)S(1)}, bf16[8,3072]{1,0:T(8,128)(2,1)S(1)}, u32[]{:S(2)}, u32[]{:S(2)}) collective-permute-start(bf16[8,3072]{1,0:T(8,128)(2,1)S(1)} %get-tuple-element.48), channel_id=1, source_target_pairs={{0,8},{4,12},{8,0},{12,4},{1,9},{5,13},{9,1},{13,5},{2,10},{6,14},... | collective-permute-start | bytes 147464 | tf_op jit(solution)/shard_map/ppermute | solution.py:487
  36.6 0.7 %collective-permute-start.11 = (bf16[8,3072]{1,0:T(8,128)(2,1)S(1)}, bf16[8,3072]{1,0:T(8,128)(2,1)S(1)}, u32[]{:S(2)}, u32[]{:S(2)}) collective-permute-start(bf16[8,3072]{1,0:T(8,128)(2,1)S(1)} %get-tuple-element.49), channel_id=1, source_target_pairs={{0,12},{4,8},{8,4},{12,0},{1,13},{5,9},{9,5},{13,1},{2,14},{6,10},... | collective-permute-start | bytes 147464 | tf_op jit(solution)/shard_map/ppermute | solution.py:487
  37.4 2.6 %collective-permute-done.10.refs_2_ = bf16[8,3072]{1,0:T(8,128)(2,1)S(1)} collective-permute-done((bf16[8,3072]{1,0:T(8,128)(2,1)S(1)}, bf16[8,3072]{1,0:T(8,128)(2,1)S(1)}, u32[]{:S(2)}, u32[]{:S(2)}) %collective-permute-start.10) | collective-permute-done | bytes 49184 | tf_op jit(solution)/shard_map/ppermute | solution.py:487
  40.0 2.5 %collective-permute-done.11.refs_3_ = bf16[8,3072]{1,0:T(8,128)(2,1)S(1)} collective-permute-done((bf16[8,3072]{1,0:T(8,128)(2,1)S(1)}, bf16[8,3072]{1,0:T(8,128)(2,1)S(1)}, u32[]{:S(2)}, u32[]{:S(2)}) %collective-permute-start.11) | collective-permute-done | bytes 49184 | tf_op jit(solution)/shard_map/ppermute | solution.py:487
  42.6 1.6 %collective-permute-start.12 = (bf16[4,3072]{1,0:T(4,128)(2,1)S(1)}, bf16[4,3072]{1,0:T(4,128)(2,1)S(1)}, u32[]{:S(2)}, u32[]{:S(2)}) collective-permute-start(bf16[4,3072]{1,0:T(4,128)(2,1)S(1)} %get-tuple-element.50._), channel_id=1, source_target_pairs={{0,2},{2,0},{1,3},{3,1},{4,6},{6,4},{5,7},{7,5},{8,10},{10,8},{9,1... | collective-permute-start | bytes 73736 | tf_op jit(solution)/shard_map/ppermute | solution.py:564
  44.1 0.6 %attn.1 = bf16[2,2,3072]{2,1,0:T(2,128)(2,1)} custom-call(bf16[4,32,896]{2,1,0:T(8,128)(2,1)S(1)} %stack.1.x_ref.own_ref, bf16[4,3072]{1,0:T(4,128)(2,1)S(1)} %get-tuple-element.50._), custom_call_target="tpu_custom_call" | custom-call | tf_op jit(solution)/shard_map/attn/pallas_call | solution.py:566
  44.8 1.7 %collective-permute-done.12.peer_ref = bf16[4,3072]{1,0:T(4,128)(2,1)S(1)} collective-permute-done((bf16[4,3072]{1,0:T(4,128)(2,1)S(1)}, bf16[4,3072]{1,0:T(4,128)(2,1)S(1)}, u32[]{:S(2)}, u32[]{:S(2)}) %collective-permute-start.12) | collective-permute-done | bytes 24608 | tf_op jit(solution)/shard_map/ppermute | solution.py:564
  46.5 1.2 %mix.1 = bf16[2,2,3072]{2,1,0:T(2,128)(2,1)} custom-call(s32[2,2,2]{2,1,0:T(2,128)S(1)} %copy-done.2, f32[2,2,2]{2,1,0:T(2,128)S(1)} %copy-done.3, bf16[4,3072]{1,0:T(4,128)(2,1)S(1)} %get-tuple-element.51.own_ref, bf16[4,3072]{1,0:T(4,128)(2,1)S(1)} %collective-permute-done.12.peer_ref), custom_call_target="tpu_custom_call" | custom-call | tf_op jit(solution)/shard_map/mix/pallas_call | solution.py:567
  (24 shorter events, 0.1 us)
Async XLA Ops:
  1.6 11.9 %copy-start.4 = (bf16[6144]{0:T(1024)(128)(2,1)S(1)}, bf16[6144]{0:T(1024)(128)(2,1)}, u32[]{:S(2)}) copy-start(bf16[6144]{0:T(1024)(128)(2,1)} %param.16) | copy-start | bytes 36868
  1.6 21.0 %copy-start = (bf16[1,6144,1024]{2,1,0:T(8,128)(2,1)S(1)}, bf16[1,6144,1024]{2,1,0:T(8,128)(2,1)}, u32[]{:S(2)}) copy-start(bf16[1,6144,1024]{2,1,0:T(8,128)(2,1)} %gate_w.5) | copy-start | bytes 37748740
  1.7 21.0 %copy-start.1 = (bf16[1,6144,1024]{2,1,0:T(8,128)(2,1)S(1)}, bf16[1,6144,1024]{2,1,0:T(8,128)(2,1)}, u32[]{:S(2)}) copy-start(bf16[1,6144,1024]{2,1,0:T(8,128)(2,1)} %up_w.5) | copy-start | bytes 37748740
  1.9 5.7 %collective-permute-start = (bf16[192,128]{1,0:T(8,128)(2,1)S(1)}, bf16[192,128]{1,0:T(8,128)(2,1)S(1)}, u32[]{:S(2)}, u32[]{:S(2)}) collective-permute-start(bf16[192,128]{1,0:T(8,128)(2,1)S(1)} %get-tuple-element.33), channel_id=1, source_target_pairs={{0,4},{4,0},{8,12},{12,8},{1,5},{5,1},{9,13},{13,9},{2,6},{6,2},{1... | collective-permute-start | bytes 147464 | tf_op jit(solution)/shard_map/ppermute | solution.py:487
  5.0 5.9 %collective-permute-start.1 = (bf16[192,128]{1,0:T(8,128)(2,1)S(1)}, bf16[192,128]{1,0:T(8,128)(2,1)S(1)}, u32[]{:S(2)}, u32[]{:S(2)}) collective-permute-start(bf16[192,128]{1,0:T(8,128)(2,1)S(1)} %get-tuple-element.34), channel_id=1, source_target_pairs={{0,8},{4,12},{8,0},{12,4},{1,9},{5,13},{9,1},{13,5},{2,10},{6,14},... | collective-permute-start | bytes 147464 | tf_op jit(solution)/shard_map/ppermute | solution.py:487
  7.6 5.9 %collective-permute-start.2 = (bf16[192,128]{1,0:T(8,128)(2,1)S(1)}, bf16[192,128]{1,0:T(8,128)(2,1)S(1)}, u32[]{:S(2)}, u32[]{:S(2)}) collective-permute-start(bf16[192,128]{1,0:T(8,128)(2,1)S(1)} %get-tuple-element.35), channel_id=1, source_target_pairs={{0,12},{4,8},{8,4},{12,0},{1,13},{5,9},{9,5},{13,1},{2,14},{6,10},... | collective-permute-start | bytes 147464 | tf_op jit(solution)/shard_map/ppermute | solution.py:487
  14.2 3.9 %collective-permute-start.3 = (bf16[16,896]{1,0:T(8,128)(2,1)S(1)}, bf16[16,896]{1,0:T(8,128)(2,1)S(1)}, u32[]{:S(2)}, u32[]{:S(2)}) collective-permute-start(bf16[16,896]{1,0:T(8,128)(2,1)S(1)} %get-tuple-element.36.own_ref), channel_id=1, source_target_pairs={{0,2},{2,0},{1,3},{3,1},{4,6},{6,4},{5,7},{7,5},{8,10},{10,8},{9,1... | collective-permute-start | bytes 86024 | tf_op jit(solution)/shard_map/ppermute | solution.py:508
  18.2 5.1 %collective-permute-start.4 = (bf16[32,896]{1,0:T(8,128)(2,1)S(1)}, bf16[32,896]{1,0:T(8,128)(2,1)S(1)}, u32[]{:S(2)}, u32[]{:S(2)}) collective-permute-start(bf16[32,896]{1,0:T(8,128)(2,1)S(1)} %get-tuple-element.39), channel_id=1, source_target_pairs={{0,4},{4,0},{8,12},{12,8},{1,5},{5,1},{9,13},{13,9},{2,6},{6,2},{1... | collective-permute-start | bytes 172040 | tf_op jit(solution)/shard_map/ppermute | solution.py:487
  18.2 5.1 %collective-permute-start.5 = (bf16[32,896]{1,0:T(8,128)(2,1)S(1)}, bf16[32,896]{1,0:T(8,128)(2,1)S(1)}, u32[]{:S(2)}, u32[]{:S(2)}) collective-permute-start(bf16[32,896]{1,0:T(8,128)(2,1)S(1)} %get-tuple-element.40), channel_id=1, source_target_pairs={{0,8},{4,12},{8,0},{12,4},{1,9},{5,13},{9,1},{13,5},{2,10},{6,14},... | collective-permute-start | bytes 172040 | tf_op jit(solution)/shard_map/ppermute | solution.py:487
  19.5 6.0 %collective-permute-start.6 = (bf16[32,896]{1,0:T(8,128)(2,1)S(1)}, bf16[32,896]{1,0:T(8,128)(2,1)S(1)}, u32[]{:S(2)}, u32[]{:S(2)}) collective-permute-start(bf16[32,896]{1,0:T(8,128)(2,1)S(1)} %get-tuple-element.41), channel_id=1, source_target_pairs={{0,12},{4,8},{8,4},{12,0},{1,13},{5,9},{9,5},{13,1},{2,14},{6,10},... | collective-permute-start | bytes 172040 | tf_op jit(solution)/shard_map/ppermute | solution.py:487
  25.5 1.8 %collective-permute-start.7 = (bf16[4,32,896]{2,1,0:T(8,128)(2,1)S(1)}, bf16[4,32,896]{2,1,0:T(8,128)(2,1)S(1)}, u32[]{:S(2)}, u32[]{:S(2)}) collective-permute-start(bf16[4,32,896]{2,1,0:T(8,128)(2,1)S(1)} %stack.1.x_ref.own_ref), channel_id=1, source_target_pairs={{0,1},{1,0},{2,3},{3,2},{4,5},{5,4},{6,7},{7,6},{8,9},{9,8},{10,11... | collective-permute-start | bytes 688136 | tf_op jit(solution)/shard_map/ppermute | solution.py:529
  25.6 4.6 %slice-start = ((s8[12582912]{0:T(1024)(128)(4,1)}), s8[4194304]{0:T(1024)(128)(4,1)S(1)}, s32[]{:S(2)}) async-start(s8[12582912]{0:T(1024)(128)(4,1)} %bitcast.1), calls=%async_computation | async-start | bytes 8388608
  25.6 4.6 %slice-start.1 = ((s8[12582912]{0:T(1024)(128)(4,1)}), s8[4194304]{0:T(1024)(128)(4,1)S(1)}, s32[]{:S(2)}) async-start(s8[12582912]{0:T(1024)(128)(4,1)} %bitcast.1), calls=%async_computation.1 | async-start | bytes 8388608
  27.4 3.1 %slice-start.2 = ((s8[12582912]{0:T(1024)(128)(4,1)}), s8[4194304]{0:T(1024)(128)(4,1)S(1)}, s32[]{:S(2)}) async-start(s8[12582912]{0:T(1024)(128)(4,1)} %bitcast.1), calls=%async_computation.2 | async-start | bytes 8388608
  29.7 2.0 %collective-permute-start.8 = (bf16[32,1024]{1,0:T(8,128)(2,1)S(1)}, bf16[32,1024]{1,0:T(8,128)(2,1)S(1)}, u32[]{:S(2)}, u32[]{:S(2)}) collective-permute-start(bf16[32,1024]{1,0:T(8,128)(2,1)S(1)} %second_half.1.hidden_ref), channel_id=1, source_target_pairs={{0,1},{1,0},{2,3},{3,2},{4,5},{5,4},{6,7},{7,6},{8,9},{9,8},{10,11... | collective-permute-start | bytes 196616 | tf_op jit(solution)/shard_map/ppermute | solution.py:546
  31.7 14.8 %copy-start.2 = (s32[2,2,2]{2,1,0:T(2,128)S(1)}, s32[2,2,2]{2,1,0:T(2,128)}, u32[]{:S(2)}) copy-start(s32[2,2,2]{2,1,0:T(2,128)} %routes_ref.1) | copy-start | bytes 100
  31.7 14.8 %copy-start.3 = (f32[2,2,2]{2,1,0:T(2,128)S(1)}, f32[2,2,2]{2,1,0:T(2,128)}, u32[]{:S(2)}) copy-start(f32[2,2,2]{2,1,0:T(2,128)} %gates_ref.1) | copy-start | bytes 100
  32.9 4.5 %collective-permute-start.9 = (bf16[8,3072]{1,0:T(8,128)(2,1)S(1)}, bf16[8,3072]{1,0:T(8,128)(2,1)S(1)}, u32[]{:S(2)}, u32[]{:S(2)}) collective-permute-start(bf16[8,3072]{1,0:T(8,128)(2,1)S(1)} %get-tuple-element.47), channel_id=1, source_target_pairs={{0,4},{4,0},{8,12},{12,8},{1,5},{5,1},{9,13},{13,9},{2,6},{6,2},{1... | collective-permute-start | bytes 147464 | tf_op jit(solution)/shard_map/ppermute | solution.py:487
  33.0 7.0 %collective-permute-start.10 = (bf16[8,3072]{1,0:T(8,128)(2,1)S(1)}, bf16[8,3072]{1,0:T(8,128)(2,1)S(1)}, u32[]{:S(2)}, u32[]{:S(2)}) collective-permute-start(bf16[8,3072]{1,0:T(8,128)(2,1)S(1)} %get-tuple-element.48), channel_id=1, source_target_pairs={{0,8},{4,12},{8,0},{12,4},{1,9},{5,13},{9,1},{13,5},{2,10},{6,14},... | collective-permute-start | bytes 147464 | tf_op jit(solution)/shard_map/ppermute | solution.py:487
  36.6 5.9 %collective-permute-start.11 = (bf16[8,3072]{1,0:T(8,128)(2,1)S(1)}, bf16[8,3072]{1,0:T(8,128)(2,1)S(1)}, u32[]{:S(2)}, u32[]{:S(2)}) collective-permute-start(bf16[8,3072]{1,0:T(8,128)(2,1)S(1)} %get-tuple-element.49), channel_id=1, source_target_pairs={{0,12},{4,8},{8,4},{12,0},{1,13},{5,9},{9,5},{13,1},{2,14},{6,10},... | collective-permute-start | bytes 147464 | tf_op jit(solution)/shard_map/ppermute | solution.py:487
  42.6 3.9 %collective-permute-start.12 = (bf16[4,3072]{1,0:T(4,128)(2,1)S(1)}, bf16[4,3072]{1,0:T(4,128)(2,1)S(1)}, u32[]{:S(2)}, u32[]{:S(2)}) collective-permute-start(bf16[4,3072]{1,0:T(4,128)(2,1)S(1)} %get-tuple-element.50._), channel_id=1, source_target_pairs={{0,2},{2,0},{1,3},{3,1},{4,6},{6,4},{5,7},{7,5},{8,10},{10,8},{9,1... | collective-permute-start | bytes 73736 | tf_op jit(solution)/shard_map/ppermute | solution.py:564

commit v7 on v6

--- a/solution.py
+++ b/solution.py
@@ -6,6 +6,7 @@
 from jax.experimental import pallas as pl
 from jax.experimental.pallas import tpu as pltpu
 from jax.sharding import PartitionSpec as P
+
 
 HEADS = 48
 KV_HEADS = 8
@@ -22,6 +23,7 @@
 FIRST_LIMIT = 4 * MIB
 SECOND_LIMIT = 4 * MIB
 DOWN_LIMIT = 4 * MIB
+DOWN_COVER = MIB // 8
 ATTEND_COVER = MIB
 MERGE_COVER = MIB
 
@@ -136,7 +138,7 @@
     return (attn_out, moe_out)
 
 
-def call(body, outs, in_spaces, name, scratch=(), limit=4 * MIB, cost=None):
+def call(body, outs, in_spaces, scratch=(), limit=4 * MIB, cost=None):
     spaces = {"v": VMEM, "s": pltpu.SMEM, "a": pl.ANY}
     single = not isinstance(outs, (list, tuple))
     shapes = [outs] if single else list(outs)
@@ -149,14 +151,12 @@
         scratch_shapes=list(scratch),
         compiler_params=pltpu.CompilerParams(vmem_limit_bytes=limit),
         cost_estimate=cost,
-        name=name,
     )
 
 
 class Plan:
-    def __init__(self, queries, new_kv, prefix_kv):
+    def __init__(self, queries, prefix_kv):
         self.steps, self.conts, self.half = queries.shape
-        self.kv_local = new_kv.shape[-1] // HEAD_DIM
         self.prompts, self.positions = prefix_kv.shape[:2]
         self.tokens = self.steps * self.conts
         self.block = self.prompts * self.positions * 2
@@ -167,24 +167,38 @@
         self.rows = -(-(self.prompt + self.tokens) // 16) * 16
 
 
-def fetch_body(plan, *refs):
-    count = (len(refs) - 2) // 2
-    sources, targets, (prompts, sems) = refs[:count], refs[count : 2 * count], refs[2 * count :]
+def fetch_body(plan, experts, *refs):
+    f32, bf16 = jnp.float32, jnp.bfloat16
+    sources, targets, scalars, sems = refs[:7], refs[7:12], refs[12:15], refs[15]
     copies = [
         pltpu.make_async_copy(source, target, sems.at[i])
-        for i, (source, target) in enumerate(zip(sources, (prompts,) + targets[1:]))
+        for i, (source, target) in enumerate(zip(sources, scalars + targets[1:]))
     ]
     for copy in copies:
         copy.start()
     for copy in copies:
         copy.wait()
-    c = plan.conts
+    prompts, routes, gates = scalars
     base = lax.axis_index("experts") * plan.prompts
-    row = lax.broadcasted_iota(jnp.int32, (c, HEAD_DIM), 0)
-    local = jnp.zeros((c, HEAD_DIM), jnp.float32)
-    for i in range(c):
-        local = jnp.where(row == i, (prompts[i] - base).astype(jnp.float32), local)
-    targets[0][...] = local.astype(jnp.bfloat16)
+    shape = (plan.tokens, HEAD_DIM)
+    row = lax.broadcasted_iota(jnp.int32, shape, 0)
+    lane = lax.broadcasted_iota(jnp.int32, shape, 1)
+    value = jnp.zeros(shape, f32)
+    for s in range(plan.steps):
+        for c in range(plan.conts):
+            here = row == s * plan.conts + c
+            value = jnp.where(here & (lane == 0), (prompts[c] - base).astype(f32), value)
+            for e in range(experts):
+                amount = f32(0.0)
+                for k in range(routes.shape[2]):
+                    amount = amount + jnp.where(routes[s, c, k] == e, gates[s, c, k], 0.0)
+                value = jnp.where(here & ((lane + 2) // 3 == e + 1), amount, value)
+    high = value.astype(bf16).astype(f32)
+    middle = (value - high).astype(bf16).astype(f32)
+    low = value - high - middle
+    which = (lane + 2) % 3
+    parts = jnp.where(lane == 0, high, jnp.where(which == 0, high, jnp.where(which == 1, middle, low)))
+    targets[0][...] = parts.astype(bf16)
 
 
 def pack_body(plan, local_ref, q_ref, new_ref, prefix_ref, resid_ref, *outs):
@@ -203,11 +217,12 @@
                 head = pl.ds(pl.multiple_of((h * GROUP + g) * HEAD_DIM, HEAD_DIM), HEAD_DIM)
                 out_ref[pl.ds(plan.query + g * t + s * c, c), :] = q_ref[s, :, head]
                 out_ref[pl.ds(plan.resid + g * t + s * c, c), :] = resid_ref[s, :, head]
-            out_ref[pl.ds(plan.prompt + s * c, c), :] = local_ref[...]
+        out_ref[pl.ds(plan.prompt, t), :] = local_ref[...]
 
 
 def attend_body(plan, rows, *refs):
-    pieces, (gain_ref, x_ref, attn_ref, q_s, r_s, kv_s, p_s, gain_s) = refs[:rows], refs[rows:]
+    pieces = refs[:rows]
+    gain_ref, x_ref, attn_ref, share_ref, q_s, r_s, kv_s, p_s, gain_s = refs[rows:]
     t, c = plan.tokens, plan.conts
     total = rows * t
     f32 = jnp.float32
@@ -236,7 +251,13 @@
     shape = scores.shape
     row = lax.broadcasted_iota(jnp.int32, shape, 0) % total
     col = lax.broadcasted_iota(jnp.int32, shape, 1)
-    prompt = p_s[...].astype(f32)[:, :1]
+    local = p_s[...].astype(f32)
+    lane = lax.broadcasted_iota(jnp.int32, local.shape, 1)
+    expert = lax.axis_index("experts")
+    for i in range(share_ref.shape[0]):
+        part = jnp.where((lane > 0) & ((lane + 2) // 3 == (expert ^ i) + 1), local, 0.0)
+        share_ref[i] = jnp.broadcast_to(jnp.sum(part, axis=1, keepdims=True), local.shape)
+    prompt = local[:, :1]
     prompt = jnp.concatenate([prompt] * GROUP, axis=0).astype(jnp.int32)
     in_prefix = (col < rows * plan.block) & ((col % plan.block) // (2 * plan.positions) == prompt)
     late = col - rows * plan.block
@@ -363,42 +384,56 @@
     hidden_ref[...] = (gate / (1.0 + jnp.exp(-gate)) * up).astype(jnp.bfloat16)
 
 
-def down_product(side, hidden_ref, down_w):
+def down_product(side, hidden_ref, down_w, lanes):
     depth = hidden_ref.shape[1]
     core = lax.axis_index("heads")
     first = pl.multiple_of((1 - core if side else core) * depth, depth)
     return jnp.dot(
-        hidden_ref[...], down_w[0, pl.ds(first, depth)], preferred_element_type=jnp.float32
+        hidden_ref[...], down_w[0, pl.ds(first, depth), lanes], preferred_element_type=jnp.float32
     )
 
 
 def down_first_body(hidden_ref, down_w, out_ref):
-    out_ref[...] = down_product(0, hidden_ref, down_w)
-
-
-def down_second_body(plan, rows, hidden_ref, own_ref, down_w, *outs):
-    result = own_ref[...] + down_product(1, hidden_ref, down_w)
+    out_ref[...] = down_product(0, hidden_ref, down_w, slice(None))
+
+
+def down_second_body(part, hidden_ref, first_ref, down_w, _, own_ref, peer_ref):
+    total, width = own_ref.shape
+    lanes = pl.ds(part * width, width)
+    result = first_ref[:, lanes] + down_product(1, hidden_ref, down_w, lanes)
+    own_ref[...] = result[:total]
+    peer_ref[...] = result[total:].astype(jnp.bfloat16)
+
+
+def blend_body(plan, rows, share_ref, *refs):
+    parts = (len(refs) - rows) // 2
+    owns, peers, outs = refs[:parts], refs[parts : 2 * parts], refs[2 * parts :]
     t = plan.tokens
-    total = rows * t
+    own_share, peer_share = share_ref[0][:, :1], share_ref[1][:, :1]
+    mixed = [
+        own_share * own_ref[...] + peer_share * peer_ref[...].astype(jnp.float32)
+        for own_ref, peer_ref in zip(owns, peers)
+    ]
+    width = mixed[0].shape[1]
 
     def place(own):
         for k, out_ref in enumerate(outs):
             first = (own ^ k) * t
-            pair = [result[i : i + t] for i in (first, first + total)]
-            out_ref[...] = jnp.concatenate(pair, axis=0).astype(jnp.bfloat16)
+            for i, part in enumerate(mixed):
+                out_ref[:, pl.ds(i * width, width)] = part[first : first + t].astype(jnp.bfloat16)
 
     for own in range(rows):
         pl.when(lax.axis_index("rows") == own)(functools.partial(place, own))
 
 
-def sum_body(*refs):
-    *pieces, own_ref, peer_ref = refs
+def total_body(plan, *refs):
+    *pieces, moe_ref = refs
     total = pieces[0][...].astype(jnp.float32)
     for ref in pieces[1:]:
         total = total + ref[...].astype(jnp.float32)
-    t = own_ref.shape[0]
-    own_ref[...] = total[:t].astype(jnp.bfloat16)
-    peer_ref[...] = total[t:].astype(jnp.bfloat16)
+    total = total.astype(jnp.bfloat16)
+    for s in range(plan.steps):
+        moe_ref[s] = total[s * plan.conts : (s + 1) * plan.conts]
 
 
 def attn_body(plan, rows, own_ref, _, attn_ref):
@@ -412,26 +447,6 @@
                 attn_ref[s, :, lanes] = own_ref[
                     k, pl.ds(g * t + s * plan.conts, plan.conts), pl.ds(depth, HEAD_DIM)
                 ]
-
-
-def mix_body(plan, routes_ref, gates_ref, own_ref, peer_ref, moe_ref):
-    own = lax.axis_index("experts")
-    row = lax.broadcasted_iota(jnp.int32, (plan.tokens, 1), 0)
-    mixture = None
-    for expert, ref in ((own, own_ref), (1 - own, peer_ref)):
-        share = jnp.zeros((plan.tokens, 1), jnp.float32)
-        for s in range(plan.steps):
-            for c in range(plan.conts):
-                amount = jnp.float32(0.0)
-                for k in range(routes_ref.shape[2]):
-                    chosen = routes_ref[s, c, k] == expert
-                    amount = amount + jnp.where(chosen, gates_ref[s, c, k], 0.0)
-                share = jnp.where(row == s * plan.conts + c, amount, share)
-        part = share * ref[...].astype(jnp.float32)
-        mixture = part if mixture is None else mixture + part
-    mixture = mixture.astype(jnp.bfloat16)
-    for s in range(plan.steps):
-        moe_ref[s] = mixture[s * plan.conts : (s + 1) * plan.conts]
 
 
 def per_device(
@@ -448,7 +463,7 @@
     route_gates,
 ):
     rows, experts = lax.axis_size("rows"), lax.axis_size("experts")
-    plan = Plan(queries, new_kv, prefix_kv)
+    plan = Plan(queries, prefix_kv)
     bf16, f32 = jnp.bfloat16, jnp.float32
     shape = jax.ShapeDtypeStruct
     piece = GROUP * HEAD_DIM
@@ -462,23 +477,19 @@
     def cover(size):
         return pl.CostEstimate(flops=FLOPS * size, bytes_accessed=size, transcendentals=0)
 
-    sources = (cont_prompt, queries, new_kv, prefix_kv, resid)
+    scalars = (cont_prompt, routes, route_gates)
+    arrays = (queries, new_kv, prefix_kv, resid)
     fetched = call(
-        functools.partial(fetch_body, plan),
-        (VMEM((plan.conts, HEAD_DIM), bf16),)
-        + tuple(VMEM(source.shape, bf16) for source in sources[1:]),
-        "aaaaa",
-        "fetch",
-        scratch=(
-            pltpu.SMEM(cont_prompt.shape, jnp.int32),
-            pltpu.SemaphoreType.DMA((len(sources),)),
-        ),
-    )(*map(hbm, sources))
+        functools.partial(fetch_body, plan, experts),
+        (VMEM((plan.tokens, HEAD_DIM), bf16),) + tuple(VMEM(a.shape, bf16) for a in arrays),
+        "a" * (len(scalars) + len(arrays)),
+        scratch=tuple(pltpu.SMEM(a.shape, a.dtype) for a in scalars)
+        + (pltpu.SemaphoreType.DMA((len(scalars) + len(arrays),)),),
+    )(*map(hbm, scalars + arrays))
     packed = call(
         functools.partial(pack_body, plan),
         (shape((plan.rows, HEAD_DIM), bf16),) * rows,
         "vvvvv",
-        "pack",
         cost=cover(PACK_COVER),
     )(*map(vmem, fetched))
 
@@ -490,11 +501,14 @@
 
     keys = -(-(rows * (plan.block + 2 * plan.tokens)) // 128) * 128
     lanes = piece + HEAD_DIM
-    x, attn = call(
+    x, attn, share = call(
         functools.partial(attend_body, plan, rows),
-        (shape((total, lanes), bf16), shape((GROUP * total, HEAD_DIM), bf16)),
+        (
+            shape((total, lanes), bf16),
+            shape((GROUP * total, HEAD_DIM), bf16),
+            shape((experts, total, HEAD_DIM), f32),
+        ),
         "v" * (rows + 1),
-        "attend",
         scratch=(
             VMEM((GROUP * total, HEAD_DIM), bf16),
             VMEM((GROUP * total, HEAD_DIM), bf16),
@@ -510,28 +524,20 @@
         functools.partial(merge_body, plan, rows),
         (shape((tokens, lanes), bf16),) * rows,
         "vvv",
-        "merge",
         cost=cover(MERGE_COVER),
     )(x, peer, attn)
     chunks = spread(merged)
     units = w_gate.shape[2]
     products_of = shape((tokens, units), f32)
     gate, up = call(
-        own_chunk_body,
-        (products_of, products_of),
-        "vvv",
-        "own_chunk",
-        cost=cover(OWN_COVER),
+        own_chunk_body, (products_of, products_of), "vvv", cost=cover(OWN_COVER)
     )(merged[0], gate_w, up_w)
-    own = call(stack_body, shape((rows, tokens, lanes), bf16), "v" * (rows + 1), "stack")(
-        *chunks, gate
-    )
+    own = call(stack_body, shape((rows, tokens, lanes), bf16), "v" * (rows + 1))(*chunks, gate)
     other = lax.ppermute(own, "heads", swap)
     gate, up = call(
         first_half_body,
         (products_of, products_of),
         "vvvvv",
-        "first_half",
         limit=FIRST_LIMIT,
         cost=cover(FIRST_COVER),
     )(own, gate, up, gate_w, up_w)
@@ -539,7 +545,6 @@
         functools.partial(second_half_body, plan),
         shape((tokens, units), bf16),
         "vvvvvv",
-        "second_half",
         limit=SECOND_LIMIT,
         cost=cover(SECOND_COVER),
     )(other, own, gate, up, gate_w, up_w)
@@ -548,25 +553,30 @@
         down_first_body,
         shape((tokens, plan.half), f32),
         "vv",
-        "down_first",
         limit=DOWN_LIMIT,
-        cost=cover(2 * plan.half * units),
+        cost=cover(DOWN_COVER),
     )(hidden, down_w)
-    blocks = call(
-        functools.partial(down_second_body, plan, rows),
-        (shape((experts * plan.tokens, plan.half), bf16),) * rows,
-        "vvv",
-        "down_second",
-        cost=cover(2 * plan.half * units),
-    )(other_hidden, partial, down_w)
-    output = shape((plan.tokens, plan.half), bf16)
-    mine, theirs = call(sum_body, (output, output), "v" * rows, "sum")(*spread(blocks))
-    returned = lax.ppermute(theirs, "experts", swap)
+    parts = 2
+    width = plan.half // parts
+    owns, peers, back = [], [], []
+    for part in range(parts):
+        own_part, peer_part = call(
+            functools.partial(down_second_body, part),
+            (shape((total, width), f32), shape((total, width), bf16)),
+            "vvvv",
+            cost=cover(DOWN_COVER),
+        )(other_hidden, partial, down_w, peers[-1] if peers else share)
+        owns.append(own_part)
+        peers.append(peer_part)
+        back.append(lax.ppermute(peer_part, "experts", swap))
     out = shape(queries.shape, bf16)
-    attn_out = call(functools.partial(attn_body, plan, rows), out, "vv", "attn")(own, theirs)
-    moe_out = call(functools.partial(mix_body, plan), out, "ssvv", "mix")(
-        routes, route_gates, mine, returned
-    )
+    attn_out = call(functools.partial(attn_body, plan, rows), out, "vv")(own, peers[-1])
+    blended = call(
+        functools.partial(blend_body, plan, rows),
+        (shape((plan.tokens, plan.half), bf16),) * rows,
+        "v" * (1 + 2 * parts),
+    )(share, *owns, *back)
+    moe_out = call(functools.partial(total_body, plan), out, "v" * rows)(*spread(blended))
     return (attn_out, moe_out)
 
 

time: 47.9 us -> 48.9 us (1.021)
  local copies, waits for them, and re-layouts: 0.33 us -> 1.23 us
    ppermute x1 -> x2, waiting for transfers between devices: 1.7 us -> 3.55 us  [per_device(): back.append(lax.ppermute(peer_part, 'experts', swap))]
    ppermute x9, waiting for transfers between devices: 13.3 us -> 11.9 us  [spread(): lax.ppermute(pieces[k], 'rows', [(i, i ^ k) for i in range(rows)])]
    unnamed x16 -> x18, local copies, waits for them, and re-layouts: 0.33 us -> 1.23 us
    ppermute x1 -> x2, starting transfers between devices: 1.56 us -> 2.04 us  [per_device(): back.append(lax.ppermute(peer_part, 'experts', swap))]
    pallas_call x9 -> x10, Pallas kernels: 7.69 us -> 7.28 us  [the longest x1 1.7 us: per_device(): call(first_half_body, (products_of, products_of), 'vvvvv', limit=FIRST_LI...]
  transfers between devices with their start and end apart: 13 -> 14, of which waited for: 8 -> 8; matrix products, arithmetic and copies ran while one was open for 0% -> 0% of each run, Pallas kernels for 9% -> 9%
where the time goes in v7:
time: 48.9 us; the launch traced here: 48.8 us
  starting transfers between devices  18.3 us (37%)
  waiting for transfers between devices  17.8 us (36%)
  Pallas kernels  10.6 us (22%)
  local copies, waits for them, and re-layouts  1.23 us (3%)
  between operations  0.78 us (2%)
    ppermute x9, starting transfers between devices, spread(): lax.ppermute(pieces[k], 'rows', [(i, i ^ k) for i in range(rows)])  14.6 us
    ppermute x9, waiting for transfers between devices, spread(): lax.ppermute(pieces[k], 'rows', [(i, i ^ k) for i in range(rows)])  11.9 us
    ppermute x2, waiting for transfers between devices, per_device(): back.append(lax.ppermute(peer_part, 'experts', swap))  3.55 us
    ppermute x1, waiting for transfers between devices, per_device(): peer = lax.ppermute(x, 'experts', swap)  2.38 us
    pallas_call x1, Pallas kernels, per_device(): call(functools.partial(second_half_body, plan), shape((tokens, units), bf...  2.29 us
    ppermute x2, starting transfers between devices, per_device(): back.append(lax.ppermute(peer_part, 'experts', swap))  2.04 us
    pallas_call x1, Pallas kernels, per_device(): call(first_half_body, (products_of, products_of), 'vvvvv', limit=FIRST_LI...  1.7 us
    ppermute x1, starting transfers between devices, per_device(): peer = lax.ppermute(x, 'experts', swap)  1.5 us
  transfers between devices with their start and end apart: 14, of which 8 were waited for; matrix products, arithmetic and copies ran while one was open for 0% of the time, Pallas kernels for 9%

profile of v7, /device:TPU:0, one launch (start us, length us, event | category | flops | bytes accessed | tf_op | source)
XLA Modules:
  0.0 48.8 jit_solution(17116954992241167745)
XLA Ops:
  0.6 1.0 %shard_map.122 = (bf16[4,128]{1,0:T(4,128)(2,1)S(1)}, bf16[2,2,3072]{2,1,0:T(2,128)(2,1)S(1)}, bf16[2,2,2,512]{3,2,1,0:T(2,128)(2,1)S(1)}, bf16[2,32,2,512]{3,2,1,0:T(2,128)(2,1)S(1)}, bf16[2,2,3072]{2,1,0:T(2,128)(2,1)S(1)}) custom-call(s32[2]{0:T(128)} %refs_0_.1, s32[2,2,2]{2,1,0:T(2,128)} %refs_1_.1, f32[2,2,2]{2,1,0:T(2,128)} %refs_2_.1, ...), custom_call_target="tpu_custom_call" | custom-call | tf_op jit(solution)/shard_map/pallas_call | solution.py:482
  1.7 0.3 shard_map.123
  2.0 3.1 %collective-permute-start = (bf16[192,128]{1,0:T(8,128)(2,1)S(1)}, bf16[192,128]{1,0:T(8,128)(2,1)S(1)}, u32[]{:S(2)}, u32[]{:S(2)}) collective-permute-start(bf16[192,128]{1,0:T(8,128)(2,1)S(1)} %get-tuple-element.36), channel_id=1, source_target_pairs={{0,4},{4,0},{8,12},{12,8},{1,5},{5,1},{9,13},{13,9},{2,6},{6,2},{1... | collective-permute-start | bytes 147464 | tf_op jit(solution)/shard_map/ppermute | solution.py:498
  5.1 2.6 %collective-permute-start.1 = (bf16[192,128]{1,0:T(8,128)(2,1)S(1)}, bf16[192,128]{1,0:T(8,128)(2,1)S(1)}, u32[]{:S(2)}, u32[]{:S(2)}) collective-permute-start(bf16[192,128]{1,0:T(8,128)(2,1)S(1)} %get-tuple-element.37), channel_id=1, source_target_pairs={{0,8},{4,12},{8,0},{12,4},{1,9},{5,13},{9,1},{13,5},{2,10},{6,14},... | collective-permute-start | bytes 147464 | tf_op jit(solution)/shard_map/ppermute | solution.py:498
  7.7 3.3 %collective-permute-done.1.refs_2_ = bf16[192,128]{1,0:T(8,128)(2,1)S(1)} collective-permute-done((bf16[192,128]{1,0:T(8,128)(2,1)S(1)}, bf16[192,128]{1,0:T(8,128)(2,1)S(1)}, u32[]{:S(2)}, u32[]{:S(2)}) %collective-permute-start.1) | collective-permute-done | bytes 49184 | tf_op jit(solution)/shard_map/ppermute | solution.py:498
  11.0 2.6 %collective-permute-done.2.refs_3_ = bf16[192,128]{1,0:T(8,128)(2,1)S(1)} collective-permute-done((bf16[192,128]{1,0:T(8,128)(2,1)S(1)}, bf16[192,128]{1,0:T(8,128)(2,1)S(1)}, u32[]{:S(2)}, u32[]{:S(2)}) %collective-permute-start.2) | collective-permute-done | bytes 49184 | tf_op jit(solution)/shard_map/ppermute | solution.py:498
  13.6 0.7 %shard_map.124 = (bf16[16,896]{1,0:T(8,128)(2,1)S(1)}, bf16[96,128]{1,0:T(8,128)(2,1)S(1)}, f32[2,16,128]{2,1,0:T(8,128)S(1)}) custom-call(bf16[192,128]{1,0:T(8,128)(2,1)S(1)} %get-tuple-element.35.refs_0_, bf16[192,128]{1,0:T(8,128)(2,1)S(1)} %collective-permute-done.refs_1_, bf16[192,128]{1,0:T(8,128)(2,1)S(1)} %collective-permute-done.1.refs_2_, ...), custom_call_target="tpu_custom_call" | custom-call | flops 1048576000 | bytes 1048576 | tf_op jit(solution)/shard_map/pallas_call | solution.py:504
  14.2 1.5 %collective-permute-start.3 = (bf16[16,896]{1,0:T(8,128)(2,1)S(1)}, bf16[16,896]{1,0:T(8,128)(2,1)S(1)}, u32[]{:S(2)}, u32[]{:S(2)}) collective-permute-start(bf16[16,896]{1,0:T(8,128)(2,1)S(1)} %get-tuple-element.39.own_ref), channel_id=1, source_target_pairs={{0,2},{2,0},{1,3},{3,1},{4,6},{6,4},{5,7},{7,5},{8,10},{10,8},{9,1... | collective-permute-start | bytes 86024 | tf_op jit(solution)/shard_map/ppermute | solution.py:522
  15.7 2.4 %collective-permute-done.3.peer_ref = bf16[16,896]{1,0:T(8,128)(2,1)S(1)} collective-permute-done((bf16[16,896]{1,0:T(8,128)(2,1)S(1)}, bf16[16,896]{1,0:T(8,128)(2,1)S(1)}, u32[]{:S(2)}, u32[]{:S(2)}) %collective-permute-start.3) | collective-permute-done | bytes 28704 | tf_op jit(solution)/shard_map/ppermute | solution.py:522
  18.3 1.3 %collective-permute-start.5 = (bf16[32,896]{1,0:T(8,128)(2,1)S(1)}, bf16[32,896]{1,0:T(8,128)(2,1)S(1)}, u32[]{:S(2)}, u32[]{:S(2)}) collective-permute-start(bf16[32,896]{1,0:T(8,128)(2,1)S(1)} %get-tuple-element.43), channel_id=1, source_target_pairs={{0,8},{4,12},{8,0},{12,4},{1,9},{5,13},{9,1},{13,5},{2,10},{6,14},... | collective-permute-start | bytes 172040 | tf_op jit(solution)/shard_map/ppermute | solution.py:498
  19.6 3.1 %collective-permute-start.6 = (bf16[32,896]{1,0:T(8,128)(2,1)S(1)}, bf16[32,896]{1,0:T(8,128)(2,1)S(1)}, u32[]{:S(2)}, u32[]{:S(2)}) collective-permute-start(bf16[32,896]{1,0:T(8,128)(2,1)S(1)} %get-tuple-element.44), channel_id=1, source_target_pairs={{0,12},{4,8},{8,4},{12,0},{1,13},{5,9},{9,5},{13,1},{2,14},{6,10},... | collective-permute-start | bytes 172040 | tf_op jit(solution)/shard_map/ppermute | solution.py:498
  22.7 0.7 %shard_map.126 = (f32[32,1024]{1,0:T(8,128)S(1)}, f32[32,1024]{1,0:T(8,128)S(1)}) custom-call(bf16[32,896]{1,0:T(8,128)(2,1)S(1)} %get-tuple-element.41.x_ref.refs_0_, bf16[1,6144,1024]{2,1,0:T(8,128)(2,1)S(1)} %copy-done, bf16[1,6144,1024]{2,1,0:T(8,128)(2,1)S(1)} %copy-done.1), custom_call_target="tpu_custom_call" | custom-call | flops 41943040000 | bytes 41943040 | tf_op jit(solution)/shard_map/pallas_call | solution.py:532
  23.3 0.1 collective-permute-done.5.refs_2_
  23.4 2.1 %collective-permute-done.6.refs_3_ = bf16[32,896]{1,0:T(8,128)(2,1)S(1)} collective-permute-done((bf16[32,896]{1,0:T(8,128)(2,1)S(1)}, bf16[32,896]{1,0:T(8,128)(2,1)S(1)}, u32[]{:S(2)}, u32[]{:S(2)}) %collective-permute-start.6) | collective-permute-done | bytes 57376 | tf_op jit(solution)/shard_map/ppermute | solution.py:498
  25.7 0.5 slice-done.5
  26.2 1.7 %shard_map.128 = (f32[32,1024]{1,0:T(8,128)S(1)}, f32[32,1024]{1,0:T(8,128)S(1)}) custom-call(bf16[4,32,896]{2,1,0:T(8,128)(2,1)S(1)} %shard_map.127.x_ref.own_ref, f32[32,1024]{1,0:T(8,128)S(1)} %get-tuple-element.45.refs_4_.gate_in, f32[32,1024]{1,0:T(8,128)S(1)} %get-tuple-element.46.up_in, bf16[1,6144,1024]{2,1,0:T(8,128)(2,1)S(1)} %copy-done, ...), custom_call_target="tpu_custom_call" | custom-call | flops 1048576000 | bytes 1048576 | tf_op jit(solution)/shard_map/pallas_call | solution.py:537
  27.9 2.3 %shard_map.129.hidden_ref = bf16[32,1024]{1,0:T(8,128)(2,1)S(1)} custom-call(bf16[4,32,896]{2,1,0:T(8,128)(2,1)S(1)} %collective-permute-done.7.x_ref, bf16[4,32,896]{2,1,0:T(8,128)(2,1)S(1)} %shard_map.127.x_ref.own_ref, f32[32,1024]{1,0:T(8,128)S(1)} %get-tuple-element.47.gate_in, f32[32,1024]{1,0:T(8,128)S(1)} %get-tuple-element.48.up_in, ...), custom_call_target="tpu_custom_call" | custom-call | flops 1048576000 | bytes 1048576 | tf_op jit(solution)/shard_map/pallas_call | solution.py:544
  30.2 0.1 collective-permute-start.8
  30.3 0.7 %slice-done.2 = s8[4194304]{0:T(1024)(128)(4,1)S(1)} async-done(((s8[12582912]{0:T(1024)(128)(4,1)}), s8[4194304]{0:T(1024)(128)(4,1)S(1)}, s32[]{:S(2)}) %slice-start.2) | async-done | bytes 4194328
  31.0 1.2 %shard_map.130.first_ref = f32[32,3072]{1,0:T(8,128)S(1)} custom-call(bf16[32,1024]{1,0:T(8,128)(2,1)S(1)} %shard_map.129.hidden_ref, bf16[1,2048,3072]{2,1,0:T(8,128)(2,1)S(1)} %bitcast.2), custom_call_target="tpu_custom_call" | custom-call | flops 131072000 | bytes 131072 | tf_op jit(solution)/shard_map/pallas_call | solution.py:552
  32.2 0.7 %shard_map.131 = (f32[16,1536]{1,0:T(8,128)S(1)}, bf16[16,1536]{1,0:T(8,128)(2,1)S(1)}) custom-call(bf16[32,1024]{1,0:T(8,128)(2,1)S(1)} %collective-permute-done.8.hidden_ref, f32[32,3072]{1,0:T(8,128)S(1)} %shard_map.130.first_ref, bf16[1,2048,3072]{2,1,0:T(8,128)(2,1)S(1)} %bitcast.2, f32[2,16,128]{2,1,0:T(8,128)S(1)} %get-tuple-element.49._.share_ref), custom_call_target="tpu_custom_call" | custom-call | flops 131072000 | bytes 131072 | tf_op jit(solution)/shard_map/pallas_call | solution.py:563
  32.9 0.7 %shard_map.132 = (f32[16,1536]{1,0:T(8,128)S(1)}, bf16[16,1536]{1,0:T(8,128)(2,1)S(1)}) custom-call(bf16[32,1024]{1,0:T(8,128)(2,1)S(1)} %collective-permute-done.8.hidden_ref, f32[32,3072]{1,0:T(8,128)S(1)} %shard_map.130.first_ref, bf16[1,2048,3072]{2,1,0:T(8,128)(2,1)S(1)} %bitcast.2, bf16[16,1536]{1,0:T(8,128)(2,1)S(1)} %get-tuple-element.50._), custom_call_target="tpu_custom_call" | custom-call | flops 131072000 | bytes 131072 | tf_op jit(solution)/shard_map/pallas_call | solution.py:563
  33.5 1.5 %collective-permute-start.10 = (bf16[16,1536]{1,0:T(8,128)(2,1)S(1)}, bf16[16,1536]{1,0:T(8,128)(2,1)S(1)}, u32[]{:S(2)}, u32[]{:S(2)}) collective-permute-start(bf16[16,1536]{1,0:T(8,128)(2,1)S(1)} %get-tuple-element.51._), channel_id=1, source_target_pairs={{0,2},{2,0},{1,3},{3,1},{4,6},{6,4},{5,7},{7,5},{8,10},{10,8},{9,1... | collective-permute-start | bytes 147464 | tf_op jit(solution)/shard_map/ppermute | solution.py:571
  35.0 0.5 %collective-permute-start.9 = (bf16[16,1536]{1,0:T(8,128)(2,1)S(1)}, bf16[16,1536]{1,0:T(8,128)(2,1)S(1)}, u32[]{:S(2)}, u32[]{:S(2)}) collective-permute-start(bf16[16,1536]{1,0:T(8,128)(2,1)S(1)} %get-tuple-element.50._), channel_id=1, source_target_pairs={{0,2},{2,0},{1,3},{3,1},{4,6},{6,4},{5,7},{7,5},{8,10},{10,8},{9,1... | collective-permute-start | bytes 147464 | tf_op jit(solution)/shard_map/ppermute | solution.py:571
  35.6 2.3 %collective-permute-done.10.refs_3_ = bf16[16,1536]{1,0:T(8,128)(2,1)S(1)} collective-permute-done((bf16[16,1536]{1,0:T(8,128)(2,1)S(1)}, bf16[16,1536]{1,0:T(8,128)(2,1)S(1)}, u32[]{:S(2)}, u32[]{:S(2)}) %collective-permute-start.10) | collective-permute-done | bytes 49184 | tf_op jit(solution)/shard_map/ppermute | solution.py:571
  37.9 1.2 %collective-permute-done.9.refs_2_ = bf16[16,1536]{1,0:T(8,128)(2,1)S(1)} collective-permute-done((bf16[16,1536]{1,0:T(8,128)(2,1)S(1)}, bf16[16,1536]{1,0:T(8,128)(2,1)S(1)}, u32[]{:S(2)}, u32[]{:S(2)}) %collective-permute-start.9) | collective-permute-done | bytes 49184 | tf_op jit(solution)/shard_map/ppermute | solution.py:571
  39.1 0.1 shard_map.134
  39.3 3.2 %collective-permute-start.12 = (bf16[4,3072]{1,0:T(4,128)(2,1)S(1)}, bf16[4,3072]{1,0:T(4,128)(2,1)S(1)}, u32[]{:S(2)}, u32[]{:S(2)}) collective-permute-start(bf16[4,3072]{1,0:T(4,128)(2,1)S(1)} %get-tuple-element.56), channel_id=1, source_target_pairs={{0,8},{4,12},{8,0},{12,4},{1,9},{5,13},{9,1},{13,5},{2,10},{6,14},... | collective-permute-start | bytes 73736 | tf_op jit(solution)/shard_map/ppermute | solution.py:498
  42.5 1.2 %collective-permute-start.13 = (bf16[4,3072]{1,0:T(4,128)(2,1)S(1)}, bf16[4,3072]{1,0:T(4,128)(2,1)S(1)}, u32[]{:S(2)}, u32[]{:S(2)}) collective-permute-start(bf16[4,3072]{1,0:T(4,128)(2,1)S(1)} %get-tuple-element.57), channel_id=1, source_target_pairs={{0,12},{4,8},{8,4},{12,0},{1,13},{5,9},{9,5},{13,1},{2,14},{6,10},... | collective-permute-start | bytes 73736 | tf_op jit(solution)/shard_map/ppermute | solution.py:498
  43.7 0.6 %shard_map.133 = bf16[2,2,3072]{2,1,0:T(2,128)(2,1)} custom-call(bf16[4,32,896]{2,1,0:T(8,128)(2,1)S(1)} %shard_map.127.x_ref.own_ref, bf16[16,1536]{1,0:T(8,128)(2,1)S(1)} %get-tuple-element.51._), custom_call_target="tpu_custom_call" | custom-call | tf_op jit(solution)/shard_map/pallas_call | solution.py:573
  44.3 3.8 %collective-permute-done.13.refs_3_ = bf16[4,3072]{1,0:T(4,128)(2,1)S(1)} collective-permute-done((bf16[4,3072]{1,0:T(4,128)(2,1)S(1)}, bf16[4,3072]{1,0:T(4,128)(2,1)S(1)}, u32[]{:S(2)}, u32[]{:S(2)}) %collective-permute-start.13) | collective-permute-done | bytes 24608 | tf_op jit(solution)/shard_map/ppermute | solution.py:498
  48.1 0.6 %shard_map.135 = bf16[2,2,3072]{2,1,0:T(2,128)(2,1)} custom-call(bf16[4,3072]{1,0:T(4,128)(2,1)S(1)} %get-tuple-element.54.refs_0_, bf16[4,3072]{1,0:T(4,128)(2,1)S(1)} %collective-permute-done.11.refs_1_, bf16[4,3072]{1,0:T(4,128)(2,1)S(1)} %collective-permute-done.12.refs_2_, bf16[4,3072]{1,0:T(4,128)(2,1)S(1)} %collective-permute-done.13.refs_3_), custom_call_target="tpu_custom_call" | custom-call | tf_op jit(solution)/shard_map/pallas_call | solution.py:579
  (30 shorter events, 0.4 us)
Async XLA Ops:
  1.7 11.9 %copy-start.2 = (bf16[6144]{0:T(1024)(128)(2,1)S(1)}, bf16[6144]{0:T(1024)(128)(2,1)}, u32[]{:S(2)}) copy-start(bf16[6144]{0:T(1024)(128)(2,1)} %param.16) | copy-start | bytes 36868
  1.7 21.0 %copy-start = (bf16[1,6144,1024]{2,1,0:T(8,128)(2,1)S(1)}, bf16[1,6144,1024]{2,1,0:T(8,128)(2,1)}, u32[]{:S(2)}) copy-start(bf16[1,6144,1024]{2,1,0:T(8,128)(2,1)} %gate_w.5) | copy-start | bytes 37748740
  1.7 21.0 %copy-start.1 = (bf16[1,6144,1024]{2,1,0:T(8,128)(2,1)S(1)}, bf16[1,6144,1024]{2,1,0:T(8,128)(2,1)}, u32[]{:S(2)}) copy-start(bf16[1,6144,1024]{2,1,0:T(8,128)(2,1)} %up_w.5) | copy-start | bytes 37748740
  2.0 5.7 %collective-permute-start = (bf16[192,128]{1,0:T(8,128)(2,1)S(1)}, bf16[192,128]{1,0:T(8,128)(2,1)S(1)}, u32[]{:S(2)}, u32[]{:S(2)}) collective-permute-start(bf16[192,128]{1,0:T(8,128)(2,1)S(1)} %get-tuple-element.36), channel_id=1, source_target_pairs={{0,4},{4,0},{8,12},{12,8},{1,5},{5,1},{9,13},{13,9},{2,6},{6,2},{1... | collective-permute-start | bytes 147464 | tf_op jit(solution)/shard_map/ppermute | solution.py:498
  5.1 5.9 %collective-permute-start.1 = (bf16[192,128]{1,0:T(8,128)(2,1)S(1)}, bf16[192,128]{1,0:T(8,128)(2,1)S(1)}, u32[]{:S(2)}, u32[]{:S(2)}) collective-permute-start(bf16[192,128]{1,0:T(8,128)(2,1)S(1)} %get-tuple-element.37), channel_id=1, source_target_pairs={{0,8},{4,12},{8,0},{12,4},{1,9},{5,13},{9,1},{13,5},{2,10},{6,14},... | collective-permute-start | bytes 147464 | tf_op jit(solution)/shard_map/ppermute | solution.py:498
  7.7 5.9 %collective-permute-start.2 = (bf16[192,128]{1,0:T(8,128)(2,1)S(1)}, bf16[192,128]{1,0:T(8,128)(2,1)S(1)}, u32[]{:S(2)}, u32[]{:S(2)}) collective-permute-start(bf16[192,128]{1,0:T(8,128)(2,1)S(1)} %get-tuple-element.38), channel_id=1, source_target_pairs={{0,12},{4,8},{8,4},{12,0},{1,13},{5,9},{9,5},{13,1},{2,14},{6,10},... | collective-permute-start | bytes 147464 | tf_op jit(solution)/shard_map/ppermute | solution.py:498
  14.2 3.9 %collective-permute-start.3 = (bf16[16,896]{1,0:T(8,128)(2,1)S(1)}, bf16[16,896]{1,0:T(8,128)(2,1)S(1)}, u32[]{:S(2)}, u32[]{:S(2)}) collective-permute-start(bf16[16,896]{1,0:T(8,128)(2,1)S(1)} %get-tuple-element.39.own_ref), channel_id=1, source_target_pairs={{0,2},{2,0},{1,3},{3,1},{4,6},{6,4},{5,7},{7,5},{8,10},{10,8},{9,1... | collective-permute-start | bytes 86024 | tf_op jit(solution)/shard_map/ppermute | solution.py:522
  18.1 7.5 %slice-start.3 = ((s8[12582912]{0:T(1024)(128)(4,1)}), s8[4194304]{0:T(1024)(128)(4,1)S(1)}, s32[]{:S(2)}) async-start(s8[12582912]{0:T(1024)(128)(4,1)} %bitcast.3), calls=%async_computation.3 | async-start | bytes 8388608
  18.2 5.1 %collective-permute-start.4 = (bf16[32,896]{1,0:T(8,128)(2,1)S(1)}, bf16[32,896]{1,0:T(8,128)(2,1)S(1)}, u32[]{:S(2)}, u32[]{:S(2)}) collective-permute-start(bf16[32,896]{1,0:T(8,128)(2,1)S(1)} %get-tuple-element.42), channel_id=1, source_target_pairs={{0,4},{4,0},{8,12},{12,8},{1,5},{5,1},{9,13},{13,9},{2,6},{6,2},{1... | collective-permute-start | bytes 172040 | tf_op jit(solution)/shard_map/ppermute | solution.py:498
  18.3 5.1 %collective-permute-start.5 = (bf16[32,896]{1,0:T(8,128)(2,1)S(1)}, bf16[32,896]{1,0:T(8,128)(2,1)S(1)}, u32[]{:S(2)}, u32[]{:S(2)}) collective-permute-start(bf16[32,896]{1,0:T(8,128)(2,1)S(1)} %get-tuple-element.43), channel_id=1, source_target_pairs={{0,8},{4,12},{8,0},{12,4},{1,9},{5,13},{9,1},{13,5},{2,10},{6,14},... | collective-permute-start | bytes 172040 | tf_op jit(solution)/shard_map/ppermute | solution.py:498
  19.6 6.0 %collective-permute-start.6 = (bf16[32,896]{1,0:T(8,128)(2,1)S(1)}, bf16[32,896]{1,0:T(8,128)(2,1)S(1)}, u32[]{:S(2)}, u32[]{:S(2)}) collective-permute-start(bf16[32,896]{1,0:T(8,128)(2,1)S(1)} %get-tuple-element.44), channel_id=1, source_target_pairs={{0,12},{4,8},{8,4},{12,0},{1,13},{5,9},{9,5},{13,1},{2,14},{6,10},... | collective-permute-start | bytes 172040 | tf_op jit(solution)/shard_map/ppermute | solution.py:498
  22.7 3.0 %slice-start.4 = ((s8[12582912]{0:T(1024)(128)(4,1)}), s8[4194304]{0:T(1024)(128)(4,1)S(1)}, s32[]{:S(2)}) async-start(s8[12582912]{0:T(1024)(128)(4,1)} %bitcast.3), calls=%async_computation.4 | async-start | bytes 8388608
  22.7 3.5 %slice-start.5 = ((s8[12582912]{0:T(1024)(128)(4,1)}), s8[4194304]{0:T(1024)(128)(4,1)S(1)}, s32[]{:S(2)}) async-start(s8[12582912]{0:T(1024)(128)(4,1)} %bitcast.3), calls=%async_computation.5 | async-start | bytes 8388608
  25.6 2.3 %collective-permute-start.7 = (bf16[4,32,896]{2,1,0:T(8,128)(2,1)S(1)}, bf16[4,32,896]{2,1,0:T(8,128)(2,1)S(1)}, u32[]{:S(2)}, u32[]{:S(2)}) collective-permute-start(bf16[4,32,896]{2,1,0:T(8,128)(2,1)S(1)} %shard_map.127.x_ref.own_ref), channel_id=1, source_target_pairs={{0,1},{1,0},{2,3},{3,2},{4,5},{5,4},{6,7},{7,6},{8,9},{9,8},{10,11... | collective-permute-start | bytes 688136 | tf_op jit(solution)/shard_map/ppermute | solution.py:536
  26.1 4.2 %slice-start = ((s8[12582912]{0:T(1024)(128)(4,1)}), s8[4194304]{0:T(1024)(128)(4,1)S(1)}, s32[]{:S(2)}) async-start(s8[12582912]{0:T(1024)(128)(4,1)} %bitcast.1), calls=%async_computation | async-start | bytes 8388608
  26.2 4.2 %slice-start.1 = ((s8[12582912]{0:T(1024)(128)(4,1)}), s8[4194304]{0:T(1024)(128)(4,1)S(1)}, s32[]{:S(2)}) async-start(s8[12582912]{0:T(1024)(128)(4,1)} %bitcast.1), calls=%async_computation.1 | async-start | bytes 8388608
  27.9 3.1 %slice-start.2 = ((s8[12582912]{0:T(1024)(128)(4,1)}), s8[4194304]{0:T(1024)(128)(4,1)S(1)}, s32[]{:S(2)}) async-start(s8[12582912]{0:T(1024)(128)(4,1)} %bitcast.1), calls=%async_computation.2 | async-start | bytes 8388608
  30.2 2.0 %collective-permute-start.8 = (bf16[32,1024]{1,0:T(8,128)(2,1)S(1)}, bf16[32,1024]{1,0:T(8,128)(2,1)S(1)}, u32[]{:S(2)}, u32[]{:S(2)}) collective-permute-start(bf16[32,1024]{1,0:T(8,128)(2,1)S(1)} %shard_map.129.hidden_ref), channel_id=1, source_target_pairs={{0,1},{1,0},{2,3},{3,2},{4,5},{5,4},{6,7},{7,6},{8,9},{9,8},{10,11... | collective-permute-start | bytes 196616 | tf_op jit(solution)/shard_map/ppermute | solution.py:551
  33.5 4.4 %collective-permute-start.10 = (bf16[16,1536]{1,0:T(8,128)(2,1)S(1)}, bf16[16,1536]{1,0:T(8,128)(2,1)S(1)}, u32[]{:S(2)}, u32[]{:S(2)}) collective-permute-start(bf16[16,1536]{1,0:T(8,128)(2,1)S(1)} %get-tuple-element.51._), channel_id=1, source_target_pairs={{0,2},{2,0},{1,3},{3,1},{4,6},{6,4},{5,7},{7,5},{8,10},{10,8},{9,1... | collective-permute-start | bytes 147464 | tf_op jit(solution)/shard_map/ppermute | solution.py:571
  35.0 4.1 %collective-permute-start.9 = (bf16[16,1536]{1,0:T(8,128)(2,1)S(1)}, bf16[16,1536]{1,0:T(8,128)(2,1)S(1)}, u32[]{:S(2)}, u32[]{:S(2)}) collective-permute-start(bf16[16,1536]{1,0:T(8,128)(2,1)S(1)} %get-tuple-element.50._), channel_id=1, source_target_pairs={{0,2},{2,0},{1,3},{3,1},{4,6},{6,4},{5,7},{7,5},{8,10},{10,8},{9,1... | collective-permute-start | bytes 147464 | tf_op jit(solution)/shard_map/ppermute | solution.py:571
  39.2 5.1 %collective-permute-start.11 = (bf16[4,3072]{1,0:T(4,128)(2,1)S(1)}, bf16[4,3072]{1,0:T(4,128)(2,1)S(1)}, u32[]{:S(2)}, u32[]{:S(2)}) collective-permute-start(bf16[4,3072]{1,0:T(4,128)(2,1)S(1)} %get-tuple-element.55), channel_id=1, source_target_pairs={{0,4},{4,0},{8,12},{12,8},{1,5},{5,1},{9,13},{13,9},{2,6},{6,2},{1... | collective-permute-start | bytes 73736 | tf_op jit(solution)/shard_map/ppermute | solution.py:498
  39.3 5.0 %collective-permute-start.12 = (bf16[4,3072]{1,0:T(4,128)(2,1)S(1)}, bf16[4,3072]{1,0:T(4,128)(2,1)S(1)}, u32[]{:S(2)}, u32[]{:S(2)}) collective-permute-start(bf16[4,3072]{1,0:T(4,128)(2,1)S(1)} %get-tuple-element.56), channel_id=1, source_target_pairs={{0,8},{4,12},{8,0},{12,4},{1,9},{5,13},{9,1},{13,5},{2,10},{6,14},... | collective-permute-start | bytes 73736 | tf_op jit(solution)/shard_map/ppermute | solution.py:498
  42.5 5.6 %collective-permute-start.13 = (bf16[4,3072]{1,0:T(4,128)(2,1)S(1)}, bf16[4,3072]{1,0:T(4,128)(2,1)S(1)}, u32[]{:S(2)}, u32[]{:S(2)}) collective-permute-start(bf16[4,3072]{1,0:T(4,128)(2,1)S(1)} %get-tuple-element.57), channel_id=1, source_target_pairs={{0,12},{4,8},{8,4},{12,0},{1,13},{5,9},{9,5},{13,1},{2,14},{6,10},... | collective-permute-start | bytes 73736 | tf_op jit(solution)/shard_map/ppermute | solution.py:498

commit v8 on v7

--- a/solution.py
+++ b/solution.py
@@ -23,7 +23,6 @@
 FIRST_LIMIT = 4 * MIB
 SECOND_LIMIT = 4 * MIB
 DOWN_LIMIT = 4 * MIB
-DOWN_COVER = MIB // 8
 ATTEND_COVER = MIB
 MERGE_COVER = MIB
 
@@ -221,8 +220,7 @@
 
 
 def attend_body(plan, rows, *refs):
-    pieces = refs[:rows]
-    gain_ref, x_ref, attn_ref, share_ref, q_s, r_s, kv_s, p_s, gain_s = refs[rows:]
+    pieces, (gain_ref, x_ref, attn_ref, q_s, r_s, kv_s, p_s, gain_s) = refs[:rows], refs[rows:]
     t, c = plan.tokens, plan.conts
     total = rows * t
     f32 = jnp.float32
@@ -251,13 +249,7 @@
     shape = scores.shape
     row = lax.broadcasted_iota(jnp.int32, shape, 0) % total
     col = lax.broadcasted_iota(jnp.int32, shape, 1)
-    local = p_s[...].astype(f32)
-    lane = lax.broadcasted_iota(jnp.int32, local.shape, 1)
-    expert = lax.axis_index("experts")
-    for i in range(share_ref.shape[0]):
-        part = jnp.where((lane > 0) & ((lane + 2) // 3 == (expert ^ i) + 1), local, 0.0)
-        share_ref[i] = jnp.broadcast_to(jnp.sum(part, axis=1, keepdims=True), local.shape)
-    prompt = local[:, :1]
+    prompt = p_s[...].astype(f32)[:, :1]
     prompt = jnp.concatenate([prompt] * GROUP, axis=0).astype(jnp.int32)
     in_prefix = (col < rows * plan.block) & ((col % plan.block) // (2 * plan.positions) == prompt)
     late = col - rows * plan.block
@@ -384,56 +376,42 @@
     hidden_ref[...] = (gate / (1.0 + jnp.exp(-gate)) * up).astype(jnp.bfloat16)
 
 
-def down_product(side, hidden_ref, down_w, lanes):
+def down_product(side, hidden_ref, down_w):
     depth = hidden_ref.shape[1]
     core = lax.axis_index("heads")
     first = pl.multiple_of((1 - core if side else core) * depth, depth)
     return jnp.dot(
-        hidden_ref[...], down_w[0, pl.ds(first, depth), lanes], preferred_element_type=jnp.float32
+        hidden_ref[...], down_w[0, pl.ds(first, depth)], preferred_element_type=jnp.float32
     )
 
 
 def down_first_body(hidden_ref, down_w, out_ref):
-    out_ref[...] = down_product(0, hidden_ref, down_w, slice(None))
-
-
-def down_second_body(part, hidden_ref, first_ref, down_w, _, own_ref, peer_ref):
-    total, width = own_ref.shape
-    lanes = pl.ds(part * width, width)
-    result = first_ref[:, lanes] + down_product(1, hidden_ref, down_w, lanes)
-    own_ref[...] = result[:total]
-    peer_ref[...] = result[total:].astype(jnp.bfloat16)
-
-
-def blend_body(plan, rows, share_ref, *refs):
-    parts = (len(refs) - rows) // 2
-    owns, peers, outs = refs[:parts], refs[parts : 2 * parts], refs[2 * parts :]
+    out_ref[...] = down_product(0, hidden_ref, down_w)
+
+
+def down_second_body(plan, rows, hidden_ref, own_ref, down_w, *outs):
+    result = own_ref[...] + down_product(1, hidden_ref, down_w)
     t = plan.tokens
-    own_share, peer_share = share_ref[0][:, :1], share_ref[1][:, :1]
-    mixed = [
-        own_share * own_ref[...] + peer_share * peer_ref[...].astype(jnp.float32)
-        for own_ref, peer_ref in zip(owns, peers)
-    ]
-    width = mixed[0].shape[1]
+    total = rows * t
 
     def place(own):
         for k, out_ref in enumerate(outs):
             first = (own ^ k) * t
-            for i, part in enumerate(mixed):
-                out_ref[:, pl.ds(i * width, width)] = part[first : first + t].astype(jnp.bfloat16)
+            pair = [result[i : i + t] for i in (first, first + total)]
+            out_ref[...] = jnp.concatenate(pair, axis=0).astype(jnp.bfloat16)
 
     for own in range(rows):
         pl.when(lax.axis_index("rows") == own)(functools.partial(place, own))
 
 
-def total_body(plan, *refs):
-    *pieces, moe_ref = refs
+def sum_body(*refs):
+    *pieces, own_ref, peer_ref = refs
     total = pieces[0][...].astype(jnp.float32)
     for ref in pieces[1:]:
         total = total + ref[...].astype(jnp.float32)
-    total = total.astype(jnp.bfloat16)
-    for s in range(plan.steps):
-        moe_ref[s] = total[s * plan.conts : (s + 1) * plan.conts]
+    t = own_ref.shape[0]
+    own_ref[...] = total[:t].astype(jnp.bfloat16)
+    peer_ref[...] = total[t:].astype(jnp.bfloat16)
 
 
 def attn_body(plan, rows, own_ref, _, attn_ref):
@@ -447,6 +425,20 @@
                 attn_ref[s, :, lanes] = own_ref[
                     k, pl.ds(g * t + s * plan.conts, plan.conts), pl.ds(depth, HEAD_DIM)
                 ]
+
+
+def mix_body(plan, local_ref, own_ref, peer_ref, moe_ref):
+    own = lax.axis_index("experts")
+    local = local_ref[...].astype(jnp.float32)
+    lane = lax.broadcasted_iota(jnp.int32, local.shape, 1)
+    mixture = None
+    for i, ref in enumerate((own_ref, peer_ref)):
+        parts = jnp.where((lane > 0) & ((lane + 2) // 3 == (own ^ i) + 1), local, 0.0)
+        part = jnp.sum(parts, axis=1, keepdims=True) * ref[...].astype(jnp.float32)
+        mixture = part if mixture is None else mixture + part
+    mixture = mixture.astype(jnp.bfloat16)
+    for s in range(plan.steps):
+        moe_ref[s] = mixture[s * plan.conts : (s + 1) * plan.conts]
 
 
 def per_device(
@@ -494,20 +486,16 @@
     )(*map(vmem, fetched))
 
     def spread(pieces):
-        return [
-            lax.ppermute(pieces[k], "rows", [(i, i ^ k) for i in range(rows)]) if k else pieces[0]
-            for k in range(rows)
-        ]
+        got = [pieces[0]]
+        for k in range(1, rows):
+            got.append(lax.ppermute(pieces[k], "rows", [(i, i ^ k) for i in range(rows)]))
+        return got
 
     keys = -(-(rows * (plan.block + 2 * plan.tokens)) // 128) * 128
     lanes = piece + HEAD_DIM
-    x, attn, share = call(
+    x, attn = call(
         functools.partial(attend_body, plan, rows),
-        (
-            shape((total, lanes), bf16),
-            shape((GROUP * total, HEAD_DIM), bf16),
-            shape((experts, total, HEAD_DIM), f32),
-        ),
+        (shape((total, lanes), bf16), shape((GROUP * total, HEAD_DIM), bf16)),
         "v" * (rows + 1),
         scratch=(
             VMEM((GROUP * total, HEAD_DIM), bf16),
@@ -554,29 +542,20 @@
         shape((tokens, plan.half), f32),
         "vv",
         limit=DOWN_LIMIT,
-        cost=cover(DOWN_COVER),
+        cost=cover(2 * plan.half * units),
     )(hidden, down_w)
-    parts = 2
-    width = plan.half // parts
-    owns, peers, back = [], [], []
-    for part in range(parts):
-        own_part, peer_part = call(
-            functools.partial(down_second_body, part),
-            (shape((total, width), f32), shape((total, width), bf16)),
-            "vvvv",
-            cost=cover(DOWN_COVER),
-        )(other_hidden, partial, down_w, peers[-1] if peers else share)
-        owns.append(own_part)
-        peers.append(peer_part)
-        back.append(lax.ppermute(peer_part, "experts", swap))
+    blocks = call(
+        functools.partial(down_second_body, plan, rows),
+        (shape((experts * plan.tokens, plan.half), bf16),) * rows,
+        "vvv",
+        cost=cover(2 * plan.half * units),
+    )(other_hidden, partial, down_w)
+    output = shape((plan.tokens, plan.half), bf16)
+    mine, theirs = call(sum_body, (output, output), "v" * rows)(*spread(blocks))
+    returned = lax.ppermute(theirs, "experts", swap)
     out = shape(queries.shape, bf16)
-    attn_out = call(functools.partial(attn_body, plan, rows), out, "vv")(own, peers[-1])
-    blended = call(
-        functools.partial(blend_body, plan, rows),
-        (shape((plan.tokens, plan.half), bf16),) * rows,
-        "v" * (1 + 2 * parts),
-    )(share, *owns, *back)
-    moe_out = call(functools.partial(total_body, plan), out, "v" * rows)(*spread(blended))
+    attn_out = call(functools.partial(attn_body, plan, rows), out, "vv")(own, theirs)
+    moe_out = call(functools.partial(mix_body, plan), out, "vvv")(vmem(fetched[0]), mine, returned)
     return (attn_out, moe_out)
 
 

time: 48.9 us -> 47.4 us (0.969)
  local copies, waits for them, and re-layouts: 1.23 us -> 0.33 us
    ppermute x2 -> x1, waiting for transfers between devices: 3.55 us -> 1.7 us  [per_device(): returned = lax.ppermute(theirs, 'experts', swap)]
    ppermute x9, waiting for transfers between devices: 11.9 us -> 13.3 us  [spread(): lax.ppermute(pieces[k], 'rows', [(i, i ^ k) for i in range(rows)])]
    unnamed x18 -> x12, local copies, waits for them, and re-layouts: 1.23 us -> 0.33 us
    ppermute x2 -> x1, starting transfers between devices: 2.04 us -> 1.56 us  [per_device(): returned = lax.ppermute(theirs, 'experts', swap)]
    pallas_call x5 -> x4, Pallas kernels: 2.7 us -> 2.63 us  [the longest x1 1.25 us: per_device(): call(functools.partial(down_second_body, plan, rows), (shape((experts * p...]
  transfers between devices with their start and end apart: 14 -> 13, of which waited for: 8 -> 8; matrix products, arithmetic and copies ran while one was open for 0% -> 0% of each run, Pallas kernels for 9% -> 9%
where the time goes in v8:
time: 47.4 us; the launch traced here: 47.2 us
  starting transfers between devices  18.3 us (39%)
  waiting for transfers between devices  17.4 us (37%)
  Pallas kernels  10.5 us (22%)
  between operations  0.77 us (2%)
    ppermute x9, starting transfers between devices, spread(): lax.ppermute(pieces[k], 'rows', [(i, i ^ k) for i in range(rows)])  14.6 us
    ppermute x9, waiting for transfers between devices, spread(): lax.ppermute(pieces[k], 'rows', [(i, i ^ k) for i in range(rows)])  13.3 us
    ppermute x1, waiting for transfers between devices, per_device(): peer = lax.ppermute(x, 'experts', swap)  2.38 us
    pallas_call x1, Pallas kernels, per_device(): call(functools.partial(second_half_body, plan), shape((tokens, units), bf...  2.26 us
    pallas_call x1, Pallas kernels, per_device(): call(first_half_body, (products_of, products_of), 'vvvvv', limit=FIRST_LI...  1.71 us
    ppermute x1, waiting for transfers between devices, per_device(): returned = lax.ppermute(theirs, 'experts', swap)  1.7 us
    ppermute x1, starting transfers between devices, per_device(): returned = lax.ppermute(theirs, 'experts', swap)  1.56 us
    ppermute x1, starting transfers between devices, per_device(): peer = lax.ppermute(x, 'experts', swap)  1.5 us
  transfers between devices with their start and end apart: 13, of which 8 were waited for; matrix products, arithmetic and copies ran while one was open for 0% of the time, Pallas kernels for 9%

profile of v8, /device:TPU:0, one launch (start us, length us, event | category | flops | bytes accessed | tf_op | source)
XLA Modules:
  0.0 47.2 jit_solution(1670503814438640614)
XLA Ops:
  0.6 1.0 %shard_map.122 = (bf16[4,128]{1,0:T(4,128)(2,1)S(1)}, bf16[2,2,3072]{2,1,0:T(2,128)(2,1)S(1)}, bf16[2,2,2,512]{3,2,1,0:T(2,128)(2,1)S(1)}, bf16[2,32,2,512]{3,2,1,0:T(2,128)(2,1)S(1)}, bf16[2,2,3072]{2,1,0:T(2,128)(2,1)S(1)}) custom-call(s32[2]{0:T(128)} %refs_0_.1, s32[2,2,2]{2,1,0:T(2,128)} %refs_1_.1, f32[2,2,2]{2,1,0:T(2,128)} %refs_2_.1, ...), custom_call_target="tpu_custom_call" | custom-call | tf_op jit(solution)/shard_map/pallas_call | solution.py:474
  1.7 0.3 shard_map.123
  2.0 3.1 %collective-permute-start = (bf16[192,128]{1,0:T(8,128)(2,1)S(1)}, bf16[192,128]{1,0:T(8,128)(2,1)S(1)}, u32[]{:S(2)}, u32[]{:S(2)}) collective-permute-start(bf16[192,128]{1,0:T(8,128)(2,1)S(1)} %get-tuple-element.33), channel_id=1, source_target_pairs={{0,4},{4,0},{8,12},{12,8},{1,5},{5,1},{9,13},{13,9},{2,6},{6,2},{1... | collective-permute-start | bytes 147464 | tf_op jit(solution)/shard_map/ppermute | solution.py:491
  5.1 2.6 %collective-permute-start.1 = (bf16[192,128]{1,0:T(8,128)(2,1)S(1)}, bf16[192,128]{1,0:T(8,128)(2,1)S(1)}, u32[]{:S(2)}, u32[]{:S(2)}) collective-permute-start(bf16[192,128]{1,0:T(8,128)(2,1)S(1)} %get-tuple-element.34), channel_id=1, source_target_pairs={{0,8},{4,12},{8,0},{12,4},{1,9},{5,13},{9,1},{13,5},{2,10},{6,14},... | collective-permute-start | bytes 147464 | tf_op jit(solution)/shard_map/ppermute | solution.py:491
  7.7 3.3 %collective-permute-done.1.refs_2_ = bf16[192,128]{1,0:T(8,128)(2,1)S(1)} collective-permute-done((bf16[192,128]{1,0:T(8,128)(2,1)S(1)}, bf16[192,128]{1,0:T(8,128)(2,1)S(1)}, u32[]{:S(2)}, u32[]{:S(2)}) %collective-permute-start.1) | collective-permute-done | bytes 49184 | tf_op jit(solution)/shard_map/ppermute | solution.py:491
  11.0 2.6 %collective-permute-done.2.refs_3_ = bf16[192,128]{1,0:T(8,128)(2,1)S(1)} collective-permute-done((bf16[192,128]{1,0:T(8,128)(2,1)S(1)}, bf16[192,128]{1,0:T(8,128)(2,1)S(1)}, u32[]{:S(2)}, u32[]{:S(2)}) %collective-permute-start.2) | collective-permute-done | bytes 49184 | tf_op jit(solution)/shard_map/ppermute | solution.py:491
  13.6 0.7 %shard_map.124 = (bf16[16,896]{1,0:T(8,128)(2,1)S(1)}, bf16[96,128]{1,0:T(8,128)(2,1)S(1)}) custom-call(bf16[192,128]{1,0:T(8,128)(2,1)S(1)} %get-tuple-element.32.refs_0_, bf16[192,128]{1,0:T(8,128)(2,1)S(1)} %collective-permute-done.refs_1_, bf16[192,128]{1,0:T(8,128)(2,1)S(1)} %collective-permute-done.1.refs_2_, ...), custom_call_target="tpu_custom_call" | custom-call | flops 1048576000 | bytes 1048576 | tf_op jit(solution)/shard_map/pallas_call | solution.py:496
  14.2 1.5 %collective-permute-start.3 = (bf16[16,896]{1,0:T(8,128)(2,1)S(1)}, bf16[16,896]{1,0:T(8,128)(2,1)S(1)}, u32[]{:S(2)}, u32[]{:S(2)}) collective-permute-start(bf16[16,896]{1,0:T(8,128)(2,1)S(1)} %get-tuple-element.36.own_ref), channel_id=1, source_target_pairs={{0,2},{2,0},{1,3},{3,1},{4,6},{6,4},{5,7},{7,5},{8,10},{10,8},{9,1... | collective-permute-start | bytes 86024 | tf_op jit(solution)/shard_map/ppermute | solution.py:510
  15.7 2.4 %collective-permute-done.3.peer_ref = bf16[16,896]{1,0:T(8,128)(2,1)S(1)} collective-permute-done((bf16[16,896]{1,0:T(8,128)(2,1)S(1)}, bf16[16,896]{1,0:T(8,128)(2,1)S(1)}, u32[]{:S(2)}, u32[]{:S(2)}) %collective-permute-start.3) | collective-permute-done | bytes 28704 | tf_op jit(solution)/shard_map/ppermute | solution.py:510
  18.1 0.1 shard_map.125
  18.2 0.1 collective-permute-start.4
  18.3 1.3 %collective-permute-start.5 = (bf16[32,896]{1,0:T(8,128)(2,1)S(1)}, bf16[32,896]{1,0:T(8,128)(2,1)S(1)}, u32[]{:S(2)}, u32[]{:S(2)}) collective-permute-start(bf16[32,896]{1,0:T(8,128)(2,1)S(1)} %get-tuple-element.40), channel_id=1, source_target_pairs={{0,8},{4,12},{8,0},{12,4},{1,9},{5,13},{9,1},{13,5},{2,10},{6,14},... | collective-permute-start | bytes 172040 | tf_op jit(solution)/shard_map/ppermute | solution.py:491
  19.6 3.1 %collective-permute-start.6 = (bf16[32,896]{1,0:T(8,128)(2,1)S(1)}, bf16[32,896]{1,0:T(8,128)(2,1)S(1)}, u32[]{:S(2)}, u32[]{:S(2)}) collective-permute-start(bf16[32,896]{1,0:T(8,128)(2,1)S(1)} %get-tuple-element.41), channel_id=1, source_target_pairs={{0,12},{4,8},{8,4},{12,0},{1,13},{5,9},{9,5},{13,1},{2,14},{6,10},... | collective-permute-start | bytes 172040 | tf_op jit(solution)/shard_map/ppermute | solution.py:491
  22.7 0.6 %shard_map.126 = (f32[32,1024]{1,0:T(8,128)S(1)}, f32[32,1024]{1,0:T(8,128)S(1)}) custom-call(bf16[32,896]{1,0:T(8,128)(2,1)S(1)} %get-tuple-element.38.x_ref.refs_0_, bf16[1,6144,1024]{2,1,0:T(8,128)(2,1)S(1)} %copy-done, bf16[1,6144,1024]{2,1,0:T(8,128)(2,1)S(1)} %copy-done.1), custom_call_target="tpu_custom_call" | custom-call | flops 41943040000 | bytes 41943040 | tf_op jit(solution)/shard_map/pallas_call | solution.py:520
  23.3 0.1 collective-permute-done.5.refs_2_
  23.4 2.1 %collective-permute-done.6.refs_3_ = bf16[32,896]{1,0:T(8,128)(2,1)S(1)} collective-permute-done((bf16[32,896]{1,0:T(8,128)(2,1)S(1)}, bf16[32,896]{1,0:T(8,128)(2,1)S(1)}, u32[]{:S(2)}, u32[]{:S(2)}) %collective-permute-start.6) | collective-permute-done | bytes 57376 | tf_op jit(solution)/shard_map/ppermute | solution.py:491
  25.6 0.1 collective-permute-start.7
  25.7 1.7 %shard_map.128 = (f32[32,1024]{1,0:T(8,128)S(1)}, f32[32,1024]{1,0:T(8,128)S(1)}) custom-call(bf16[4,32,896]{2,1,0:T(8,128)(2,1)S(1)} %shard_map.127.x_ref.own_ref, f32[32,1024]{1,0:T(8,128)S(1)} %get-tuple-element.42.refs_4_.gate_in, f32[32,1024]{1,0:T(8,128)S(1)} %get-tuple-element.43.up_in, bf16[1,6144,1024]{2,1,0:T(8,128)(2,1)S(1)} %copy-done, ...), custom_call_target="tpu_custom_call" | custom-call | flops 1048576000 | bytes 1048576 | tf_op jit(solution)/shard_map/pallas_call | solution.py:525
  27.4 2.3 %shard_map.129.hidden_ref = bf16[32,1024]{1,0:T(8,128)(2,1)S(1)} custom-call(bf16[4,32,896]{2,1,0:T(8,128)(2,1)S(1)} %collective-permute-done.7.x_ref, bf16[4,32,896]{2,1,0:T(8,128)(2,1)S(1)} %shard_map.127.x_ref.own_ref, f32[32,1024]{1,0:T(8,128)S(1)} %get-tuple-element.44.gate_in, f32[32,1024]{1,0:T(8,128)S(1)} %get-tuple-element.45.up_in, ...), custom_call_target="tpu_custom_call" | custom-call | flops 1048576000 | bytes 1048576 | tf_op jit(solution)/shard_map/pallas_call | solution.py:532
  29.7 0.5 %collective-permute-start.8 = (bf16[32,1024]{1,0:T(8,128)(2,1)S(1)}, bf16[32,1024]{1,0:T(8,128)(2,1)S(1)}, u32[]{:S(2)}, u32[]{:S(2)}) collective-permute-start(bf16[32,1024]{1,0:T(8,128)(2,1)S(1)} %shard_map.129.hidden_ref), channel_id=1, source_target_pairs={{0,1},{1,0},{2,3},{3,2},{4,5},{5,4},{6,7},{7,6},{8,9},{9,8},{10,11... | collective-permute-start | bytes 196616 | tf_op jit(solution)/shard_map/ppermute | solution.py:539
  30.2 0.3 slice-done.2
  30.5 1.2 %shard_map.130.own_ref = f32[32,3072]{1,0:T(8,128)S(1)} custom-call(bf16[32,1024]{1,0:T(8,128)(2,1)S(1)} %shard_map.129.hidden_ref, bf16[1,2048,3072]{2,1,0:T(8,128)(2,1)S(1)} %bitcast.2), custom_call_target="tpu_custom_call" | custom-call | flops 6291456000 | bytes 6291456 | tf_op jit(solution)/shard_map/pallas_call | solution.py:540
  31.7 1.2 %shard_map.131 = (bf16[8,3072]{1,0:T(8,128)(2,1)S(1)}, bf16[8,3072]{1,0:T(8,128)(2,1)S(1)}, bf16[8,3072]{1,0:T(8,128)(2,1)S(1)}, bf16[8,3072]{1,0:T(8,128)(2,1)S(1)}) custom-call(bf16[32,1024]{1,0:T(8,128)(2,1)S(1)} %collective-permute-done.8.hidden_ref, f32[32,3072]{1,0:T(8,128)S(1)} %shard_map.130.own_ref, bf16[1,2048,3072]{2,1,0:T(8,128)(2,1)S(1)} %bitcast.2), custom_call_target="tpu_custom_call" | custom-call | flops 6291456000 | bytes 6291456 | tf_op jit(solution)/shard_map/pallas_call | solution.py:547
  33.0 0.1 collective-permute-start.9
  33.0 3.6 %collective-permute-start.10 = (bf16[8,3072]{1,0:T(8,128)(2,1)S(1)}, bf16[8,3072]{1,0:T(8,128)(2,1)S(1)}, u32[]{:S(2)}, u32[]{:S(2)}) collective-permute-start(bf16[8,3072]{1,0:T(8,128)(2,1)S(1)} %get-tuple-element.48), channel_id=1, source_target_pairs={{0,8},{4,12},{8,0},{12,4},{1,9},{5,13},{9,1},{13,5},{2,10},{6,14},... | collective-permute-start | bytes 147464 | tf_op jit(solution)/shard_map/ppermute | solution.py:491
  36.7 0.7 %collective-permute-start.11 = (bf16[8,3072]{1,0:T(8,128)(2,1)S(1)}, bf16[8,3072]{1,0:T(8,128)(2,1)S(1)}, u32[]{:S(2)}, u32[]{:S(2)}) collective-permute-start(bf16[8,3072]{1,0:T(8,128)(2,1)S(1)} %get-tuple-element.49), channel_id=1, source_target_pairs={{0,12},{4,8},{8,4},{12,0},{1,13},{5,9},{9,5},{13,1},{2,14},{6,10},... | collective-permute-start | bytes 147464 | tf_op jit(solution)/shard_map/ppermute | solution.py:491
  37.4 2.6 %collective-permute-done.10.refs_2_ = bf16[8,3072]{1,0:T(8,128)(2,1)S(1)} collective-permute-done((bf16[8,3072]{1,0:T(8,128)(2,1)S(1)}, bf16[8,3072]{1,0:T(8,128)(2,1)S(1)}, u32[]{:S(2)}, u32[]{:S(2)}) %collective-permute-start.10) | collective-permute-done | bytes 49184 | tf_op jit(solution)/shard_map/ppermute | solution.py:491
  40.0 2.5 %collective-permute-done.11.refs_3_ = bf16[8,3072]{1,0:T(8,128)(2,1)S(1)} collective-permute-done((bf16[8,3072]{1,0:T(8,128)(2,1)S(1)}, bf16[8,3072]{1,0:T(8,128)(2,1)S(1)}, u32[]{:S(2)}, u32[]{:S(2)}) %collective-permute-start.11) | collective-permute-done | bytes 49184 | tf_op jit(solution)/shard_map/ppermute | solution.py:491
  42.6 1.6 %collective-permute-start.12 = (bf16[4,3072]{1,0:T(4,128)(2,1)S(1)}, bf16[4,3072]{1,0:T(4,128)(2,1)S(1)}, u32[]{:S(2)}, u32[]{:S(2)}) collective-permute-start(bf16[4,3072]{1,0:T(4,128)(2,1)S(1)} %get-tuple-element.50._), channel_id=1, source_target_pairs={{0,2},{2,0},{1,3},{3,1},{4,6},{6,4},{5,7},{7,5},{8,10},{10,8},{9,1... | collective-permute-start | bytes 73736 | tf_op jit(solution)/shard_map/ppermute | solution.py:555
  44.2 0.6 %shard_map.133 = bf16[2,2,3072]{2,1,0:T(2,128)(2,1)} custom-call(bf16[4,32,896]{2,1,0:T(8,128)(2,1)S(1)} %shard_map.127.x_ref.own_ref, bf16[4,3072]{1,0:T(4,128)(2,1)S(1)} %get-tuple-element.50._), custom_call_target="tpu_custom_call" | custom-call | tf_op jit(solution)/shard_map/pallas_call | solution.py:557
  44.8 1.7 %collective-permute-done.12.peer_ref = bf16[4,3072]{1,0:T(4,128)(2,1)S(1)} collective-permute-done((bf16[4,3072]{1,0:T(4,128)(2,1)S(1)}, bf16[4,3072]{1,0:T(4,128)(2,1)S(1)}, u32[]{:S(2)}, u32[]{:S(2)}) %collective-permute-start.12) | collective-permute-done | bytes 24608 | tf_op jit(solution)/shard_map/ppermute | solution.py:555
  46.5 0.7 %shard_map.134 = bf16[2,2,3072]{2,1,0:T(2,128)(2,1)} custom-call(bf16[4,128]{1,0:T(4,128)(2,1)S(1)} %get-tuple-element.27.local_ref, bf16[4,3072]{1,0:T(4,128)(2,1)S(1)} %get-tuple-element.51.own_ref, bf16[4,3072]{1,0:T(4,128)(2,1)S(1)} %collective-permute-done.12.peer_ref), custom_call_target="tpu_custom_call" | custom-call | tf_op jit(solution)/shard_map/pallas_call | solution.py:558
  (20 shorter events, 0.1 us)
Async XLA Ops:
  1.7 11.9 %copy-start.2 = (bf16[6144]{0:T(1024)(128)(2,1)S(1)}, bf16[6144]{0:T(1024)(128)(2,1)}, u32[]{:S(2)}) copy-start(bf16[6144]{0:T(1024)(128)(2,1)} %param.16) | copy-start | bytes 36868
  1.7 21.0 %copy-start = (bf16[1,6144,1024]{2,1,0:T(8,128)(2,1)S(1)}, bf16[1,6144,1024]{2,1,0:T(8,128)(2,1)}, u32[]{:S(2)}) copy-start(bf16[1,6144,1024]{2,1,0:T(8,128)(2,1)} %gate_w.5) | copy-start | bytes 37748740
  1.7 21.0 %copy-start.1 = (bf16[1,6144,1024]{2,1,0:T(8,128)(2,1)S(1)}, bf16[1,6144,1024]{2,1,0:T(8,128)(2,1)}, u32[]{:S(2)}) copy-start(bf16[1,6144,1024]{2,1,0:T(8,128)(2,1)} %up_w.5) | copy-start | bytes 37748740
  2.0 5.7 %collective-permute-start = (bf16[192,128]{1,0:T(8,128)(2,1)S(1)}, bf16[192,128]{1,0:T(8,128)(2,1)S(1)}, u32[]{:S(2)}, u32[]{:S(2)}) collective-permute-start(bf16[192,128]{1,0:T(8,128)(2,1)S(1)} %get-tuple-element.33), channel_id=1, source_target_pairs={{0,4},{4,0},{8,12},{12,8},{1,5},{5,1},{9,13},{13,9},{2,6},{6,2},{1... | collective-permute-start | bytes 147464 | tf_op jit(solution)/shard_map/ppermute | solution.py:491
  5.1 5.9 %collective-permute-start.1 = (bf16[192,128]{1,0:T(8,128)(2,1)S(1)}, bf16[192,128]{1,0:T(8,128)(2,1)S(1)}, u32[]{:S(2)}, u32[]{:S(2)}) collective-permute-start(bf16[192,128]{1,0:T(8,128)(2,1)S(1)} %get-tuple-element.34), channel_id=1, source_target_pairs={{0,8},{4,12},{8,0},{12,4},{1,9},{5,13},{9,1},{13,5},{2,10},{6,14},... | collective-permute-start | bytes 147464 | tf_op jit(solution)/shard_map/ppermute | solution.py:491
  7.7 5.9 %collective-permute-start.2 = (bf16[192,128]{1,0:T(8,128)(2,1)S(1)}, bf16[192,128]{1,0:T(8,128)(2,1)S(1)}, u32[]{:S(2)}, u32[]{:S(2)}) collective-permute-start(bf16[192,128]{1,0:T(8,128)(2,1)S(1)} %get-tuple-element.35), channel_id=1, source_target_pairs={{0,12},{4,8},{8,4},{12,0},{1,13},{5,9},{9,5},{13,1},{2,14},{6,10},... | collective-permute-start | bytes 147464 | tf_op jit(solution)/shard_map/ppermute | solution.py:491
  14.2 3.9 %collective-permute-start.3 = (bf16[16,896]{1,0:T(8,128)(2,1)S(1)}, bf16[16,896]{1,0:T(8,128)(2,1)S(1)}, u32[]{:S(2)}, u32[]{:S(2)}) collective-permute-start(bf16[16,896]{1,0:T(8,128)(2,1)S(1)} %get-tuple-element.36.own_ref), channel_id=1, source_target_pairs={{0,2},{2,0},{1,3},{3,1},{4,6},{6,4},{5,7},{7,5},{8,10},{10,8},{9,1... | collective-permute-start | bytes 86024 | tf_op jit(solution)/shard_map/ppermute | solution.py:510
  18.2 5.1 %collective-permute-start.4 = (bf16[32,896]{1,0:T(8,128)(2,1)S(1)}, bf16[32,896]{1,0:T(8,128)(2,1)S(1)}, u32[]{:S(2)}, u32[]{:S(2)}) collective-permute-start(bf16[32,896]{1,0:T(8,128)(2,1)S(1)} %get-tuple-element.39), channel_id=1, source_target_pairs={{0,4},{4,0},{8,12},{12,8},{1,5},{5,1},{9,13},{13,9},{2,6},{6,2},{1... | collective-permute-start | bytes 172040 | tf_op jit(solution)/shard_map/ppermute | solution.py:491
  18.3 5.1 %collective-permute-start.5 = (bf16[32,896]{1,0:T(8,128)(2,1)S(1)}, bf16[32,896]{1,0:T(8,128)(2,1)S(1)}, u32[]{:S(2)}, u32[]{:S(2)}) collective-permute-start(bf16[32,896]{1,0:T(8,128)(2,1)S(1)} %get-tuple-element.40), channel_id=1, source_target_pairs={{0,8},{4,12},{8,0},{12,4},{1,9},{5,13},{9,1},{13,5},{2,10},{6,14},... | collective-permute-start | bytes 172040 | tf_op jit(solution)/shard_map/ppermute | solution.py:491
  19.6 6.0 %collective-permute-start.6 = (bf16[32,896]{1,0:T(8,128)(2,1)S(1)}, bf16[32,896]{1,0:T(8,128)(2,1)S(1)}, u32[]{:S(2)}, u32[]{:S(2)}) collective-permute-start(bf16[32,896]{1,0:T(8,128)(2,1)S(1)} %get-tuple-element.41), channel_id=1, source_target_pairs={{0,12},{4,8},{8,4},{12,0},{1,13},{5,9},{9,5},{13,1},{2,14},{6,10},... | collective-permute-start | bytes 172040 | tf_op jit(solution)/shard_map/ppermute | solution.py:491
  25.6 1.8 %collective-permute-start.7 = (bf16[4,32,896]{2,1,0:T(8,128)(2,1)S(1)}, bf16[4,32,896]{2,1,0:T(8,128)(2,1)S(1)}, u32[]{:S(2)}, u32[]{:S(2)}) collective-permute-start(bf16[4,32,896]{2,1,0:T(8,128)(2,1)S(1)} %shard_map.127.x_ref.own_ref), channel_id=1, source_target_pairs={{0,1},{1,0},{2,3},{3,2},{4,5},{5,4},{6,7},{7,6},{8,9},{9,8},{10,11... | collective-permute-start | bytes 688136 | tf_op jit(solution)/shard_map/ppermute | solution.py:524
  25.7 4.6 %slice-start = ((s8[12582912]{0:T(1024)(128)(4,1)}), s8[4194304]{0:T(1024)(128)(4,1)S(1)}, s32[]{:S(2)}) async-start(s8[12582912]{0:T(1024)(128)(4,1)} %bitcast.1), calls=%async_computation | async-start | bytes 8388608
  25.7 4.6 %slice-start.1 = ((s8[12582912]{0:T(1024)(128)(4,1)}), s8[4194304]{0:T(1024)(128)(4,1)S(1)}, s32[]{:S(2)}) async-start(s8[12582912]{0:T(1024)(128)(4,1)} %bitcast.1), calls=%async_computation.1 | async-start | bytes 8388608
  27.4 3.1 %slice-start.2 = ((s8[12582912]{0:T(1024)(128)(4,1)}), s8[4194304]{0:T(1024)(128)(4,1)S(1)}, s32[]{:S(2)}) async-start(s8[12582912]{0:T(1024)(128)(4,1)} %bitcast.1), calls=%async_computation.2 | async-start | bytes 8388608
  29.7 2.0 %collective-permute-start.8 = (bf16[32,1024]{1,0:T(8,128)(2,1)S(1)}, bf16[32,1024]{1,0:T(8,128)(2,1)S(1)}, u32[]{:S(2)}, u32[]{:S(2)}) collective-permute-start(bf16[32,1024]{1,0:T(8,128)(2,1)S(1)} %shard_map.129.hidden_ref), channel_id=1, source_target_pairs={{0,1},{1,0},{2,3},{3,2},{4,5},{5,4},{6,7},{7,6},{8,9},{9,8},{10,11... | collective-permute-start | bytes 196616 | tf_op jit(solution)/shard_map/ppermute | solution.py:539
  33.0 4.5 %collective-permute-start.9 = (bf16[8,3072]{1,0:T(8,128)(2,1)S(1)}, bf16[8,3072]{1,0:T(8,128)(2,1)S(1)}, u32[]{:S(2)}, u32[]{:S(2)}) collective-permute-start(bf16[8,3072]{1,0:T(8,128)(2,1)S(1)} %get-tuple-element.47), channel_id=1, source_target_pairs={{0,4},{4,0},{8,12},{12,8},{1,5},{5,1},{9,13},{13,9},{2,6},{6,2},{1... | collective-permute-start | bytes 147464 | tf_op jit(solution)/shard_map/ppermute | solution.py:491
  33.0 7.0 %collective-permute-start.10 = (bf16[8,3072]{1,0:T(8,128)(2,1)S(1)}, bf16[8,3072]{1,0:T(8,128)(2,1)S(1)}, u32[]{:S(2)}, u32[]{:S(2)}) collective-permute-start(bf16[8,3072]{1,0:T(8,128)(2,1)S(1)} %get-tuple-element.48), channel_id=1, source_target_pairs={{0,8},{4,12},{8,0},{12,4},{1,9},{5,13},{9,1},{13,5},{2,10},{6,14},... | collective-permute-start | bytes 147464 | tf_op jit(solution)/shard_map/ppermute | solution.py:491
  36.7 5.9 %collective-permute-start.11 = (bf16[8,3072]{1,0:T(8,128)(2,1)S(1)}, bf16[8,3072]{1,0:T(8,128)(2,1)S(1)}, u32[]{:S(2)}, u32[]{:S(2)}) collective-permute-start(bf16[8,3072]{1,0:T(8,128)(2,1)S(1)} %get-tuple-element.49), channel_id=1, source_target_pairs={{0,12},{4,8},{8,4},{12,0},{1,13},{5,9},{9,5},{13,1},{2,14},{6,10},... | collective-permute-start | bytes 147464 | tf_op jit(solution)/shard_map/ppermute | solution.py:491
  42.6 3.9 %collective-permute-start.12 = (bf16[4,3072]{1,0:T(4,128)(2,1)S(1)}, bf16[4,3072]{1,0:T(4,128)(2,1)S(1)}, u32[]{:S(2)}, u32[]{:S(2)}) collective-permute-start(bf16[4,3072]{1,0:T(4,128)(2,1)S(1)} %get-tuple-element.50._), channel_id=1, source_target_pairs={{0,2},{2,0},{1,3},{3,1},{4,6},{6,4},{5,7},{7,5},{8,10},{10,8},{9,1... | collective-permute-start | bytes 73736 | tf_op jit(solution)/shard_map/ppermute | solution.py:555

commit v9 on v8

--- a/solution.py
+++ b/solution.py
@@ -344,33 +344,43 @@
     up_ref[...] = products(0, x, up_w, 0, None)
 
 
+def pair_chunk_body(x_ref, gate_in, up_in, gate_w, up_w, gate_ref, up_ref):
+    x = x_ref[:, pl.ds(0, x_ref.shape[1] - HEAD_DIM)]
+    gate_ref[...] = products(1, x, gate_w, 0, gate_in[...])
+    up_ref[...] = products(1, x, up_w, 0, up_in[...])
+
+
 def first_half_body(x_ref, gate_in, up_in, gate_w, up_w, gate_ref, up_ref):
     chunks, _, width = x_ref.shape
     gate, up = gate_in[...], up_in[...]
-    for k in range(1, chunks):
+    for k in range(chunks):
         x = x_ref[k, :, pl.ds(0, width - HEAD_DIM)]
-        gate = products(0, x, gate_w, k, gate)
-        up = products(0, x, up_w, k, up)
+        gate = products(0, x, gate_w, k + 1, gate)
+        up = products(0, x, up_w, k + 1, up)
     gate_ref[...] = gate
     up_ref[...] = up
 
 
-def second_half_body(plan, x_ref, own_ref, gate_in, up_in, gate_w, up_w, hidden_ref):
+def second_half_body(
+    plan, x_ref, own_ref, mine_ref, pair_ref, gate_in, up_in, gate_w, up_w, hidden_ref
+):
     chunks, tokens, width = x_ref.shape
     depth = width - HEAD_DIM
     first = GROUP * plan.tokens
     square = jnp.zeros((tokens - first, HEAD_DIM), jnp.float32)
+    rows, spare = pl.ds(first, tokens - first), pl.ds(depth, HEAD_DIM)
     for ref in (own_ref, x_ref):
         for k in range(chunks):
-            extra = ref[k, pl.ds(first, tokens - first), pl.ds(depth, HEAD_DIM)]
-            square = square + extra.astype(jnp.float32)
+            square = square + ref[k, rows, spare].astype(jnp.float32)
+    for ref in (mine_ref, pair_ref):
+        square = square + ref[rows, spare].astype(jnp.float32)
     square = to_column(square[0:1] + square[1:2], tokens)
-    scale = lax.rsqrt(square / (2 * chunks * depth) + 1e-05)
+    scale = lax.rsqrt(square / (2 * (chunks + 1) * depth) + 1e-05)
     gate, up = gate_in[...], up_in[...]
     for k in range(chunks):
         x = x_ref[k, :, pl.ds(0, depth)]
-        gate = products(1, x, gate_w, k, gate)
-        up = products(1, x, up_w, k, up)
+        gate = products(1, x, gate_w, k + 1, gate)
+        up = products(1, x, up_w, k + 1, up)
     gate = gate * scale
     up = up * scale
     hidden_ref[...] = (gate / (1.0 + jnp.exp(-gate)) * up).astype(jnp.bfloat16)
@@ -414,7 +424,7 @@
     peer_ref[...] = total[t:].astype(jnp.bfloat16)
 
 
-def attn_body(plan, rows, own_ref, _, attn_ref):
+def attn_body(plan, rows, mine_ref, own_ref, _, attn_ref):
     t = plan.tokens
     depth = own_ref.shape[2] - HEAD_DIM
     for k in range(rows):
@@ -422,8 +432,9 @@
         for g in range(GROUP):
             lanes = pl.ds(pl.multiple_of((head + g) * HEAD_DIM, HEAD_DIM), HEAD_DIM)
             for s in range(plan.steps):
-                attn_ref[s, :, lanes] = own_ref[
-                    k, pl.ds(g * t + s * plan.conts, plan.conts), pl.ds(depth, HEAD_DIM)
+                ref = own_ref.at[k - 1] if k else mine_ref
+                attn_ref[s, :, lanes] = ref[
+                    pl.ds(g * t + s * plan.conts, plan.conts), pl.ds(depth, HEAD_DIM)
                 ]
 
 
@@ -517,10 +528,14 @@
     chunks = spread(merged)
     units = w_gate.shape[2]
     products_of = shape((tokens, units), f32)
+    pair = lax.ppermute(merged[0], "heads", swap)
     gate, up = call(
         own_chunk_body, (products_of, products_of), "vvv", cost=cover(OWN_COVER)
     )(merged[0], gate_w, up_w)
-    own = call(stack_body, shape((rows, tokens, lanes), bf16), "v" * (rows + 1))(*chunks, gate)
+    gate, up = call(
+        pair_chunk_body, (products_of, products_of), "vvvvv", cost=cover(FIRST_COVER)
+    )(pair, gate, up, gate_w, up_w)
+    own = call(stack_body, shape((rows - 1, tokens, lanes), bf16), "v" * rows)(*chunks[1:], gate)
     other = lax.ppermute(own, "heads", swap)
     gate, up = call(
         first_half_body,
@@ -532,10 +547,10 @@
     hidden = call(
         functools.partial(second_half_body, plan),
         shape((tokens, units), bf16),
-        "vvvvvv",
+        "vvvvvvvv",
         limit=SECOND_LIMIT,
         cost=cover(SECOND_COVER),
-    )(other, own, gate, up, gate_w, up_w)
+    )(other, own, merged[0], pair, gate, up, gate_w, up_w)
     other_hidden = lax.ppermute(hidden, "heads", swap)
     partial = call(
         down_first_body,
@@ -554,7 +569,7 @@
     mine, theirs = call(sum_body, (output, output), "v" * rows)(*spread(blocks))
     returned = lax.ppermute(theirs, "experts", swap)
     out = shape(queries.shape, bf16)
-    attn_out = call(functools.partial(attn_body, plan, rows), out, "vv")(own, theirs)
+    attn_out = call(functools.partial(attn_body, plan, rows), out, "vvv")(merged[0], own, theirs)
     moe_out = call(functools.partial(mix_body, plan), out, "vvv")(vmem(fetched[0]), mine, returned)
     return (attn_out, moe_out)
 

time: 47.4 us -> 47.4 us (level)
  waiting for transfers between devices: 17.4 us -> 16.7 us
  local copies, waits for them, and re-layouts: 0.33 us -> 0.85 us
    ppermute x9, waiting for transfers between devices: 13.3 us -> 12 us  [spread(): lax.ppermute(pieces[k], 'rows', [(i, i ^ k) for i in range(rows)])]
    pallas_call x2 -> x3, Pallas kernels: 0.66 us -> 1.29 us  [the longest x1 0.64 us: per_device(): call(functools.partial(attn_body, plan, rows), out, 'vvv')]
    ppermute x0 -> x1, waiting for transfers between devices: none -> 0.58 us  [per_device(): pair = lax.ppermute(merged[0], 'heads', swap)]
    unnamed x12, local copies, waits for them, and re-layouts: 0.33 us -> 0.85 us
    pallas_call x1, Pallas kernels: 2.26 us -> 1.75 us  [per_device(): call(functools.partial(second_half_body, plan), shape((tokens, units), bf...]
  transfers between devices with their start and end apart: 13 -> 14, of which waited for: 8 -> 8; matrix products, arithmetic and copies ran while one was open for 0% -> 0% of each run, Pallas kernels for 9% -> 10%
where the time goes in v9:
time: 47.4 us; the launch traced here: 47.2 us
  starting transfers between devices  18.2 us (38%)
  waiting for transfers between devices  16.7 us (35%)
  Pallas kernels  10.6 us (22%)
  local copies, waits for them, and re-layouts  0.85 us (2%)
  between operations  0.79 us (2%)
    ppermute x9, starting transfers between devices, spread(): lax.ppermute(pieces[k], 'rows', [(i, i ^ k) for i in range(rows)])  14.6 us
    ppermute x9, waiting for transfers between devices, spread(): lax.ppermute(pieces[k], 'rows', [(i, i ^ k) for i in range(rows)])  12 us
    ppermute x1, waiting for transfers between devices, per_device(): peer = lax.ppermute(x, 'experts', swap)  2.38 us
    pallas_call x1, Pallas kernels, per_device(): call(functools.partial(second_half_body, plan), shape((tokens, units), bf...  1.75 us
    pallas_call x1, Pallas kernels, per_device(): call(first_half_body, (products_of, products_of), 'vvvvv', limit=FIRST_LI...  1.71 us
    ppermute x1, waiting for transfers between devices, per_device(): returned = lax.ppermute(theirs, 'experts', swap)  1.69 us
    ppermute x1, starting transfers between devices, per_device(): returned = lax.ppermute(theirs, 'experts', swap)  1.56 us
    ppermute x1, starting transfers between devices, per_device(): peer = lax.ppermute(x, 'experts', swap)  1.5 us
  transfers between devices with their start and end apart: 14, of which 8 were waited for; matrix products, arithmetic and copies ran while one was open for 0% of the time, Pallas kernels for 10%

profile of v9, /device:TPU:0, one launch (start us, length us, event | category | flops | bytes accessed | tf_op | source)
XLA Modules:
  0.0 47.2 jit_solution(1887324343490269772)
XLA Ops:
  0.6 1.0 %shard_map.122 = (bf16[4,128]{1,0:T(4,128)(2,1)S(1)}, bf16[2,2,3072]{2,1,0:T(2,128)(2,1)S(1)}, bf16[2,2,2,512]{3,2,1,0:T(2,128)(2,1)S(1)}, bf16[2,32,2,512]{3,2,1,0:T(2,128)(2,1)S(1)}, bf16[2,2,3072]{2,1,0:T(2,128)(2,1)S(1)}) custom-call(s32[2]{0:T(128)} %refs_0_.1, s32[2,2,2]{2,1,0:T(2,128)} %refs_1_.1, f32[2,2,2]{2,1,0:T(2,128)} %refs_2_.1, ...), custom_call_target="tpu_custom_call" | custom-call | tf_op jit(solution)/shard_map/pallas_call | solution.py:485
  1.7 0.3 shard_map.123
  2.0 3.1 %collective-permute-start = (bf16[192,128]{1,0:T(8,128)(2,1)S(1)}, bf16[192,128]{1,0:T(8,128)(2,1)S(1)}, u32[]{:S(2)}, u32[]{:S(2)}) collective-permute-start(bf16[192,128]{1,0:T(8,128)(2,1)S(1)} %get-tuple-element.35), channel_id=1, source_target_pairs={{0,4},{4,0},{8,12},{12,8},{1,5},{5,1},{9,13},{13,9},{2,6},{6,2},{1... | collective-permute-start | bytes 147464 | tf_op jit(solution)/shard_map/ppermute | solution.py:502
  5.1 2.6 %collective-permute-start.1 = (bf16[192,128]{1,0:T(8,128)(2,1)S(1)}, bf16[192,128]{1,0:T(8,128)(2,1)S(1)}, u32[]{:S(2)}, u32[]{:S(2)}) collective-permute-start(bf16[192,128]{1,0:T(8,128)(2,1)S(1)} %get-tuple-element.36), channel_id=1, source_target_pairs={{0,8},{4,12},{8,0},{12,4},{1,9},{5,13},{9,1},{13,5},{2,10},{6,14},... | collective-permute-start | bytes 147464 | tf_op jit(solution)/shard_map/ppermute | solution.py:502
  7.7 3.3 %collective-permute-done.1.refs_2_ = bf16[192,128]{1,0:T(8,128)(2,1)S(1)} collective-permute-done((bf16[192,128]{1,0:T(8,128)(2,1)S(1)}, bf16[192,128]{1,0:T(8,128)(2,1)S(1)}, u32[]{:S(2)}, u32[]{:S(2)}) %collective-permute-start.1) | collective-permute-done | bytes 49184 | tf_op jit(solution)/shard_map/ppermute | solution.py:502
  11.0 2.6 %collective-permute-done.2.refs_3_ = bf16[192,128]{1,0:T(8,128)(2,1)S(1)} collective-permute-done((bf16[192,128]{1,0:T(8,128)(2,1)S(1)}, bf16[192,128]{1,0:T(8,128)(2,1)S(1)}, u32[]{:S(2)}, u32[]{:S(2)}) %collective-permute-start.2) | collective-permute-done | bytes 49184 | tf_op jit(solution)/shard_map/ppermute | solution.py:502
  13.6 0.7 %shard_map.124 = (bf16[16,896]{1,0:T(8,128)(2,1)S(1)}, bf16[96,128]{1,0:T(8,128)(2,1)S(1)}) custom-call(bf16[192,128]{1,0:T(8,128)(2,1)S(1)} %get-tuple-element.34.refs_0_, bf16[192,128]{1,0:T(8,128)(2,1)S(1)} %collective-permute-done.refs_1_, bf16[192,128]{1,0:T(8,128)(2,1)S(1)} %collective-permute-done.1.refs_2_, ...), custom_call_target="tpu_custom_call" | custom-call | flops 1048576000 | bytes 1048576 | tf_op jit(solution)/shard_map/pallas_call | solution.py:507
  14.2 1.5 %collective-permute-start.3 = (bf16[16,896]{1,0:T(8,128)(2,1)S(1)}, bf16[16,896]{1,0:T(8,128)(2,1)S(1)}, u32[]{:S(2)}, u32[]{:S(2)}) collective-permute-start(bf16[16,896]{1,0:T(8,128)(2,1)S(1)} %get-tuple-element.38.own_ref), channel_id=1, source_target_pairs={{0,2},{2,0},{1,3},{3,1},{4,6},{6,4},{5,7},{7,5},{8,10},{10,8},{9,1... | collective-permute-start | bytes 86024 | tf_op jit(solution)/shard_map/ppermute | solution.py:521
  15.7 2.4 %collective-permute-done.3.peer_ref = bf16[16,896]{1,0:T(8,128)(2,1)S(1)} collective-permute-done((bf16[16,896]{1,0:T(8,128)(2,1)S(1)}, bf16[16,896]{1,0:T(8,128)(2,1)S(1)}, u32[]{:S(2)}, u32[]{:S(2)}) %collective-permute-start.3) | collective-permute-done | bytes 28704 | tf_op jit(solution)/shard_map/ppermute | solution.py:521
  18.1 0.1 shard_map.125
  18.2 0.1 collective-permute-start.4
  18.3 1.3 %collective-permute-start.5 = (bf16[32,896]{1,0:T(8,128)(2,1)S(1)}, bf16[32,896]{1,0:T(8,128)(2,1)S(1)}, u32[]{:S(2)}, u32[]{:S(2)}) collective-permute-start(bf16[32,896]{1,0:T(8,128)(2,1)S(1)} %get-tuple-element.42), channel_id=1, source_target_pairs={{0,8},{4,12},{8,0},{12,4},{1,9},{5,13},{9,1},{13,5},{2,10},{6,14},... | collective-permute-start | bytes 172040 | tf_op jit(solution)/shard_map/ppermute | solution.py:502
  19.6 3.1 %collective-permute-start.6 = (bf16[32,896]{1,0:T(8,128)(2,1)S(1)}, bf16[32,896]{1,0:T(8,128)(2,1)S(1)}, u32[]{:S(2)}, u32[]{:S(2)}) collective-permute-start(bf16[32,896]{1,0:T(8,128)(2,1)S(1)} %get-tuple-element.43), channel_id=1, source_target_pairs={{0,12},{4,8},{8,4},{12,0},{1,13},{5,9},{9,5},{13,1},{2,14},{6,10},... | collective-permute-start | bytes 172040 | tf_op jit(solution)/shard_map/ppermute | solution.py:502
  22.7 0.7 %shard_map.126 = (f32[32,1024]{1,0:T(8,128)S(1)}, f32[32,1024]{1,0:T(8,128)S(1)}) custom-call(bf16[32,896]{1,0:T(8,128)(2,1)S(1)} %get-tuple-element.40.x_ref.mine_ref, bf16[1,6144,1024]{2,1,0:T(8,128)(2,1)S(1)} %copy-done, bf16[1,6144,1024]{2,1,0:T(8,128)(2,1)S(1)} %copy-done.1), custom_call_target="tpu_custom_call" | custom-call | flops 41943040000 | bytes 41943040 | tf_op jit(solution)/shard_map/pallas_call | solution.py:532
  23.3 0.6 %collective-permute-done.7.x_ref.pair_ref = bf16[32,896]{1,0:T(8,128)(2,1)S(1)} collective-permute-done((bf16[32,896]{1,0:T(8,128)(2,1)S(1)}, bf16[32,896]{1,0:T(8,128)(2,1)S(1)}, u32[]{:S(2)}, u32[]{:S(2)}) %collective-permute-start.7) | collective-permute-done | bytes 57376 | tf_op jit(solution)/shard_map/ppermute | solution.py:531
  23.9 0.6 %shard_map.127 = (f32[32,1024]{1,0:T(8,128)S(1)}, f32[32,1024]{1,0:T(8,128)S(1)}) custom-call(bf16[32,896]{1,0:T(8,128)(2,1)S(1)} %collective-permute-done.7.x_ref.pair_ref, f32[32,1024]{1,0:T(8,128)S(1)} %get-tuple-element.44.gate_in, f32[32,1024]{1,0:T(8,128)S(1)} %get-tuple-element.45.up_in, bf16[1,6144,1024]{2,1,0:T(8,128)(2,1)S(1)} %copy-done, ...), custom_call_target="tpu_custom_call" | custom-call | flops 1048576000 | bytes 1048576 | tf_op jit(solution)/shard_map/pallas_call | solution.py:535
  24.6 1.0 %collective-permute-done.6.refs_2_ = bf16[32,896]{1,0:T(8,128)(2,1)S(1)} collective-permute-done((bf16[32,896]{1,0:T(8,128)(2,1)S(1)}, bf16[32,896]{1,0:T(8,128)(2,1)S(1)}, u32[]{:S(2)}, u32[]{:S(2)}) %collective-permute-start.6) | collective-permute-done | bytes 57376 | tf_op jit(solution)/shard_map/ppermute | solution.py:502
  25.7 1.7 %shard_map.129 = (f32[32,1024]{1,0:T(8,128)S(1)}, f32[32,1024]{1,0:T(8,128)S(1)}) custom-call(bf16[3,32,896]{2,1,0:T(8,128)(2,1)S(1)} %shard_map.128.x_ref.own_ref, f32[32,1024]{1,0:T(8,128)S(1)} %get-tuple-element.46.refs_3_.gate_in, f32[32,1024]{1,0:T(8,128)S(1)} %get-tuple-element.47.up_in, bf16[1,6144,1024]{2,1,0:T(8,128)(2,1)S(1)} %copy-done, ...), custom_call_target="tpu_custom_call" | custom-call | flops 1048576000 | bytes 1048576 | tf_op jit(solution)/shard_map/pallas_call | solution.py:540
  27.4 1.7 %shard_map.130.hidden_ref = bf16[32,1024]{1,0:T(8,128)(2,1)S(1)} custom-call(bf16[3,32,896]{2,1,0:T(8,128)(2,1)S(1)} %collective-permute-done.8.x_ref, bf16[3,32,896]{2,1,0:T(8,128)(2,1)S(1)} %shard_map.128.x_ref.own_ref, bf16[32,896]{1,0:T(8,128)(2,1)S(1)} %get-tuple-element.40.x_ref.mine_ref, bf16[32,896]{1,0:T(8,128)(2,1)S(1)} %collective-permute-done.7.x_ref.pair_ref, ...), custom_call_target="tpu_custom_call" | custom-call | flops 1048576000 | bytes 1048576 | tf_op jit(solution)/shard_map/pallas_call | solution.py:547
  29.2 0.5 %collective-permute-start.9 = (bf16[32,1024]{1,0:T(8,128)(2,1)S(1)}, bf16[32,1024]{1,0:T(8,128)(2,1)S(1)}, u32[]{:S(2)}, u32[]{:S(2)}) collective-permute-start(bf16[32,1024]{1,0:T(8,128)(2,1)S(1)} %shard_map.130.hidden_ref), channel_id=1, source_target_pairs={{0,1},{1,0},{2,3},{3,2},{4,5},{5,4},{6,7},{7,6},{8,9},{9,8},{10,11... | collective-permute-start | bytes 196616 | tf_op jit(solution)/shard_map/ppermute | solution.py:554
  29.7 0.8 %slice-done.2 = s8[4194304]{0:T(1024)(128)(4,1)S(1)} async-done(((s8[12582912]{0:T(1024)(128)(4,1)}), s8[4194304]{0:T(1024)(128)(4,1)S(1)}, s32[]{:S(2)}) %slice-start.2) | async-done | bytes 4194328
  30.5 1.2 %shard_map.131.own_ref = f32[32,3072]{1,0:T(8,128)S(1)} custom-call(bf16[32,1024]{1,0:T(8,128)(2,1)S(1)} %shard_map.130.hidden_ref, bf16[1,2048,3072]{2,1,0:T(8,128)(2,1)S(1)} %bitcast.2), custom_call_target="tpu_custom_call" | custom-call | flops 6291456000 | bytes 6291456 | tf_op jit(solution)/shard_map/pallas_call | solution.py:555
  31.7 1.3 %shard_map.132 = (bf16[8,3072]{1,0:T(8,128)(2,1)S(1)}, bf16[8,3072]{1,0:T(8,128)(2,1)S(1)}, bf16[8,3072]{1,0:T(8,128)(2,1)S(1)}, bf16[8,3072]{1,0:T(8,128)(2,1)S(1)}) custom-call(bf16[32,1024]{1,0:T(8,128)(2,1)S(1)} %collective-permute-done.9.hidden_ref, f32[32,3072]{1,0:T(8,128)S(1)} %shard_map.131.own_ref, bf16[1,2048,3072]{2,1,0:T(8,128)(2,1)S(1)} %bitcast.2), custom_call_target="tpu_custom_call" | custom-call | flops 6291456000 | bytes 6291456 | tf_op jit(solution)/shard_map/pallas_call | solution.py:562
  33.0 0.1 collective-permute-start.10
  33.0 3.6 %collective-permute-start.11 = (bf16[8,3072]{1,0:T(8,128)(2,1)S(1)}, bf16[8,3072]{1,0:T(8,128)(2,1)S(1)}, u32[]{:S(2)}, u32[]{:S(2)}) collective-permute-start(bf16[8,3072]{1,0:T(8,128)(2,1)S(1)} %get-tuple-element.52), channel_id=1, source_target_pairs={{0,8},{4,12},{8,0},{12,4},{1,9},{5,13},{9,1},{13,5},{2,10},{6,14},... | collective-permute-start | bytes 147464 | tf_op jit(solution)/shard_map/ppermute | solution.py:502
  36.7 0.7 %collective-permute-start.12 = (bf16[8,3072]{1,0:T(8,128)(2,1)S(1)}, bf16[8,3072]{1,0:T(8,128)(2,1)S(1)}, u32[]{:S(2)}, u32[]{:S(2)}) collective-permute-start(bf16[8,3072]{1,0:T(8,128)(2,1)S(1)} %get-tuple-element.53), channel_id=1, source_target_pairs={{0,12},{4,8},{8,4},{12,0},{1,13},{5,9},{9,5},{13,1},{2,14},{6,10},... | collective-permute-start | bytes 147464 | tf_op jit(solution)/shard_map/ppermute | solution.py:502
  37.4 2.6 %collective-permute-done.11.refs_2_ = bf16[8,3072]{1,0:T(8,128)(2,1)S(1)} collective-permute-done((bf16[8,3072]{1,0:T(8,128)(2,1)S(1)}, bf16[8,3072]{1,0:T(8,128)(2,1)S(1)}, u32[]{:S(2)}, u32[]{:S(2)}) %collective-permute-start.11) | collective-permute-done | bytes 49184 | tf_op jit(solution)/shard_map/ppermute | solution.py:502
  40.0 2.5 %collective-permute-done.12.refs_3_ = bf16[8,3072]{1,0:T(8,128)(2,1)S(1)} collective-permute-done((bf16[8,3072]{1,0:T(8,128)(2,1)S(1)}, bf16[8,3072]{1,0:T(8,128)(2,1)S(1)}, u32[]{:S(2)}, u32[]{:S(2)}) %collective-permute-start.12) | collective-permute-done | bytes 49184 | tf_op jit(solution)/shard_map/ppermute | solution.py:502
  42.6 1.6 %collective-permute-start.13 = (bf16[4,3072]{1,0:T(4,128)(2,1)S(1)}, bf16[4,3072]{1,0:T(4,128)(2,1)S(1)}, u32[]{:S(2)}, u32[]{:S(2)}) collective-permute-start(bf16[4,3072]{1,0:T(4,128)(2,1)S(1)} %get-tuple-element.54._), channel_id=1, source_target_pairs={{0,2},{2,0},{1,3},{3,1},{4,6},{6,4},{5,7},{7,5},{8,10},{10,8},{9,1... | collective-permute-start | bytes 73736 | tf_op jit(solution)/shard_map/ppermute | solution.py:570
  44.2 0.6 %shard_map.134 = bf16[2,2,3072]{2,1,0:T(2,128)(2,1)} custom-call(bf16[32,896]{1,0:T(8,128)(2,1)S(1)} %get-tuple-element.40.x_ref.mine_ref, bf16[3,32,896]{2,1,0:T(8,128)(2,1)S(1)} %shard_map.128.x_ref.own_ref, bf16[4,3072]{1,0:T(4,128)(2,1)S(1)} %get-tuple-element.54._), custom_call_target="tpu_custom_call" | custom-call | tf_op jit(solution)/shard_map/pallas_call | solution.py:572
  44.8 1.7 %collective-permute-done.13.peer_ref = bf16[4,3072]{1,0:T(4,128)(2,1)S(1)} collective-permute-done((bf16[4,3072]{1,0:T(4,128)(2,1)S(1)}, bf16[4,3072]{1,0:T(4,128)(2,1)S(1)}, u32[]{:S(2)}, u32[]{:S(2)}) %collective-permute-start.13) | collective-permute-done | bytes 24608 | tf_op jit(solution)/shard_map/ppermute | solution.py:570
  46.5 0.7 %shard_map.135 = bf16[2,2,3072]{2,1,0:T(2,128)(2,1)} custom-call(bf16[4,128]{1,0:T(4,128)(2,1)S(1)} %get-tuple-element.29.local_ref, bf16[4,3072]{1,0:T(4,128)(2,1)S(1)} %get-tuple-element.55.own_ref, bf16[4,3072]{1,0:T(4,128)(2,1)S(1)} %collective-permute-done.13.peer_ref), custom_call_target="tpu_custom_call" | custom-call | tf_op jit(solution)/shard_map/pallas_call | solution.py:573
  (23 shorter events, 0.2 us)
Async XLA Ops:
  1.7 11.9 %copy-start.2 = (bf16[6144]{0:T(1024)(128)(2,1)S(1)}, bf16[6144]{0:T(1024)(128)(2,1)}, u32[]{:S(2)}) copy-start(bf16[6144]{0:T(1024)(128)(2,1)} %param.16) | copy-start | bytes 36868
  1.7 21.0 %copy-start = (bf16[1,6144,1024]{2,1,0:T(8,128)(2,1)S(1)}, bf16[1,6144,1024]{2,1,0:T(8,128)(2,1)}, u32[]{:S(2)}) copy-start(bf16[1,6144,1024]{2,1,0:T(8,128)(2,1)} %gate_w.7) | copy-start | bytes 37748740
  1.7 21.0 %copy-start.1 = (bf16[1,6144,1024]{2,1,0:T(8,128)(2,1)S(1)}, bf16[1,6144,1024]{2,1,0:T(8,128)(2,1)}, u32[]{:S(2)}) copy-start(bf16[1,6144,1024]{2,1,0:T(8,128)(2,1)} %up_w.7) | copy-start | bytes 37748740
  2.0 5.7 %collective-permute-start = (bf16[192,128]{1,0:T(8,128)(2,1)S(1)}, bf16[192,128]{1,0:T(8,128)(2,1)S(1)}, u32[]{:S(2)}, u32[]{:S(2)}) collective-permute-start(bf16[192,128]{1,0:T(8,128)(2,1)S(1)} %get-tuple-element.35), channel_id=1, source_target_pairs={{0,4},{4,0},{8,12},{12,8},{1,5},{5,1},{9,13},{13,9},{2,6},{6,2},{1... | collective-permute-start | bytes 147464 | tf_op jit(solution)/shard_map/ppermute | solution.py:502
  5.1 5.9 %collective-permute-start.1 = (bf16[192,128]{1,0:T(8,128)(2,1)S(1)}, bf16[192,128]{1,0:T(8,128)(2,1)S(1)}, u32[]{:S(2)}, u32[]{:S(2)}) collective-permute-start(bf16[192,128]{1,0:T(8,128)(2,1)S(1)} %get-tuple-element.36), channel_id=1, source_target_pairs={{0,8},{4,12},{8,0},{12,4},{1,9},{5,13},{9,1},{13,5},{2,10},{6,14},... | collective-permute-start | bytes 147464 | tf_op jit(solution)/shard_map/ppermute | solution.py:502
  7.7 5.9 %collective-permute-start.2 = (bf16[192,128]{1,0:T(8,128)(2,1)S(1)}, bf16[192,128]{1,0:T(8,128)(2,1)S(1)}, u32[]{:S(2)}, u32[]{:S(2)}) collective-permute-start(bf16[192,128]{1,0:T(8,128)(2,1)S(1)} %get-tuple-element.37), channel_id=1, source_target_pairs={{0,12},{4,8},{8,4},{12,0},{1,13},{5,9},{9,5},{13,1},{2,14},{6,10},... | collective-permute-start | bytes 147464 | tf_op jit(solution)/shard_map/ppermute | solution.py:502
  14.2 3.9 %collective-permute-start.3 = (bf16[16,896]{1,0:T(8,128)(2,1)S(1)}, bf16[16,896]{1,0:T(8,128)(2,1)S(1)}, u32[]{:S(2)}, u32[]{:S(2)}) collective-permute-start(bf16[16,896]{1,0:T(8,128)(2,1)S(1)} %get-tuple-element.38.own_ref), channel_id=1, source_target_pairs={{0,2},{2,0},{1,3},{3,1},{4,6},{6,4},{5,7},{7,5},{8,10},{10,8},{9,1... | collective-permute-start | bytes 86024 | tf_op jit(solution)/shard_map/ppermute | solution.py:521
  18.2 6.4 %collective-permute-start.4 = (bf16[32,896]{1,0:T(8,128)(2,1)S(1)}, bf16[32,896]{1,0:T(8,128)(2,1)S(1)}, u32[]{:S(2)}, u32[]{:S(2)}) collective-permute-start(bf16[32,896]{1,0:T(8,128)(2,1)S(1)} %get-tuple-element.41), channel_id=1, source_target_pairs={{0,4},{4,0},{8,12},{12,8},{1,5},{5,1},{9,13},{13,9},{2,6},{6,2},{1... | collective-permute-start | bytes 172040 | tf_op jit(solution)/shard_map/ppermute | solution.py:502
  18.3 6.3 %collective-permute-start.5 = (bf16[32,896]{1,0:T(8,128)(2,1)S(1)}, bf16[32,896]{1,0:T(8,128)(2,1)S(1)}, u32[]{:S(2)}, u32[]{:S(2)}) collective-permute-start(bf16[32,896]{1,0:T(8,128)(2,1)S(1)} %get-tuple-element.42), channel_id=1, source_target_pairs={{0,8},{4,12},{8,0},{12,4},{1,9},{5,13},{9,1},{13,5},{2,10},{6,14},... | collective-permute-start | bytes 172040 | tf_op jit(solution)/shard_map/ppermute | solution.py:502
  19.6 6.0 %collective-permute-start.6 = (bf16[32,896]{1,0:T(8,128)(2,1)S(1)}, bf16[32,896]{1,0:T(8,128)(2,1)S(1)}, u32[]{:S(2)}, u32[]{:S(2)}) collective-permute-start(bf16[32,896]{1,0:T(8,128)(2,1)S(1)} %get-tuple-element.43), channel_id=1, source_target_pairs={{0,12},{4,8},{8,4},{12,0},{1,13},{5,9},{9,5},{13,1},{2,14},{6,10},... | collective-permute-start | bytes 172040 | tf_op jit(solution)/shard_map/ppermute | solution.py:502
  22.7 1.2 %collective-permute-start.7 = (bf16[32,896]{1,0:T(8,128)(2,1)S(1)}, bf16[32,896]{1,0:T(8,128)(2,1)S(1)}, u32[]{:S(2)}, u32[]{:S(2)}) collective-permute-start(bf16[32,896]{1,0:T(8,128)(2,1)S(1)} %get-tuple-element.40.x_ref.mine_ref), channel_id=1, source_target_pairs={{0,1},{1,0},{2,3},{3,2},{4,5},{5,4},{6,7},{7,6},{8,9},{9,8},{10,11... | collective-permute-start | bytes 172040 | tf_op jit(solution)/shard_map/ppermute | solution.py:531
  25.6 1.8 %collective-permute-start.8 = (bf16[3,32,896]{2,1,0:T(8,128)(2,1)S(1)}, bf16[3,32,896]{2,1,0:T(8,128)(2,1)S(1)}, u32[]{:S(2)}, u32[]{:S(2)}) collective-permute-start(bf16[3,32,896]{2,1,0:T(8,128)(2,1)S(1)} %shard_map.128.x_ref.own_ref), channel_id=1, source_target_pairs={{0,1},{1,0},{2,3},{3,2},{4,5},{5,4},{6,7},{7,6},{8,9},{9,8},{10,11... | collective-permute-start | bytes 516104 | tf_op jit(solution)/shard_map/ppermute | solution.py:539
  25.6 4.1 %slice-start = ((s8[12582912]{0:T(1024)(128)(4,1)}), s8[4194304]{0:T(1024)(128)(4,1)S(1)}, s32[]{:S(2)}) async-start(s8[12582912]{0:T(1024)(128)(4,1)} %bitcast.1), calls=%async_computation | async-start | bytes 8388608
  25.7 4.0 %slice-start.1 = ((s8[12582912]{0:T(1024)(128)(4,1)}), s8[4194304]{0:T(1024)(128)(4,1)S(1)}, s32[]{:S(2)}) async-start(s8[12582912]{0:T(1024)(128)(4,1)} %bitcast.1), calls=%async_computation.1 | async-start | bytes 8388608
  27.4 3.1 %slice-start.2 = ((s8[12582912]{0:T(1024)(128)(4,1)}), s8[4194304]{0:T(1024)(128)(4,1)S(1)}, s32[]{:S(2)}) async-start(s8[12582912]{0:T(1024)(128)(4,1)} %bitcast.1), calls=%async_computation.2 | async-start | bytes 8388608
  29.2 2.5 %collective-permute-start.9 = (bf16[32,1024]{1,0:T(8,128)(2,1)S(1)}, bf16[32,1024]{1,0:T(8,128)(2,1)S(1)}, u32[]{:S(2)}, u32[]{:S(2)}) collective-permute-start(bf16[32,1024]{1,0:T(8,128)(2,1)S(1)} %shard_map.130.hidden_ref), channel_id=1, source_target_pairs={{0,1},{1,0},{2,3},{3,2},{4,5},{5,4},{6,7},{7,6},{8,9},{9,8},{10,11... | collective-permute-start | bytes 196616 | tf_op jit(solution)/shard_map/ppermute | solution.py:554
  33.0 4.5 %collective-permute-start.10 = (bf16[8,3072]{1,0:T(8,128)(2,1)S(1)}, bf16[8,3072]{1,0:T(8,128)(2,1)S(1)}, u32[]{:S(2)}, u32[]{:S(2)}) collective-permute-start(bf16[8,3072]{1,0:T(8,128)(2,1)S(1)} %get-tuple-element.51), channel_id=1, source_target_pairs={{0,4},{4,0},{8,12},{12,8},{1,5},{5,1},{9,13},{13,9},{2,6},{6,2},{1... | collective-permute-start | bytes 147464 | tf_op jit(solution)/shard_map/ppermute | solution.py:502
  33.0 7.0 %collective-permute-start.11 = (bf16[8,3072]{1,0:T(8,128)(2,1)S(1)}, bf16[8,3072]{1,0:T(8,128)(2,1)S(1)}, u32[]{:S(2)}, u32[]{:S(2)}) collective-permute-start(bf16[8,3072]{1,0:T(8,128)(2,1)S(1)} %get-tuple-element.52), channel_id=1, source_target_pairs={{0,8},{4,12},{8,0},{12,4},{1,9},{5,13},{9,1},{13,5},{2,10},{6,14},... | collective-permute-start | bytes 147464 | tf_op jit(solution)/shard_map/ppermute | solution.py:502
  36.7 5.9 %collective-permute-start.12 = (bf16[8,3072]{1,0:T(8,128)(2,1)S(1)}, bf16[8,3072]{1,0:T(8,128)(2,1)S(1)}, u32[]{:S(2)}, u32[]{:S(2)}) collective-permute-start(bf16[8,3072]{1,0:T(8,128)(2,1)S(1)} %get-tuple-element.53), channel_id=1, source_target_pairs={{0,12},{4,8},{8,4},{12,0},{1,13},{5,9},{9,5},{13,1},{2,14},{6,10},... | collective-permute-start | bytes 147464 | tf_op jit(solution)/shard_map/ppermute | solution.py:502
  42.6 3.9 %collective-permute-start.13 = (bf16[4,3072]{1,0:T(4,128)(2,1)S(1)}, bf16[4,3072]{1,0:T(4,128)(2,1)S(1)}, u32[]{:S(2)}, u32[]{:S(2)}) collective-permute-start(bf16[4,3072]{1,0:T(4,128)(2,1)S(1)} %get-tuple-element.54._), channel_id=1, source_target_pairs={{0,2},{2,0},{1,3},{3,1},{4,6},{6,4},{5,7},{7,5},{8,10},{10,8},{9,1... | collective-permute-start | bytes 73736 | tf_op jit(solution)/shard_map/ppermute | solution.py:570

commit v10 on v9

--- a/solution.py
+++ b/solution.py
@@ -338,10 +338,32 @@
     return part if total is None else total + part
 
 
-def own_chunk_body(x_ref, gate_w, up_w, gate_ref, up_ref):
+def pull(source, first, target, sems):
+    parts = sems.shape[0]
+    step = target.shape[0] // parts
+
+    def copy(i):
+        rows = pl.ds(pl.multiple_of(first + i * step, step), step)
+        into = pl.ds(pl.multiple_of(i * step, step), step)
+        return pltpu.make_async_copy(source.at[0, rows], target.at[into], sems.at[i])
+
+    def start():
+        pl.loop(0, parts)(lambda i: copy(i).start())
+
+    def finish():
+        pl.loop(0, parts)(lambda i: copy(i).wait())
+
+    return start, finish
+
+
+def own_chunk_body(x_ref, gate_w, up_w, down_hbm, gate_ref, up_ref, down_ref, sems):
+    half = down_ref.shape[0]
+    start, finish = pull(down_hbm, lax.axis_index("heads") * half, down_ref, sems)
+    start()
     x = x_ref[:, pl.ds(0, x_ref.shape[1] - HEAD_DIM)]
     gate_ref[...] = products(0, x, gate_w, 0, None)
     up_ref[...] = products(0, x, up_w, 0, None)
+    finish()
 
 
 def pair_chunk_body(x_ref, gate_in, up_in, gate_w, up_w, gate_ref, up_ref):
@@ -350,7 +372,13 @@
     up_ref[...] = products(1, x, up_w, 0, up_in[...])
 
 
-def first_half_body(x_ref, gate_in, up_in, gate_w, up_w, gate_ref, up_ref):
+def first_half_body(
+    x_ref, gate_in, up_in, gate_w, up_w, down_hbm, gate_ref, up_ref, down_ref, sems
+):
+    quarter = down_ref.shape[0]
+    other = (1 - lax.axis_index("heads")) * (2 * quarter)
+    start, finish = pull(down_hbm, other, down_ref, sems)
+    start()
     chunks, _, width = x_ref.shape
     gate, up = gate_in[...], up_in[...]
     for k in range(chunks):
@@ -359,11 +387,28 @@
         up = products(0, x, up_w, k + 1, up)
     gate_ref[...] = gate
     up_ref[...] = up
+    finish()
 
 
 def second_half_body(
-    plan, x_ref, own_ref, mine_ref, pair_ref, gate_in, up_in, gate_w, up_w, hidden_ref
+    plan,
+    x_ref,
+    own_ref,
+    mine_ref,
+    pair_ref,
+    gate_in,
+    up_in,
+    gate_w,
+    up_w,
+    down_hbm,
+    hidden_ref,
+    down_ref,
+    sems,
 ):
+    quarter = down_ref.shape[0]
+    other = (1 - lax.axis_index("heads")) * (2 * quarter) + quarter
+    start, finish = pull(down_hbm, other, down_ref, sems)
+    start()
     chunks, tokens, width = x_ref.shape
     depth = width - HEAD_DIM
     first = GROUP * plan.tokens
@@ -384,23 +429,21 @@
     gate = gate * scale
     up = up * scale
     hidden_ref[...] = (gate / (1.0 + jnp.exp(-gate)) * up).astype(jnp.bfloat16)
-
-
-def down_product(side, hidden_ref, down_w):
-    depth = hidden_ref.shape[1]
-    core = lax.axis_index("heads")
-    first = pl.multiple_of((1 - core if side else core) * depth, depth)
-    return jnp.dot(
-        hidden_ref[...], down_w[0, pl.ds(first, depth)], preferred_element_type=jnp.float32
-    )
+    finish()
 
 
 def down_first_body(hidden_ref, down_w, out_ref):
-    out_ref[...] = down_product(0, hidden_ref, down_w)
-
-
-def down_second_body(plan, rows, hidden_ref, own_ref, down_w, *outs):
-    result = own_ref[...] + down_product(1, hidden_ref, down_w)
+    out_ref[...] = jnp.dot(hidden_ref[...], down_w[...], preferred_element_type=jnp.float32)
+
+
+def down_second_body(plan, rows, hidden_ref, own_ref, *refs):
+    weights, outs = refs[:-rows], refs[-rows:]
+    result = own_ref[...]
+    for i, weight in enumerate(weights):
+        depth = weight.shape[0]
+        result = result + jnp.dot(
+            hidden_ref[:, pl.ds(i * depth, depth)], weight[...], preferred_element_type=jnp.float32
+        )
     t = plan.tokens
     total = rows * t
 
@@ -475,7 +518,7 @@
 
     hbm = functools.partial(pltpu.with_memory_space_constraint, memory_space=pltpu.HBM)
     vmem = functools.partial(pltpu.with_memory_space_constraint, memory_space=VMEM)
-    gate_w, up_w, down_w = w_gate, w_up, w_down
+    gate_w, up_w, down_w = w_gate, w_up, hbm(w_down)
 
     def cover(size):
         return pl.CostEstimate(flops=FLOPS * size, bytes_accessed=size, transcendentals=0)
@@ -529,28 +572,36 @@
     units = w_gate.shape[2]
     products_of = shape((tokens, units), f32)
     pair = lax.ppermute(merged[0], "heads", swap)
-    gate, up = call(
-        own_chunk_body, (products_of, products_of), "vvv", cost=cover(OWN_COVER)
-    )(merged[0], gate_w, up_w)
+    half, wide = w_down.shape[1] // 2, w_down.shape[2]
+    sems = (pltpu.SemaphoreType.DMA((4,)),)
+    gate, up, down_own = call(
+        own_chunk_body,
+        (products_of, products_of, VMEM((half, wide), bf16)),
+        "vvva",
+        sems,
+        cost=cover(OWN_COVER),
+    )(merged[0], gate_w, up_w, down_w)
     gate, up = call(
         pair_chunk_body, (products_of, products_of), "vvvvv", cost=cover(FIRST_COVER)
     )(pair, gate, up, gate_w, up_w)
     own = call(stack_body, shape((rows - 1, tokens, lanes), bf16), "v" * rows)(*chunks[1:], gate)
     other = lax.ppermute(own, "heads", swap)
-    gate, up = call(
+    gate, up, down_near = call(
         first_half_body,
-        (products_of, products_of),
-        "vvvvv",
+        (products_of, products_of, VMEM((half // 2, wide), bf16)),
+        "vvvvva",
+        sems,
         limit=FIRST_LIMIT,
         cost=cover(FIRST_COVER),
-    )(own, gate, up, gate_w, up_w)
-    hidden = call(
+    )(own, gate, up, gate_w, up_w, down_w)
+    hidden, down_far = call(
         functools.partial(second_half_body, plan),
-        shape((tokens, units), bf16),
-        "vvvvvvvv",
+        (shape((tokens, units), bf16), VMEM((half // 2, wide), bf16)),
+        "vvvvvvvva",
+        sems,
         limit=SECOND_LIMIT,
         cost=cover(SECOND_COVER),
-    )(other, own, merged[0], pair, gate, up, gate_w, up_w)
+    )(other, own, merged[0], pair, gate, up, gate_w, up_w, down_w)
     other_hidden = lax.ppermute(hidden, "heads", swap)
     partial = call(
         down_first_body,
@@ -558,13 +609,13 @@
         "vv",
         limit=DOWN_LIMIT,
         cost=cover(2 * plan.half * units),
-    )(hidden, down_w)
+    )(hidden, vmem(down_own))
     blocks = call(
         functools.partial(down_second_body, plan, rows),
         (shape((experts * plan.tokens, plan.half), bf16),) * rows,
-        "vvv",
+        "vvvv",
         cost=cover(2 * plan.half * units),
-    )(other_hidden, partial, down_w)
+    )(other_hidden, partial, vmem(down_near), vmem(down_far))
     output = shape((plan.tokens, plan.half), bf16)
     mine, theirs = call(sum_body, (output, output), "v" * rows)(*spread(blocks))
     returned = lax.ppermute(theirs, "experts", swap)

time: 47.4 us -> 46.8 us (0.987)
  Pallas kernels: 10.6 us -> 13.2 us
  waiting for transfers between devices: 16.7 us -> 14.4 us
  local copies, waits for them, and re-layouts: 0.85 us -> 0.02 us
    pallas_call x3, Pallas kernels: 4.11 us -> 6.66 us  [the longest x1 2.88 us: per_device(): call(own_chunk_body, (products_of, products_of, VMEM((half, wide), bf16))...]
    ppermute x9, waiting for transfers between devices: 12 us -> 10.3 us  [spread(): lax.ppermute(pieces[k], 'rows', [(i, i ^ k) for i in range(rows)])]
    unnamed x12 -> x6, local copies, waits for them, and re-layouts: 0.85 us -> 0.02 us
    ppermute x1, waiting for transfers between devices: 0.58 us -> 0.01 us  [per_device(): pair = lax.ppermute(merged[0], 'heads', swap)]
    ppermute x1, starting transfers between devices: 0.07 us -> 0.55 us  [per_device(): other = lax.ppermute(own, 'heads', swap)]
  transfers between devices with their start and end apart: 14 -> 14, of which waited for: 8 -> 6; matrix products, arithmetic and copies ran while one was open for 0% -> 0% of each run, Pallas kernels for 10% -> 15%
where the time goes in v10:
time: 46.8 us; the launch traced here: 46.7 us
  starting transfers between devices  18.3 us (39%)
  waiting for transfers between devices  14.4 us (31%)
  Pallas kernels  13.2 us (28%)
  between operations  0.79 us (2%)
    ppermute x9, starting transfers between devices, spread(): lax.ppermute(pieces[k], 'rows', [(i, i ^ k) for i in range(rows)])  14.6 us
    ppermute x9, waiting for transfers between devices, spread(): lax.ppermute(pieces[k], 'rows', [(i, i ^ k) for i in range(rows)])  10.3 us
    pallas_call x1, Pallas kernels, per_device(): call(own_chunk_body, (products_of, products_of, VMEM((half, wide), bf16))...  2.88 us
    ppermute x1, waiting for transfers between devices, per_device(): peer = lax.ppermute(x, 'experts', swap)  2.38 us
    pallas_call x1, Pallas kernels, per_device(): call(functools.partial(second_half_body, plan), (shape((tokens, units), b...  1.9 us
    pallas_call x1, Pallas kernels, per_device(): call(first_half_body, (products_of, products_of, VMEM((half // 2, wide),...  1.88 us
    ppermute x1, waiting for transfers between devices, per_device(): returned = lax.ppermute(theirs, 'experts', swap)  1.69 us
    ppermute x1, starting transfers between devices, per_device(): returned = lax.ppermute(theirs, 'experts', swap)  1.56 us
  transfers between devices with their start and end apart: 14, of which 6 were waited for; matrix products, arithmetic and copies ran while one was open for 0% of the time, Pallas kernels for 15%

profile of v10, /device:TPU:0, one launch (start us, length us, event | category | flops | bytes accessed | tf_op | source)
XLA Modules:
  0.0 46.7 jit_solution(3159328175347704008)
XLA Ops:
  0.6 1.0 %shard_map.122 = (bf16[4,128]{1,0:T(4,128)(2,1)S(1)}, bf16[2,2,3072]{2,1,0:T(2,128)(2,1)S(1)}, bf16[2,2,2,512]{3,2,1,0:T(2,128)(2,1)S(1)}, bf16[2,32,2,512]{3,2,1,0:T(2,128)(2,1)S(1)}, bf16[2,2,3072]{2,1,0:T(2,128)(2,1)S(1)}) custom-call(s32[2]{0:T(128)} %refs_0_.1, s32[2,2,2]{2,1,0:T(2,128)} %refs_1_.1, f32[2,2,2]{2,1,0:T(2,128)} %refs_2_.1, ...), custom_call_target="tpu_custom_call" | custom-call | tf_op jit(solution)/shard_map/pallas_call | solution.py:528
  1.7 0.3 shard_map.123
  2.0 3.1 %collective-permute-start = (bf16[192,128]{1,0:T(8,128)(2,1)S(1)}, bf16[192,128]{1,0:T(8,128)(2,1)S(1)}, u32[]{:S(2)}, u32[]{:S(2)}) collective-permute-start(bf16[192,128]{1,0:T(8,128)(2,1)S(1)} %get-tuple-element.39), channel_id=1, source_target_pairs={{0,4},{4,0},{8,12},{12,8},{1,5},{5,1},{9,13},{13,9},{2,6},{6,2},{1... | collective-permute-start | bytes 147464 | tf_op jit(solution)/shard_map/ppermute | solution.py:545
  5.1 2.6 %collective-permute-start.1 = (bf16[192,128]{1,0:T(8,128)(2,1)S(1)}, bf16[192,128]{1,0:T(8,128)(2,1)S(1)}, u32[]{:S(2)}, u32[]{:S(2)}) collective-permute-start(bf16[192,128]{1,0:T(8,128)(2,1)S(1)} %get-tuple-element.40), channel_id=1, source_target_pairs={{0,8},{4,12},{8,0},{12,4},{1,9},{5,13},{9,1},{13,5},{2,10},{6,14},... | collective-permute-start | bytes 147464 | tf_op jit(solution)/shard_map/ppermute | solution.py:545
  7.7 3.3 %collective-permute-done.1.refs_2_ = bf16[192,128]{1,0:T(8,128)(2,1)S(1)} collective-permute-done((bf16[192,128]{1,0:T(8,128)(2,1)S(1)}, bf16[192,128]{1,0:T(8,128)(2,1)S(1)}, u32[]{:S(2)}, u32[]{:S(2)}) %collective-permute-start.1) | collective-permute-done | bytes 49184 | tf_op jit(solution)/shard_map/ppermute | solution.py:545
  11.0 2.6 %collective-permute-done.2.refs_3_ = bf16[192,128]{1,0:T(8,128)(2,1)S(1)} collective-permute-done((bf16[192,128]{1,0:T(8,128)(2,1)S(1)}, bf16[192,128]{1,0:T(8,128)(2,1)S(1)}, u32[]{:S(2)}, u32[]{:S(2)}) %collective-permute-start.2) | collective-permute-done | bytes 49184 | tf_op jit(solution)/shard_map/ppermute | solution.py:545
  13.6 0.7 %shard_map.124 = (bf16[16,896]{1,0:T(8,128)(2,1)S(1)}, bf16[96,128]{1,0:T(8,128)(2,1)S(1)}) custom-call(bf16[192,128]{1,0:T(8,128)(2,1)S(1)} %get-tuple-element.38.refs_0_, bf16[192,128]{1,0:T(8,128)(2,1)S(1)} %collective-permute-done.refs_1_, bf16[192,128]{1,0:T(8,128)(2,1)S(1)} %collective-permute-done.1.refs_2_, ...), custom_call_target="tpu_custom_call" | custom-call | flops 1048576000 | bytes 1048576 | tf_op jit(solution)/shard_map/pallas_call | solution.py:550
  14.2 1.5 %collective-permute-start.3 = (bf16[16,896]{1,0:T(8,128)(2,1)S(1)}, bf16[16,896]{1,0:T(8,128)(2,1)S(1)}, u32[]{:S(2)}, u32[]{:S(2)}) collective-permute-start(bf16[16,896]{1,0:T(8,128)(2,1)S(1)} %get-tuple-element.42.own_ref), channel_id=1, source_target_pairs={{0,2},{2,0},{1,3},{3,1},{4,6},{6,4},{5,7},{7,5},{8,10},{10,8},{9,1... | collective-permute-start | bytes 86024 | tf_op jit(solution)/shard_map/ppermute | solution.py:564
  15.7 2.4 %collective-permute-done.3.peer_ref = bf16[16,896]{1,0:T(8,128)(2,1)S(1)} collective-permute-done((bf16[16,896]{1,0:T(8,128)(2,1)S(1)}, bf16[16,896]{1,0:T(8,128)(2,1)S(1)}, u32[]{:S(2)}, u32[]{:S(2)}) %collective-permute-start.3) | collective-permute-done | bytes 28704 | tf_op jit(solution)/shard_map/ppermute | solution.py:564
  18.1 0.1 shard_map.125
  18.2 0.1 collective-permute-start.4
  18.3 1.3 %collective-permute-start.5 = (bf16[32,896]{1,0:T(8,128)(2,1)S(1)}, bf16[32,896]{1,0:T(8,128)(2,1)S(1)}, u32[]{:S(2)}, u32[]{:S(2)}) collective-permute-start(bf16[32,896]{1,0:T(8,128)(2,1)S(1)} %get-tuple-element.46), channel_id=1, source_target_pairs={{0,8},{4,12},{8,0},{12,4},{1,9},{5,13},{9,1},{13,5},{2,10},{6,14},... | collective-permute-start | bytes 172040 | tf_op jit(solution)/shard_map/ppermute | solution.py:545
  19.6 3.1 %collective-permute-start.6 = (bf16[32,896]{1,0:T(8,128)(2,1)S(1)}, bf16[32,896]{1,0:T(8,128)(2,1)S(1)}, u32[]{:S(2)}, u32[]{:S(2)}) collective-permute-start(bf16[32,896]{1,0:T(8,128)(2,1)S(1)} %get-tuple-element.47), channel_id=1, source_target_pairs={{0,12},{4,8},{8,4},{12,0},{1,13},{5,9},{9,5},{13,1},{2,14},{6,10},... | collective-permute-start | bytes 172040 | tf_op jit(solution)/shard_map/ppermute | solution.py:545
  22.7 2.9 %shard_map.126 = (f32[32,1024]{1,0:T(8,128)S(1)}, f32[32,1024]{1,0:T(8,128)S(1)}, bf16[1024,3072]{1,0:T(8,128)(2,1)S(1)}) custom-call(bf16[32,896]{1,0:T(8,128)(2,1)S(1)} %get-tuple-element.44.x_ref.mine_ref, bf16[1,6144,1024]{2,1,0:T(8,128)(2,1)S(1)} %copy-done, bf16[1,6144,1024]{2,1,0:T(8,128)(2,1)S(1)} %copy-done.1, bf16[1,2048,3072]{2,1,0:T(8,128)(2,1)} %down_hbm.5), custom_call_target="tpu_custom_call" | custom-call | flops 41943040000 | bytes 41943040 | tf_op jit(solution)/shard_map/pallas_call | solution.py:577
  25.6 0.6 %shard_map.127 = (f32[32,1024]{1,0:T(8,128)S(1)}, f32[32,1024]{1,0:T(8,128)S(1)}) custom-call(bf16[32,896]{1,0:T(8,128)(2,1)S(1)} %collective-permute-done.7.x_ref.pair_ref, f32[32,1024]{1,0:T(8,128)S(1)} %get-tuple-element.48.gate_in, f32[32,1024]{1,0:T(8,128)S(1)} %get-tuple-element.49.up_in, bf16[1,6144,1024]{2,1,0:T(8,128)(2,1)S(1)} %copy-done, ...), custom_call_target="tpu_custom_call" | custom-call | flops 1048576000 | bytes 1048576 | tf_op jit(solution)/shard_map/pallas_call | solution.py:584
  26.2 0.0 collective-permute-done.4.refs_0_
  26.3 0.6 %collective-permute-start.8 = (bf16[3,32,896]{2,1,0:T(8,128)(2,1)S(1)}, bf16[3,32,896]{2,1,0:T(8,128)(2,1)S(1)}, u32[]{:S(2)}, u32[]{:S(2)}) collective-permute-start(bf16[3,32,896]{2,1,0:T(8,128)(2,1)S(1)} %shard_map.128.x_ref.own_ref), channel_id=1, source_target_pairs={{0,1},{1,0},{2,3},{3,2},{4,5},{5,4},{6,7},{7,6},{8,9},{9,8},{10,11... | collective-permute-start | bytes 516104 | tf_op jit(solution)/shard_map/ppermute | solution.py:588
  26.9 1.9 %shard_map.129 = (f32[32,1024]{1,0:T(8,128)S(1)}, f32[32,1024]{1,0:T(8,128)S(1)}, bf16[512,3072]{1,0:T(8,128)(2,1)S(1)}) custom-call(bf16[3,32,896]{2,1,0:T(8,128)(2,1)S(1)} %shard_map.128.x_ref.own_ref, f32[32,1024]{1,0:T(8,128)S(1)} %get-tuple-element.50.refs_3_.gate_in, f32[32,1024]{1,0:T(8,128)S(1)} %get-tuple-element.51.up_in, ...), custom_call_target="tpu_custom_call" | custom-call | flops 1048576000 | bytes 1048576 | tf_op jit(solution)/shard_map/pallas_call | solution.py:589
  28.7 1.9 %shard_map.130 = (bf16[32,1024]{1,0:T(8,128)(2,1)S(1)}, bf16[512,3072]{1,0:T(8,128)(2,1)S(1)}) custom-call(bf16[3,32,896]{2,1,0:T(8,128)(2,1)S(1)} %collective-permute-done.8.x_ref, bf16[3,32,896]{2,1,0:T(8,128)(2,1)S(1)} %shard_map.128.x_ref.own_ref, bf16[32,896]{1,0:T(8,128)(2,1)S(1)} %get-tuple-element.44.x_ref.mine_ref, ...), custom_call_target="tpu_custom_call" | custom-call | flops 1048576000 | bytes 1048576 | tf_op jit(solution)/shard_map/pallas_call | solution.py:597
  30.7 0.1 collective-permute-start.9
  30.8 1.2 %shard_map.131.own_ref = f32[32,3072]{1,0:T(8,128)S(1)} custom-call(bf16[32,1024]{1,0:T(8,128)(2,1)S(1)} %get-tuple-element.54.hidden_ref, bf16[1024,3072]{1,0:T(8,128)(2,1)S(1)} %get-tuple-element.55.down_w), custom_call_target="tpu_custom_call" | custom-call | flops 6291456000 | bytes 6291456 | tf_op jit(solution)/shard_map/pallas_call | solution.py:606
  31.9 0.0 collective-permute-done.9.hidden_ref
  32.0 1.2 %shard_map.132 = (bf16[8,3072]{1,0:T(8,128)(2,1)S(1)}, bf16[8,3072]{1,0:T(8,128)(2,1)S(1)}, bf16[8,3072]{1,0:T(8,128)(2,1)S(1)}, bf16[8,3072]{1,0:T(8,128)(2,1)S(1)}) custom-call(bf16[32,1024]{1,0:T(8,128)(2,1)S(1)} %collective-permute-done.9.hidden_ref, f32[32,3072]{1,0:T(8,128)S(1)} %shard_map.131.own_ref, ...), custom_call_target="tpu_custom_call" | custom-call | flops 6291456000 | bytes 6291456 | tf_op jit(solution)/shard_map/pallas_call | solution.py:613
  33.2 0.1 collective-permute-start.10
  33.3 2.9 %collective-permute-start.11 = (bf16[8,3072]{1,0:T(8,128)(2,1)S(1)}, bf16[8,3072]{1,0:T(8,128)(2,1)S(1)}, u32[]{:S(2)}, u32[]{:S(2)}) collective-permute-start(bf16[8,3072]{1,0:T(8,128)(2,1)S(1)} %get-tuple-element.60), channel_id=1, source_target_pairs={{0,8},{4,12},{8,0},{12,4},{1,9},{5,13},{9,1},{13,5},{2,10},{6,14},... | collective-permute-start | bytes 147464 | tf_op jit(solution)/shard_map/ppermute | solution.py:545
  36.2 1.5 %collective-permute-start.12 = (bf16[8,3072]{1,0:T(8,128)(2,1)S(1)}, bf16[8,3072]{1,0:T(8,128)(2,1)S(1)}, u32[]{:S(2)}, u32[]{:S(2)}) collective-permute-start(bf16[8,3072]{1,0:T(8,128)(2,1)S(1)} %get-tuple-element.61), channel_id=1, source_target_pairs={{0,12},{4,8},{8,4},{12,0},{1,13},{5,9},{9,5},{13,1},{2,14},{6,10},... | collective-permute-start | bytes 147464 | tf_op jit(solution)/shard_map/ppermute | solution.py:545
  37.7 1.5 %collective-permute-done.11.refs_2_ = bf16[8,3072]{1,0:T(8,128)(2,1)S(1)} collective-permute-done((bf16[8,3072]{1,0:T(8,128)(2,1)S(1)}, bf16[8,3072]{1,0:T(8,128)(2,1)S(1)}, u32[]{:S(2)}, u32[]{:S(2)}) %collective-permute-start.11) | collective-permute-done | bytes 49184 | tf_op jit(solution)/shard_map/ppermute | solution.py:545
  39.2 2.9 %collective-permute-done.12.refs_3_ = bf16[8,3072]{1,0:T(8,128)(2,1)S(1)} collective-permute-done((bf16[8,3072]{1,0:T(8,128)(2,1)S(1)}, bf16[8,3072]{1,0:T(8,128)(2,1)S(1)}, u32[]{:S(2)}, u32[]{:S(2)}) %collective-permute-start.12) | collective-permute-done | bytes 49184 | tf_op jit(solution)/shard_map/ppermute | solution.py:545
  42.1 1.6 %collective-permute-start.13 = (bf16[4,3072]{1,0:T(4,128)(2,1)S(1)}, bf16[4,3072]{1,0:T(4,128)(2,1)S(1)}, u32[]{:S(2)}, u32[]{:S(2)}) collective-permute-start(bf16[4,3072]{1,0:T(4,128)(2,1)S(1)} %get-tuple-element.62._), channel_id=1, source_target_pairs={{0,2},{2,0},{1,3},{3,1},{4,6},{6,4},{5,7},{7,5},{8,10},{10,8},{9,1... | collective-permute-start | bytes 73736 | tf_op jit(solution)/shard_map/ppermute | solution.py:621
  43.6 0.6 %shard_map.134 = bf16[2,2,3072]{2,1,0:T(2,128)(2,1)} custom-call(bf16[32,896]{1,0:T(8,128)(2,1)S(1)} %get-tuple-element.44.x_ref.mine_ref, bf16[3,32,896]{2,1,0:T(8,128)(2,1)S(1)} %shard_map.128.x_ref.own_ref, bf16[4,3072]{1,0:T(4,128)(2,1)S(1)} %get-tuple-element.62._), custom_call_target="tpu_custom_call" | custom-call | tf_op jit(solution)/shard_map/pallas_call | solution.py:623
  44.3 1.7 %collective-permute-done.13.peer_ref = bf16[4,3072]{1,0:T(4,128)(2,1)S(1)} collective-permute-done((bf16[4,3072]{1,0:T(4,128)(2,1)S(1)}, bf16[4,3072]{1,0:T(4,128)(2,1)S(1)}, u32[]{:S(2)}, u32[]{:S(2)}) %collective-permute-start.13) | collective-permute-done | bytes 24608 | tf_op jit(solution)/shard_map/ppermute | solution.py:621
  46.0 0.7 %shard_map.135 = bf16[2,2,3072]{2,1,0:T(2,128)(2,1)} custom-call(bf16[4,128]{1,0:T(4,128)(2,1)S(1)} %get-tuple-element.33.local_ref, bf16[4,3072]{1,0:T(4,128)(2,1)S(1)} %get-tuple-element.63.own_ref, bf16[4,3072]{1,0:T(4,128)(2,1)S(1)} %collective-permute-done.13.peer_ref), custom_call_target="tpu_custom_call" | custom-call | tf_op jit(solution)/shard_map/pallas_call | solution.py:624
  (16 shorter events, 0.1 us)
Async XLA Ops:
  1.7 11.9 %copy-start.2 = (bf16[6144]{0:T(1024)(128)(2,1)S(1)}, bf16[6144]{0:T(1024)(128)(2,1)}, u32[]{:S(2)}) copy-start(bf16[6144]{0:T(1024)(128)(2,1)} %param.16) | copy-start | bytes 36868
  1.7 21.0 %copy-start = (bf16[1,6144,1024]{2,1,0:T(8,128)(2,1)S(1)}, bf16[1,6144,1024]{2,1,0:T(8,128)(2,1)}, u32[]{:S(2)}) copy-start(bf16[1,6144,1024]{2,1,0:T(8,128)(2,1)} %gate_w.7) | copy-start | bytes 37748740
  1.7 21.0 %copy-start.1 = (bf16[1,6144,1024]{2,1,0:T(8,128)(2,1)S(1)}, bf16[1,6144,1024]{2,1,0:T(8,128)(2,1)}, u32[]{:S(2)}) copy-start(bf16[1,6144,1024]{2,1,0:T(8,128)(2,1)} %up_w.7) | copy-start | bytes 37748740
  2.0 5.7 %collective-permute-start = (bf16[192,128]{1,0:T(8,128)(2,1)S(1)}, bf16[192,128]{1,0:T(8,128)(2,1)S(1)}, u32[]{:S(2)}, u32[]{:S(2)}) collective-permute-start(bf16[192,128]{1,0:T(8,128)(2,1)S(1)} %get-tuple-element.39), channel_id=1, source_target_pairs={{0,4},{4,0},{8,12},{12,8},{1,5},{5,1},{9,13},{13,9},{2,6},{6,2},{1... | collective-permute-start | bytes 147464 | tf_op jit(solution)/shard_map/ppermute | solution.py:545
  5.1 5.9 %collective-permute-start.1 = (bf16[192,128]{1,0:T(8,128)(2,1)S(1)}, bf16[192,128]{1,0:T(8,128)(2,1)S(1)}, u32[]{:S(2)}, u32[]{:S(2)}) collective-permute-start(bf16[192,128]{1,0:T(8,128)(2,1)S(1)} %get-tuple-element.40), channel_id=1, source_target_pairs={{0,8},{4,12},{8,0},{12,4},{1,9},{5,13},{9,1},{13,5},{2,10},{6,14},... | collective-permute-start | bytes 147464 | tf_op jit(solution)/shard_map/ppermute | solution.py:545
  7.7 5.9 %collective-permute-start.2 = (bf16[192,128]{1,0:T(8,128)(2,1)S(1)}, bf16[192,128]{1,0:T(8,128)(2,1)S(1)}, u32[]{:S(2)}, u32[]{:S(2)}) collective-permute-start(bf16[192,128]{1,0:T(8,128)(2,1)S(1)} %get-tuple-element.41), channel_id=1, source_target_pairs={{0,12},{4,8},{8,4},{12,0},{1,13},{5,9},{9,5},{13,1},{2,14},{6,10},... | collective-permute-start | bytes 147464 | tf_op jit(solution)/shard_map/ppermute | solution.py:545
  14.2 3.9 %collective-permute-start.3 = (bf16[16,896]{1,0:T(8,128)(2,1)S(1)}, bf16[16,896]{1,0:T(8,128)(2,1)S(1)}, u32[]{:S(2)}, u32[]{:S(2)}) collective-permute-start(bf16[16,896]{1,0:T(8,128)(2,1)S(1)} %get-tuple-element.42.own_ref), channel_id=1, source_target_pairs={{0,2},{2,0},{1,3},{3,1},{4,6},{6,4},{5,7},{7,5},{8,10},{10,8},{9,1... | collective-permute-start | bytes 86024 | tf_op jit(solution)/shard_map/ppermute | solution.py:564
  18.2 8.0 %collective-permute-start.4 = (bf16[32,896]{1,0:T(8,128)(2,1)S(1)}, bf16[32,896]{1,0:T(8,128)(2,1)S(1)}, u32[]{:S(2)}, u32[]{:S(2)}) collective-permute-start(bf16[32,896]{1,0:T(8,128)(2,1)S(1)} %get-tuple-element.45), channel_id=1, source_target_pairs={{0,4},{4,0},{8,12},{12,8},{1,5},{5,1},{9,13},{13,9},{2,6},{6,2},{1... | collective-permute-start | bytes 172040 | tf_op jit(solution)/shard_map/ppermute | solution.py:545
  18.3 8.0 %collective-permute-start.5 = (bf16[32,896]{1,0:T(8,128)(2,1)S(1)}, bf16[32,896]{1,0:T(8,128)(2,1)S(1)}, u32[]{:S(2)}, u32[]{:S(2)}) collective-permute-start(bf16[32,896]{1,0:T(8,128)(2,1)S(1)} %get-tuple-element.46), channel_id=1, source_target_pairs={{0,8},{4,12},{8,0},{12,4},{1,9},{5,13},{9,1},{13,5},{2,10},{6,14},... | collective-permute-start | bytes 172040 | tf_op jit(solution)/shard_map/ppermute | solution.py:545
  19.6 6.7 %collective-permute-start.6 = (bf16[32,896]{1,0:T(8,128)(2,1)S(1)}, bf16[32,896]{1,0:T(8,128)(2,1)S(1)}, u32[]{:S(2)}, u32[]{:S(2)}) collective-permute-start(bf16[32,896]{1,0:T(8,128)(2,1)S(1)} %get-tuple-element.47), channel_id=1, source_target_pairs={{0,12},{4,8},{8,4},{12,0},{1,13},{5,9},{9,5},{13,1},{2,14},{6,10},... | collective-permute-start | bytes 172040 | tf_op jit(solution)/shard_map/ppermute | solution.py:545
  22.7 2.9 %collective-permute-start.7 = (bf16[32,896]{1,0:T(8,128)(2,1)S(1)}, bf16[32,896]{1,0:T(8,128)(2,1)S(1)}, u32[]{:S(2)}, u32[]{:S(2)}) collective-permute-start(bf16[32,896]{1,0:T(8,128)(2,1)S(1)} %get-tuple-element.44.x_ref.mine_ref), channel_id=1, source_target_pairs={{0,1},{1,0},{2,3},{3,2},{4,5},{5,4},{6,7},{7,6},{8,9},{9,8},{10,11... | collective-permute-start | bytes 172040 | tf_op jit(solution)/shard_map/ppermute | solution.py:574
  26.3 2.4 %collective-permute-start.8 = (bf16[3,32,896]{2,1,0:T(8,128)(2,1)S(1)}, bf16[3,32,896]{2,1,0:T(8,128)(2,1)S(1)}, u32[]{:S(2)}, u32[]{:S(2)}) collective-permute-start(bf16[3,32,896]{2,1,0:T(8,128)(2,1)S(1)} %shard_map.128.x_ref.own_ref), channel_id=1, source_target_pairs={{0,1},{1,0},{2,3},{3,2},{4,5},{5,4},{6,7},{7,6},{8,9},{9,8},{10,11... | collective-permute-start | bytes 516104 | tf_op jit(solution)/shard_map/ppermute | solution.py:588
  30.7 1.3 %collective-permute-start.9 = (bf16[32,1024]{1,0:T(8,128)(2,1)S(1)}, bf16[32,1024]{1,0:T(8,128)(2,1)S(1)}, u32[]{:S(2)}, u32[]{:S(2)}) collective-permute-start(bf16[32,1024]{1,0:T(8,128)(2,1)S(1)} %get-tuple-element.54.hidden_ref), channel_id=1, source_target_pairs={{0,1},{1,0},{2,3},{3,2},{4,5},{5,4},{6,7},{7,6},{8,9},{9,8},{10,11... | collective-permute-start | bytes 196616 | tf_op jit(solution)/shard_map/ppermute | solution.py:605
  33.2 4.5 %collective-permute-start.10 = (bf16[8,3072]{1,0:T(8,128)(2,1)S(1)}, bf16[8,3072]{1,0:T(8,128)(2,1)S(1)}, u32[]{:S(2)}, u32[]{:S(2)}) collective-permute-start(bf16[8,3072]{1,0:T(8,128)(2,1)S(1)} %get-tuple-element.59), channel_id=1, source_target_pairs={{0,4},{4,0},{8,12},{12,8},{1,5},{5,1},{9,13},{13,9},{2,6},{6,2},{1... | collective-permute-start | bytes 147464 | tf_op jit(solution)/shard_map/ppermute | solution.py:545
  33.3 5.9 %collective-permute-start.11 = (bf16[8,3072]{1,0:T(8,128)(2,1)S(1)}, bf16[8,3072]{1,0:T(8,128)(2,1)S(1)}, u32[]{:S(2)}, u32[]{:S(2)}) collective-permute-start(bf16[8,3072]{1,0:T(8,128)(2,1)S(1)} %get-tuple-element.60), channel_id=1, source_target_pairs={{0,8},{4,12},{8,0},{12,4},{1,9},{5,13},{9,1},{13,5},{2,10},{6,14},... | collective-permute-start | bytes 147464 | tf_op jit(solution)/shard_map/ppermute | solution.py:545
  36.2 5.9 %collective-permute-start.12 = (bf16[8,3072]{1,0:T(8,128)(2,1)S(1)}, bf16[8,3072]{1,0:T(8,128)(2,1)S(1)}, u32[]{:S(2)}, u32[]{:S(2)}) collective-permute-start(bf16[8,3072]{1,0:T(8,128)(2,1)S(1)} %get-tuple-element.61), channel_id=1, source_target_pairs={{0,12},{4,8},{8,4},{12,0},{1,13},{5,9},{9,5},{13,1},{2,14},{6,10},... | collective-permute-start | bytes 147464 | tf_op jit(solution)/shard_map/ppermute | solution.py:545
  42.1 3.9 %collective-permute-start.13 = (bf16[4,3072]{1,0:T(4,128)(2,1)S(1)}, bf16[4,3072]{1,0:T(4,128)(2,1)S(1)}, u32[]{:S(2)}, u32[]{:S(2)}) collective-permute-start(bf16[4,3072]{1,0:T(4,128)(2,1)S(1)} %get-tuple-element.62._), channel_id=1, source_target_pairs={{0,2},{2,0},{1,3},{3,1},{4,6},{6,4},{5,7},{7,5},{8,10},{10,8},{9,1... | collective-permute-start | bytes 73736 | tf_op jit(solution)/shard_map/ppermute | solution.py:621
